TPU v7x, 32 devices: a whole 2x2x4 slice. The times are simulated.
32 devices in a mesh: dp: 8 (over z, y), head: 4 (over x, core).
Axes of the slice: x: 2, y: 2, z: 4, core: 2. Of those that a mesh axis runs over, the one named last changes fastest.
Arguments:
- features: float32 [2, 8, 768, 128], P(None, 'dp'), may hold values from -6 to 6
- targets: float32 [2, 8, 768], P(None, 'dp'), may hold values from -6 to 6
- neighbours: int32 [2, 8, 256, 256], P(None, 'dp'), may hold values from 0 to 511, as said below
- nbr_mask: int32 [2, 8, 256, 256], P(None, 'dp'), may hold values from 0 to 1, as said below
- flags: int32 [2, 8, 256], P(None, 'dp'), may hold values 0 or 1
- step_count: int32 [1], replicated, may hold values from 2 to 20
- w_qkv: float32 [2, 768, 2304], P(None, 'dp', 'head'), may hold values from -0.21875 to 0.21875
- w_out: float32 [2, 768, 768], P(None, 'dp', 'head'), may hold values from -0.875 to 0.875
- w_up: float32 [2, 768, 3072], P(None, 'dp', 'head'), may hold values from -0.21875 to 0.21875
- w_down: float32 [2, 768, 3072], P(None, 'dp', 'head'), may hold values from -0.109375 to 0.109375
- emb_weight: float32 [768, 128], P('dp'), may hold values from -0.5 to 0.5
- vectors: float32 [768, 7], P('dp'), may hold values from -4 to 4
- m_qkv: float32 [2, 768, 2304], P(None, 'dp', 'head'), may hold values from -7.6293945e-06 to 7.6293945e-06
- m_out: float32 [2, 768, 768], P(None, 'dp', 'head'), may hold values from -7.6293945e-06 to 7.6293945e-06
- m_up: float32 [2, 768, 3072], P(None, 'dp', 'head'), may hold values from -7.6293945e-06 to 7.6293945e-06
- m_down: float32 [2, 768, 3072], P(None, 'dp', 'head'), may hold values from -7.6293945e-06 to 7.6293945e-06
- m_emb: float32 [768, 128], P('dp'), may hold values from -7.6293945e-06 to 7.6293945e-06
- m_vectors: float32 [768, 7], P('dp'), may hold values from -9.1552734e-05 to 9.1552734e-05
- v_qkv: float32 [2, 768, 2304], P(None, 'dp', 'head'), may hold values from 2.8051561e-14 to 1.12206244e-13
- v_out: float32 [2, 768, 768], P(None, 'dp', 'head'), may hold values from 2.8051561e-14 to 1.12206244e-13
- v_up: float32 [2, 768, 3072], P(None, 'dp', 'head'), may hold values from 2.8051561e-14 to 1.12206244e-13
- v_down: float32 [2, 768, 3072], P(None, 'dp', 'head'), may hold values from 2.8051561e-14 to 1.12206244e-13
- v_emb: float32 [768, 128], P('dp'), may hold values from 2.8051561e-14 to 1.12206244e-13
- v_vectors: float32 [768, 7], P('dp'), may hold values from 2.805156e-12 to 1.1220624e-11
Outputs:
- loss: float32 [], replicated
- grad_norm: float32 [], replicated
- new_qkv: float32 [2, 768, 2304], P(None, 'dp', 'head')
- new_out: float32 [2, 768, 768], P(None, 'dp', 'head')
- new_up: float32 [2, 768, 3072], P(None, 'dp', 'head')
- new_down: float32 [2, 768, 3072], P(None, 'dp', 'head')
- new_emb: float32 [768, 128], P('dp')
- new_vectors: float32 [768, 7], P('dp')
- nm_qkv: float32 [2, 768, 2304], P(None, 'dp', 'head')
- nm_out: float32 [2, 768, 768], P(None, 'dp', 'head')
- nm_up: float32 [2, 768, 3072], P(None, 'dp', 'head')
- nm_down: float32 [2, 768, 3072], P(None, 'dp', 'head')
- nm_emb: float32 [768, 128], P('dp')
- nm_vectors: float32 [768, 7], P('dp')
- nv_qkv: float32 [2, 768, 2304], P(None, 'dp', 'head')
- nv_out: float32 [2, 768, 768], P(None, 'dp', 'head')
- nv_up: float32 [2, 768, 3072], P(None, 'dp', 'head')
- nv_down: float32 [2, 768, 3072], P(None, 'dp', 'head')
- nv_emb: float32 [768, 128], P('dp')
- nv_vectors: float32 [768, 7], P('dp')
Inputs may be any that keep to these rules, and one draw needn't show every extreme that they name: `neighbours`: the 256 indices of one query row are distinct. `nbr_mask`: slot 0 of every query row is live.
All inputs are finite; a program needn't handle non-finite values. No bound on the sum of `flags` on one device may be relied on, other than what follows from the above.
Results may differ from a plain program's by a relative error of at most 0.0003.
Values sent between devices are 32-bit elements; how exact they have to be, the bound alone decides.
No kernel may reach another device: no remote copies, remote signals or barrier semaphores. Data moves between devices by JAX's collectives and lax.ppermute only.
A program may use at most 256 MiB of HBM per device.

v0:
```python
from functools import partial
import math

import jax
import jax.numpy as jnp
from jax import lax
from jax.sharding import PartitionSpec as P

HD = 64


HIGHEST = lax.Precision.HIGHEST
LR_MATRIX = 0.03
LR_VECTOR = 0.2
DECAY = 0.1
CLIP_AT = 0.02


def matmul(left, right):
    return jnp.dot(left, right, precision=HIGHEST, preferred_element_type=jnp.float32)


def norm_rows(values, gain):
    centre = values - jnp.mean(values, axis=-1, keepdims=True)
    spread = jnp.mean(centre * centre, axis=-1, keepdims=True)
    return centre * lax.rsqrt(spread + 1e-05) * gain


def gain_norm(values, vec_weights, column):
    return norm_rows(values, vec_weights[:, column])


def gelu_tanh(values):
    return (
        0.5
        * values
        * (1.0 + jnp.tanh(0.7978845608 * (values + 0.044715 * values * values * values)))
    )


def allowed_rows(neigh, live, context_rows):
    query_rows, slot_count = neigh.shape
    group = math.gcd(slot_count, 32)
    neigh_blocks = jnp.transpose(neigh.reshape(query_rows, slot_count // group, group), (1, 0, 2))
    live_blocks = jnp.transpose(
        live.astype(jnp.float32).reshape(query_rows, slot_count // group, group), (1, 0, 2)
    )
    columns = jnp.arange(context_rows, dtype=jnp.int32)

    def merge_block(picks, block):
        neigh_part, live_part = block
        hits = (neigh_part[:, :, None] == columns[None, None, :]).astype(jnp.float32) * live_part[
            :, :, None
        ]
        return (jnp.maximum(picks, jnp.max(hits, axis=1)), None)

    picks, unused = lax.scan(
        merge_block, jnp.zeros((query_rows, context_rows), jnp.float32), (neigh_blocks, live_blocks)
    )
    return jnp.concatenate([jnp.ones((context_rows, context_rows), jnp.float32), picks], axis=0)


def attend(query, keys, values, allowed):
    scores = jnp.einsum("rhe,che->hrc", query, keys, precision=HIGHEST) * HD ** (-0.5)
    masked = jnp.where(allowed[None] > 0, scores, -1e30)
    top = jnp.max(masked, axis=2, keepdims=True)
    expo = jnp.exp(masked - top)
    probs = expo / jnp.sum(expo, axis=2, keepdims=True)
    return jnp.einsum("hrc,che->rhe", probs, values, precision=HIGHEST)


def table_pass(gathered, feat, target, neigh, live, flag, seed):
    w_qkv, w_out, w_up, w_down, emb_weight, vectors = gathered
    depth = w_qkv.shape[0]
    row_count = feat.shape[0]
    context_rows = row_count - neigh.shape[0]
    heads_here = w_qkv.shape[2] // (3 * HD)
    is_context = (jnp.arange(row_count) < context_rows).astype(jnp.float32)

    def embed(emb_part, vec_part):
        return (
            matmul(feat, emb_part.T)
            + (is_context * target)[:, None] * vec_part[:, 2 * depth + 1][None, :]
        )

    hidden, pull_embed = jax.vjp(embed, emb_weight, vectors)
    allowed = allowed_rows(neigh, live, context_rows)

    def attn_branch(normed, w_in, w_back):
        packed = matmul(normed, w_in).reshape(row_count, 3, heads_here, HD)
        mixed = attend(packed[:, 0], packed[:context_rows, 1], packed[:context_rows, 2], allowed)
        return matmul(mixed.reshape(row_count, heads_here * HD), w_back.T)

    def mlp_branch(normed, w_in, w_back):
        return matmul(gelu_tanh(matmul(normed, w_in)), w_back.T)

    saved = []
    for layer_idx in range(depth):
        normed, pull_first = jax.vjp(partial(gain_norm, column=layer_idx), hidden, vectors)
        branch, pull_attn = jax.vjp(attn_branch, normed, w_qkv[layer_idx], w_out[layer_idx])
        hidden = hidden + lax.psum(branch, "head")
        normed, pull_second = jax.vjp(partial(gain_norm, column=depth + layer_idx), hidden, vectors)
        branch, pull_mlp = jax.vjp(mlp_branch, normed, w_up[layer_idx], w_down[layer_idx])
        hidden = hidden + lax.psum(branch, "head")
        saved.append((pull_first, pull_attn, pull_second, pull_mlp))

    def finish(values, vec_part):
        final = norm_rows(values[context_rows:], vec_part[:, 2 * depth])
        predicted = matmul(final, vec_part[:, 2 * depth + 2])
        error = predicted - target[context_rows:]
        return jnp.sum(flag * error * error)

    loss_sum, pull_finish = jax.vjp(finish, hidden, vectors)
    back_flow, grad_vec = pull_finish(seed)
    grad_qkv, grad_out, grad_up, grad_down = ([], [], [], [])
    for layer_idx in reversed(range(depth)):
        pull_first, pull_attn, pull_second, pull_mlp = saved[layer_idx]
        d_normed, d_up, d_down = pull_mlp(back_flow)
        d_normed = lax.psum(d_normed, "head")
        d_hidden, d_vec = pull_second(d_normed)
        back_flow = back_flow + d_hidden
        grad_vec = grad_vec + d_vec
        d_normed, d_qkv, d_out = pull_attn(back_flow)
        d_normed = lax.psum(d_normed, "head")
        d_hidden, d_vec = pull_first(d_normed)
        back_flow = back_flow + d_hidden
        grad_vec = grad_vec + d_vec
        grad_qkv.insert(0, d_qkv)
        grad_out.insert(0, d_out)
        grad_up.insert(0, d_up)
        grad_down.insert(0, d_down)
    d_emb, d_vec = pull_embed(back_flow)
    grad_vec = grad_vec + d_vec
    return (
        loss_sum,
        (
            jnp.stack(grad_qkv),
            jnp.stack(grad_out),
            jnp.stack(grad_up),
            jnp.stack(grad_down),
            d_emb,
            grad_vec,
        ),
    )


def adamw(weight, grad, first, second, rate, decay, steps_taken):
    first_new = 0.9 * first + 0.1 * grad
    second_new = 0.999 * second + 0.001 * grad * grad
    first_hat = first_new / (1.0 - jnp.power(0.9, steps_taken))
    second_hat = second_new / (1.0 - jnp.power(0.999, steps_taken))
    weight_new = weight - rate * (first_hat / (jnp.sqrt(second_hat) + 1e-08) + decay * weight)
    return (weight_new, first_new, second_new)


def on_device(
    features,
    targets,
    neighbours,
    nbr_mask,
    flags,
    step_count,
    w_qkv,
    w_out,
    w_up,
    w_down,
    emb_weight,
    vectors,
    m_qkv,
    m_out,
    m_up,
    m_down,
    m_emb,
    m_vectors,
    v_qkv,
    v_out,
    v_up,
    v_down,
    v_emb,
    v_vectors,
):
    gathered = (
        lax.all_gather(w_qkv, "dp", axis=1, tiled=True),
        lax.all_gather(w_out, "dp", axis=1, tiled=True),
        lax.all_gather(w_up, "dp", axis=1, tiled=True),
        lax.all_gather(w_down, "dp", axis=1, tiled=True),
        lax.all_gather(emb_weight, "dp", axis=0, tiled=True),
        lax.all_gather(vectors, "dp", axis=0, tiled=True),
    )
    head_count = lax.axis_size("head")
    counted_local = jnp.sum(flags.astype(jnp.float32))
    counted = jnp.maximum(lax.psum(counted_local, "dp"), 1.0)
    seed = 1.0 / counted
    loss_local = jnp.zeros((), jnp.float32)
    totals = None
    for micro in range(features.shape[0]):
        part_loss, part_grads = table_pass(
            gathered,
            features[micro, 0],
            targets[micro, 0],
            neighbours[micro, 0],
            nbr_mask[micro, 0],
            flags[micro, 0].astype(jnp.float32),
            seed,
        )
        loss_local = loss_local + part_loss
        totals = (
            part_grads
            if totals is None
            else tuple((left + right for left, right in zip(totals, part_grads)))
        )
    owners = (w_qkv, w_out, w_up, w_down, emb_weight, vectors)
    split_dims = (1, 1, 1, 1, 0, 0)
    summed_all = lax.psum((totals[0], totals[1], totals[2], totals[3], totals[4], totals[5]), "dp")
    position = lax.axis_index("dp")
    owned = tuple(
        (
            lax.dynamic_slice_in_dim(
                summed_one,
                position * own_part.shape[split_dim],
                own_part.shape[split_dim],
                split_dim,
            )
            for summed_one, own_part, split_dim in zip(summed_all, owners, split_dims)
        )
    )
    squares = jnp.zeros((), jnp.float32)
    for index in range(6):
        weight_sq = jnp.sum(owned[index] * owned[index])
        squares = squares + (weight_sq / head_count if index >= 4 else weight_sq)
    square_total, loss_total = lax.psum((squares, loss_local / head_count), ("dp", "head"))
    grad_scale = jnp.ones((), jnp.float32)
    loss = loss_total / counted
    grad_norm = jnp.sqrt(square_total)
    factor = grad_scale * (CLIP_AT / jnp.maximum(grad_norm, CLIP_AT))
    steps_taken = step_count[0].astype(jnp.float32)
    firsts = (m_qkv, m_out, m_up, m_down, m_emb, m_vectors)
    seconds = (v_qkv, v_out, v_up, v_down, v_emb, v_vectors)
    new_w, new_m, new_v = ([], [], [])
    for index in range(6):
        rate = LR_VECTOR if index == 5 else LR_MATRIX
        decay = 0.0 if index == 5 else DECAY
        result = adamw(
            owners[index],
            owned[index] * factor,
            firsts[index],
            seconds[index],
            rate,
            decay,
            steps_taken,
        )
        new_w.append(result[0])
        new_m.append(result[1])
        new_v.append(result[2])
    return (
        loss,
        grad_norm,
        new_w[0],
        new_w[1],
        new_w[2],
        new_w[3],
        new_w[4],
        new_w[5],
        new_m[0],
        new_m[1],
        new_m[2],
        new_m[3],
        new_m[4],
        new_m[5],
        new_v[0],
        new_v[1],
        new_v[2],
        new_v[3],
        new_v[4],
        new_v[5],
    )


def solution(mesh):
    in_specs = (
        P(None, "dp", None, None),
        P(None, "dp", None),
        P(None, "dp", None, None),
        P(None, "dp", None, None),
        P(None, "dp", None),
        P(),
        P(None, "dp", "head"),
        P(None, "dp", "head"),
        P(None, "dp", "head"),
        P(None, "dp", "head"),
        P("dp", None),
        P("dp", None),
        P(None, "dp", "head"),
        P(None, "dp", "head"),
        P(None, "dp", "head"),
        P(None, "dp", "head"),
        P("dp", None),
        P("dp", None),
        P(None, "dp", "head"),
        P(None, "dp", "head"),
        P(None, "dp", "head"),
        P(None, "dp", "head"),
        P("dp", None),
        P("dp", None),
    )
    out_specs = (
        P(),
        P(),
        P(None, "dp", "head"),
        P(None, "dp", "head"),
        P(None, "dp", "head"),
        P(None, "dp", "head"),
        P("dp", None),
        P("dp", None),
        P(None, "dp", "head"),
        P(None, "dp", "head"),
        P(None, "dp", "head"),
        P(None, "dp", "head"),
        P("dp", None),
        P("dp", None),
        P(None, "dp", "head"),
        P(None, "dp", "head"),
        P(None, "dp", "head"),
        P(None, "dp", "head"),
        P("dp", None),
        P("dp", None),
    )
    return jax.shard_map(
        on_device, mesh=mesh, in_specs=in_specs, out_specs=out_specs, check_vma=False
    )
```

profile of v0, /device:TPU:0, one launch (start us, length us, event | category | flops | bytes accessed | tf_op | source)
XLA Modules:
  0.0 2039.0 jit_solution(9083527582310078894)
XLA Ops:
  10.7 32.6 %all-gather = f32[8,96,7]{1,2,0:T(8,128)S(1)} all-gather(f32[1,96,7]{1,2,0:T(8,128)} %bitcast.427), channel_id=1, replica_groups=mesh['dp'=8,'head'=4] {'dp'}, dimensions={0}, use_global_device_ids=true | all-gather | bytes 24192 | tf_op jit(solution)/shard_map/all_gather | solution.py:188
  44.0 32.7 %all_gather.18 = f32[768,128]{1,0:T(8,128)S(1)} all-gather(f32[96,128]{1,0:T(8,128)} %param.38), channel_id=1, replica_groups=mesh['dp'=8,'head'=4] {'dp'}, dimensions={0}, use_global_device_ids=true | all-gather | bytes 442368 | tf_op jit(solution)/shard_map/all_gather | solution.py:187
  78.3 40.8 %while.23 = (s32[]{:T(128)}, f32[256,512]{1,0:T(8,128)S(1)}, s32[8,256,32]{1,2,0:T(8,128)S(1)}, f32[8,256,32]{1,2,0:T(8,128)S(1)}, s32[]{:T(128)}, /*index=5*/s32[]{:T(128)}) while((s32[]{:T(128)}, f32[256,512]{1,0:T(8,128)S(1)}, s32[8,256,32]{1,2,0:T(8,128)S(1)}, f32[8,256,32]{1,2,0:T(8,128)S(1)}, s32[]{:T(128)}, ...), condition=%wide.region_26.27_spmd.clone, body=%wide.region_24.26_spmd.clone.sunk | while | flops 12713987 | bytes 2424927 | solution.py:57
  120.0 40.8 %while.22 = (s32[]{:T(128)}, f32[256,512]{1,0:T(8,128)S(1)}, s32[8,256,32]{1,2,0:T(8,128)S(1)}, f32[8,256,32]{1,2,0:T(8,128)S(1)}, s32[]{:T(128)}, /*index=5*/s32[]{:T(128)}) while((s32[]{:T(128)}, f32[256,512]{1,0:T(8,128)S(1)}, s32[8,256,32]{1,2,0:T(8,128)S(1)}, f32[8,256,32]{1,2,0:T(8,128)S(1)}, s32[]{:T(128)}, ...), condition=%wide.region_4.5_spmd.clone, body=%wide.region_2.4_spmd.clone.sunk | while | flops 12713987 | bytes 2424927 | solution.py:57
  219.7 93.4 %all-reduce.66.cloned.1.call-done = (f32[768,768]{0,1:T(8,128)}, f32[768,768]{0,1:T(8,128)}) async-done(((f32[768,768]{0,1:T(8,128)}, f32[768,768]{0,1:T(8,128)}), (f32[768,768]{0,1:T(8,128)}, f32[768,768]{0,1:T(8,128)})) %all-reduce.66.cloned.1.call-update) | async-done | bytes 4718608 | tf_op jit(solution)/shard_map/psum | solution.py:101
  319.1 76.1 %all-gather.10.cloned.1.call-done = f32[2,768,768]{2,1,0:T(8,128)} async-done(((f32[2,96,768]{2,1,0:T(8,128)}), f32[2,768,768]{2,1,0:T(8,128)}) %all-gather.10.cloned.1.call-update) | async-done | bytes 4718608 | tf_op jit(solution)/shard_map/all_gather | solution.py:185
  395.2 9.4 fusion.105
  404.7 8.0 fusion.119
  412.7 62.6 %all-gather.12.cloned.1.call-done = f32[2,768,768]{2,1,0:T(8,128)} async-done(((f32[2,96,768]{2,1,0:T(8,128)}), f32[2,768,768]{2,1,0:T(8,128)}) %all-gather.12.cloned.1.call-update) | async-done | bytes 4718608 | tf_op jit(solution)/shard_map/all_gather | solution.py:186
  475.3 10.6 fusion.153
  497.0 89.1 %all-reduce.64.cloned.1.call-done = (f32[768,768]{0,1:T(8,128)}, f32[768,768]{0,1:T(8,128)}) async-done(((f32[768,768]{0,1:T(8,128)}, f32[768,768]{0,1:T(8,128)}), (f32[768,768]{0,1:T(8,128)}, f32[768,768]{0,1:T(8,128)})) %all-reduce.64.cloned.1.call-update) | async-done | bytes 4718608 | tf_op jit(solution)/shard_map/psum | solution.py:104
  632.3 94.3 %all-reduce.62.cloned.1.call-done = (f32[768,768]{0,1:T(8,128)}, f32[768,768]{0,1:T(8,128)}) async-done(((f32[768,768]{0,1:T(8,128)}, f32[768,768]{0,1:T(8,128)}), (f32[768,768]{0,1:T(8,128)}, f32[768,768]{0,1:T(8,128)})) %all-reduce.62.cloned.1.call-update) | async-done | bytes 4718608 | tf_op jit(solution)/shard_map/psum | solution.py:101
  739.6 8.1 fusion.157
  755.9 7.9 fusion.156
  765.1 22.0 %psum.184 = f32[]{:T(128)} all-reduce(f32[]{:T(128)} %convert_reduce_fusion.4), channel_id=1, replica_groups=mesh['dp'=8,'head'=4] {'dp'}, use_global_device_ids=true, to_apply=%region_46.47 | all-reduce | flops 1 | bytes 8 | tf_op jit(solution)/shard_map/psum | solution.py:192
  788.5 69.9 %all-reduce.60.cloned.1.call-done = (f32[768,768]{0,1:T(8,128)}, f32[768,768]{0,1:T(8,128)}) async-done(((f32[768,768]{0,1:T(8,128)}, f32[768,768]{0,1:T(8,128)}), (f32[768,768]{0,1:T(8,128)}, f32[768,768]{0,1:T(8,128)})) %all-reduce.60.cloned.1.call-update) | async-done | bytes 4718608 | tf_op jit(solution)/shard_map/psum | solution.py:104
  866.2 10.2 fusion.39
  876.5 8.1 fusion.33
  904.2 89.6 %all-reduce.58.cloned.1.call-done = (f32[768,768]{0,1:T(8,128)}, f32[768,768]{0,1:T(8,128)}) async-done(((f32[768,768]{0,1:T(8,128)}, f32[768,768]{0,1:T(8,128)}), (f32[768,768]{0,1:T(8,128)}, f32[768,768]{0,1:T(8,128)})) %all-reduce.58.cloned.1.call-update) | async-done | bytes 4718608 | tf_op jit(solution)/shard_map/psum | solution.py:119
  1056.9 7.8 fusion.140
  1074.3 10.1 fusion.179
  1099.1 7.7 fusion.191
  1106.8 59.7 %all-reduce.56.cloned.1.call-done = (f32[768,768]{0,1:T(8,128)}, f32[768,768]{0,1:T(8,128)}) async-done(((f32[768,768]{0,1:T(8,128)}, f32[768,768]{0,1:T(8,128)}), (f32[768,768]{0,1:T(8,128)}, f32[768,768]{0,1:T(8,128)})) %all-reduce.56.cloned.1.call-update) | async-done | bytes 4718608 | tf_op jit(solution)/shard_map/psum | solution.py:124
  1179.0 11.7 fusion.36
  1190.7 11.1 fusion.30
  1209.1 7.6 fusion.148
  1245.5 8.0 convolution_bitcast_fusion.1
  1261.1 50.1 %all-reduce.54.cloned.1.call-done = (f32[768,768]{0,1:T(8,128)}, f32[768,768]{0,1:T(8,128)}) async-done(((f32[768,768]{0,1:T(8,128)}, f32[768,768]{0,1:T(8,128)}), (f32[768,768]{0,1:T(8,128)}, f32[768,768]{0,1:T(8,128)})) %all-reduce.54.cloned.1.call-update) | async-done | bytes 4718608 | tf_op jit(solution)/shard_map/psum | solution.py:119
  1431.6 58.4 %all-reduce.52.cloned.1.call-done = (f32[768,768]{0,1:T(8,128)}, f32[768,768]{0,1:T(8,128)}) async-done(((f32[768,768]{0,1:T(8,128)}, f32[768,768]{0,1:T(8,128)}), (f32[768,768]{0,1:T(8,128)}, f32[768,768]{0,1:T(8,128)})) %all-reduce.52.cloned.1.call-update) | async-done | bytes 4718608 | tf_op jit(solution)/shard_map/psum | solution.py:124
  1528.4 39.6 %psum.198 = f32[768,7]{0,1:T(8,128)S(1)} all-reduce(f32[768,7]{0,1:T(8,128)S(1)} %add_add_fusion.18), channel_id=1, replica_groups=mesh['dp'=8,'head'=4] {'dp'}, use_global_device_ids=true, to_apply=%region_109.110 | all-reduce | flops 5376 | bytes 43008 | tf_op jit(solution)/shard_map/psum | solution.py:214
  1569.3 387.9 %all-reduce.50.cloned.1.call-done = (f32[2,768,576]{1,2,0:T(8,128)}, f32[2,768,192]{1,2,0:T(8,128)}, f32[2,768,768]{2,1,0:T(8,128)}, f32[2,768,768]{2,1,0:T(8,128)}, f32[768,128]{1,0:T(8,128)}) async-done(((f32[2,768,576]{1,2,0:T(8,128)}, f32[2,768,192]{1,2,0:T(8,128)}, f32[2,768,768]{2,1,0:T(8,128)}, f32[2,768,768]{2,1,0:T(8,128)}, f32[768,128]{1,0:T(8,128)}), (f32[2,768,576]{1,2,0:T(8,128)}, ...) | async-done | bytes 14549008 | tf_op jit(solution)/shard_map/psum | solution.py:214
  1969.8 39.3 %all-reduce.30 = (f32[]{:T(128)}, f32[]{:T(128)}) all-reduce(f32[]{:T(128)S(6)} %div.400, f32[]{:T(128)S(6)} %add.514), channel_id=1, replica_groups=mesh['dp'=8,'head'=4] {'dp','head'}, use_global_device_ids=true, to_apply=%region_44.45 | all-reduce | flops 2 | bytes 16 | tf_op jit(solution)/shard_map/psum | solution.py:231
  (813 shorter events, 586.9 us)
Async XLA Ops:
  7.2 70.9 %copy-start.133 = (s32[2,1,256,256]{3,2,1,0:T(8,128)S(1)}, s32[2,1,256,256]{3,2,1,0:T(8,128)}, u32[]{:S(2)}) copy-start(s32[2,1,256,256]{3,2,1,0:T(8,128)} %param.31) | copy-start | bytes 1572868
  7.2 162.7 %all-gather.6.cloned.1.call-start = ((), (), s32[]{:S(2)}) async-start(), calls=%async_computation | async-start | bytes 4423680 | tf_op jit(solution)/shard_map/all_gather | solution.py:183
  7.9 201.9 %all-gather.8.cloned.1.call-start = ((), (), s32[]{:S(2)}) async-start(), calls=%async_computation.1 | async-start | bytes 1769472 | tf_op jit(solution)/shard_map/all_gather | solution.py:184
  8.7 304.4 %all-reduce.66.cloned.1.call-start = ((), (), s32[]{:S(2)}) async-start(), calls=%async_computation.12 | async-start | bytes 9437184 | tf_op jit(solution)/shard_map/psum | solution.py:101
  44.0 360.6 %copy-start.137 = (f32[768]{0:T(1024)}, f32[768]{0:T(1024)S(1)}, u32[]{:S(2)}) copy-start(f32[768]{0:T(1024)S(1)} %get-tuple-element.238) | copy-start | bytes 9220
  44.0 821.5 %copy-start.139 = (f32[768]{0:T(1024)}, f32[768]{0:T(1024)S(1)}, u32[]{:S(2)}) copy-start(f32[768]{0:T(1024)S(1)} %get-tuple-element.235) | copy-start | bytes 9220
  218.3 176.9 %all-gather.10.cloned.1.call-start = ((), (), s32[]{:S(2)}) async-start(), calls=%async_computation.2 | async-start | bytes 5308416 | tf_op jit(solution)/shard_map/all_gather | solution.py:185
  218.9 256.4 %all-gather.12.cloned.1.call-start = ((), (), s32[]{:S(2)}) async-start(), calls=%async_computation.3 | async-start | bytes 5308416 | tf_op jit(solution)/shard_map/all_gather | solution.py:186
  219.5 366.6 %all-reduce.64.cloned.1.call-start = ((), (), s32[]{:S(2)}) async-start(), calls=%async_computation.11 | async-start | bytes 9437184 | tf_op jit(solution)/shard_map/psum | solution.py:104
  317.6 77.6 %copy-start.4 = (f32[768,768]{0,1:T(8,128)}, f32[768,768]{0,1:T(8,128)S(1)}, u32[]{:S(2)}) copy-start(f32[768,768]{0,1:T(8,128)S(1)} %get-tuple-element.349) | copy-start | bytes 7077892
  317.6 87.0 %copy-start.141 = (f32[768]{0:T(1024)}, f32[768]{0:T(1024)S(1)}, u32[]{:S(2)}) copy-start(f32[768]{0:T(1024)S(1)} %broadcast_multiply_fusion.6) | copy-start | bytes 9220
  317.9 86.7 %copy-start.143 = (f32[768]{0:T(1024)}, f32[768]{0:T(1024)S(1)}, u32[]{:S(2)}) copy-start(f32[768]{0:T(1024)S(1)} %broadcast_multiply_fusion.2) | copy-start | bytes 9220
  319.1 85.6 %copy-start.178 = (f32[768]{0:T(1024)}, f32[768]{0:T(1024)S(1)}, u32[]{:S(2)}) copy-start(f32[768]{0:T(1024)S(1)} %multiply_reduce_fusion.24) | copy-start | bytes 9220
  319.1 85.6 %copy-start.163 = (f32[768]{0:T(1024)}, f32[768]{0:T(1024)S(1)}, u32[]{:S(2)}) copy-start(f32[768]{0:T(1024)S(1)} %fusion.368) | copy-start | bytes 9220
  319.1 85.6 %copy-start.161 = (f32[768]{0:T(1024)}, f32[768]{0:T(1024)S(1)}, u32[]{:S(2)}) copy-start(f32[768]{0:T(1024)S(1)} %fusion.372) | copy-start | bytes 9220
  412.7 73.2 %copy-start.113 = (f32[768,768]{1,0:T(8,128)S(1)}, f32[768,768]{1,0:T(8,128)}, u32[]{:S(2)}) copy-start(f32[768,768]{1,0:T(8,128)} %fusion.105) | copy-start | bytes 7077892
  493.6 233.0 %all-reduce.62.cloned.1.call-start = ((), (), s32[]{:S(2)}) async-start(), calls=%async_computation.10 | async-start | bytes 9437184 | tf_op jit(solution)/shard_map/psum | solution.py:101
  632.0 226.3 %all-reduce.60.cloned.1.call-start = ((), (), s32[]{:S(2)}) async-start(), calls=%async_computation.9 | async-start | bytes 9437184 | tf_op jit(solution)/shard_map/psum | solution.py:104
  763.8 230.0 %all-reduce.58.cloned.1.call-start = ((), (), s32[]{:S(2)}) async-start(), calls=%async_computation.8 | async-start | bytes 9437184 | tf_op jit(solution)/shard_map/psum | solution.py:119
  899.3 267.2 %all-reduce.56.cloned.1.call-start = ((), (), s32[]{:S(2)}) async-start(), calls=%async_computation.7 | async-start | bytes 9437184 | tf_op jit(solution)/shard_map/psum | solution.py:124
  1001.6 26.0 %copy-start.40 = (f32[768,768]{0,1:T(8,128)}, f32[768,768]{0,1:T(8,128)S(1)}, u32[]{:S(2)}) copy-start(f32[768,768]{0,1:T(8,128)S(1)} %get-tuple-element.329) | copy-start | bytes 7077892
  1072.0 239.3 %all-reduce.54.cloned.1.call-start = ((), (), s32[]{:S(2)}) async-start(), calls=%async_computation.6 | async-start | bytes 9437184 | tf_op jit(solution)/shard_map/psum | solution.py:119
  1216.7 273.3 %all-reduce.52.cloned.1.call-start = ((), (), s32[]{:S(2)}) async-start(), calls=%async_computation.5 | async-start | bytes 9437184 | tf_op jit(solution)/shard_map/psum | solution.py:124
  1253.5 57.7 %copy-start.6 = (f32[768,768]{0,1:T(8,128)S(1)}, f32[768,768]{0,1:T(8,128)}, u32[]{:S(2)}) copy-start(f32[768,768]{0,1:T(8,128)} %copy-done.4) | copy-start | bytes 7077892
  1253.5 57.7 %copy-start.144 = (f32[768]{0:T(1024)S(1)}, f32[768]{0:T(1024)}, u32[]{:S(2)}) copy-start(f32[768]{0:T(1024)} %copy-done.143) | copy-start | bytes 9220
  1324.2 27.2 %copy-start.23 = (f32[768,768]{0,1:T(8,128)}, f32[768,768]{0,1:T(8,128)S(1)}, u32[]{:S(2)}) copy-start(f32[768,768]{0,1:T(8,128)S(1)} %get-tuple-element.371) | copy-start | bytes 7077892
  1395.5 561.7 %all-reduce.50.cloned.1.call-start = ((), (), s32[]{:S(2)}) async-start(), calls=%async_computation.4 | async-start | bytes 29097984 | tf_op jit(solution)/shard_map/psum | solution.py:214
  1527.7 441.8 %copy-start.134 = (f32[2,96,576]{2,1,0:T(8,128)S(1)}, f32[2,96,576]{2,1,0:T(8,128)}, u32[]{:S(2)}) copy-start(f32[2,96,576]{2,1,0:T(8,128)} %param.46) | copy-start | bytes 1327108
  1528.1 482.4 %copy-start.125 = (f32[2,96,192]{1,2,0:T(8,128)S(1)}, f32[2,96,192]{1,2,0:T(8,128)}, u32[]{:S(2)}) copy-start(f32[2,96,192]{1,2,0:T(8,128)} %copy.302) | copy-start | bytes 442372
  1568.0 444.5 %copy-start.175 = (f32[768,7]{0,1:T(8,128)}, f32[768,7]{0,1:T(8,128)S(1)}, u32[]{:S(2)}) copy-start(f32[768,7]{0,1:T(8,128)S(1)} %psum.198) | copy-start | bytes 64516
  1959.3 53.9 %copy-start.105 = (f32[2,96,576]{1,2,0:T(8,128)S(1)}, f32[2,96,576]{1,2,0:T(8,128)}, u32[]{:S(2)}) copy-start(f32[2,96,576]{1,2,0:T(8,128)} %copy.300) | copy-start | bytes 1327108
  1959.3 53.9 %copy-start.106 = (f32[2,96,576]{1,2,0:T(8,128)S(1)}, f32[2,96,576]{1,2,0:T(8,128)}, u32[]{:S(2)}) copy-start(f32[2,96,576]{1,2,0:T(8,128)} %copy.297) | copy-start | bytes 1327108
  (204 other events, 1195.3 us)
Sparse Core Ops, SparseCore 0:
  10.2 78.2 all-gather.5
  90.7 43.8 all-gather.7
  218.4 94.6 all-reduce.65
  315.1 80.0 all-gather.9
  397.2 78.0 all-gather.11
  493.7 92.3 all-reduce.63
  632.2 94.3 all-reduce.61
  763.9 94.3 all-reduce.59
  899.4 94.3 all-reduce.57
  1072.1 94.3 all-reduce.55
  1216.9 94.3 all-reduce.53
  1395.7 94.3 all-reduce.51
  1503.7 453.5 all-reduce.49
where the time goes:
time: 2050 us; the launch traced here: 2040 us
  waiting for transfers between devices  1130 us (55%)
  matrix products  449 us (22%)
  other arithmetic  185 us (9%)
  blocking collectives  166 us (8%)
  local copies, waits for them, and re-layouts  75.4 us (4%)
  between operations  27.5 us (1%)
    psum x1, waiting for transfers between devices, on_device(): lax.psum((totals[0], totals[1], totals[2], totals[3], totals[4], totals[5...  388 us
    psum x4, waiting for transfers between devices, table_pass(): hidden = hidden + lax.psum(branch, 'head')  347 us
    dot_general x56, matrix products, matmul(): jnp.dot(left, right, precision=HIGHEST, preferred_element_type=jnp.float32)  327 us
    psum x4, waiting for transfers between devices, table_pass(): d_normed = lax.psum(d_normed, 'head')  258 us
    all_gather x1, waiting for transfers between devices, on_device(): lax.all_gather(w_up, 'dp', axis=1, tiled=True)  76.1 us
    reduce_max x16, other arithmetic, merge_block(): return (jnp.maximum(picks, jnp.max(hits, axis=1)), None)  74.4 us
    dot_general x12, matrix products, attend(): return jnp.einsum('hrc,che->rhe', probs, values, precision=HIGHEST)  63.9 us
    all_gather x1, waiting for transfers between devices, on_device(): lax.all_gather(w_down, 'dp', axis=1, tiled=True)  62.6 us
  transfers between devices with their start and end apart: 13, of which 11 were waited for; matrix products, arithmetic and copies ran while one was open for 15% of the time, Pallas kernels for 0%

commit v1 on v0

v1 whole, which is shorter than its diff:
```python
import math

import jax
import jax.numpy as jnp
from jax import lax
from jax.sharding import Mesh, PartitionSpec as P

HD = 64
HIGH = lax.Precision.HIGH
LR_MATRIX = 0.03
LR_VECTOR = 0.2
DECAY = 0.1
CLIP_AT = 0.02
EPS = 1e-05
SWAP = ((0, 1), (1, 0))
AXES = ("dh", "dl", "hh", "hl")


def dot(a, b, ca, cb):
    return lax.dot_general(
        a, b, (((ca,), (cb,)), ((), ())), precision=HIGH, preferred_element_type=jnp.float32
    )


def swap(values, axis):
    return lax.ppermute(values, axis, SWAP)


def head_sum(part):
    half = part.shape[0] // 2
    mine = part[:half] + swap(part[half:], "hl")
    mine = mine + swap(mine, "hh")
    return jnp.concatenate([mine, swap(mine, "hl")], axis=0)


def gather_rows(block):
    near = lax.all_gather(block, "dh", axis=0, tiled=True)
    return jnp.concatenate([near, swap(near, "dl")], axis=0)


def scatter_rows(grad):
    half = grad.shape[0] // 2
    near = grad[:half] + swap(grad[half:], "dl")
    return lax.psum_scatter(near, "dh", scatter_dimension=0, tiled=True)


def norm_stats(x):
    centre = x - jnp.mean(x, axis=-1, keepdims=True)
    rstd = lax.rsqrt(jnp.mean(centre * centre, axis=-1, keepdims=True) + EPS)
    return centre * rstd, rstd


def norm_back(dn, nh, rstd):
    return rstd * (
        dn - jnp.mean(dn, axis=-1, keepdims=True) - nh * jnp.mean(dn * nh, axis=-1, keepdims=True)
    )


def gelu(u):
    return 0.5 * u * (1.0 + jnp.tanh(0.7978845608 * (u + 0.044715 * u * u * u)))


def gelu_slope(u):
    t = jnp.tanh(0.7978845608 * (u + 0.044715 * u * u * u))
    return 0.5 * (1.0 + t) + 0.5 * u * (1.0 - t * t) * 0.7978845608 * (1.0 + 3.0 * 0.044715 * u * u)


def roll_half(x, c, axis=0):
    half = x.shape[axis] // 2
    a = lax.slice_in_dim(x, 0, half, axis=axis)
    b = lax.slice_in_dim(x, half, 2 * half, axis=axis)
    return jnp.where(
        c == 0, jnp.concatenate([a, b], axis=axis), jnp.concatenate([b, a], axis=axis)
    )


def halves(ctx, qry):
    hc, hq = ctx.shape[0] // 2, qry.shape[0] // 2
    return jnp.concatenate([ctx[:hc], qry[:hq], ctx[hc:], qry[hq:]], axis=0)


def ctx_of(x, hc, hq):
    return jnp.concatenate([x[:hc], x[hc + hq : 2 * hc + hq]], axis=0)


def qry_of(x, hc, hq):
    return jnp.concatenate([x[hc : hc + hq], x[2 * hc + hq :]], axis=0)


def neighbour_mask(neigh, live, context_rows, c):
    words = context_rows // 32
    col = jnp.bitwise_xor(neigh, c * (context_rows // 2))
    bit = jnp.left_shift(live, jnp.bitwise_and(col, 31))
    at = jnp.right_shift(col, 5)
    word = jnp.sum(
        jnp.where(at[:, None, :] == jnp.arange(words, dtype=jnp.int32)[None, :, None], bit[:, None, :], 0),
        axis=-1,
    )
    spread = jnp.broadcast_to(word[:, :, None], word.shape + (32,)).reshape(word.shape[0], context_rows)
    shift = jnp.bitwise_and(jnp.arange(context_rows, dtype=jnp.int32), 31)
    return jnp.bitwise_and(jnp.right_shift(spread, shift[None, :]), 1)


def softmax_rows(s):
    top = jnp.max(s, axis=-1, keepdims=True)
    e = jnp.exp(s - top)
    return e / jnp.sum(e, axis=-1, keepdims=True)


def heads_dot(a, b, ca, cb):
    return lax.dot_general(
        a, b, (((ca,), (cb,)), ((0,), (0,))), precision=HIGH, preferred_element_type=jnp.float32
    )


def split_heads(x):
    return jnp.transpose(x.reshape(x.shape[0], -1, HD), (1, 0, 2))


def merge_heads(x):
    return jnp.transpose(x, (1, 0, 2)).reshape(x.shape[1], -1)


def adamw(weight, grad, first, second, rate, decay, steps_taken):
    first_new = 0.9 * first + 0.1 * grad
    second_new = 0.999 * second + 0.001 * grad * grad
    first_hat = first_new / (1.0 - jnp.power(0.9, steps_taken))
    second_hat = second_new / (1.0 - jnp.power(0.999, steps_taken))
    weight_new = weight - rate * (first_hat / (jnp.sqrt(second_hat) + 1e-08) + decay * weight)
    return (weight_new, first_new, second_new)


def on_device(
    features,
    targets,
    neighbours,
    nbr_mask,
    flags,
    step_count,
    w_qkv,
    w_out,
    w_up,
    w_down,
    emb_weight,
    vectors,
    m_qkv,
    m_out,
    m_up,
    m_down,
    m_emb,
    m_vectors,
    v_qkv,
    v_out,
    v_up,
    v_down,
    v_emb,
    v_vectors,
):
    depth = w_qkv.shape[0]
    micros = features.shape[0]
    rows = features.shape[2]
    feats = features.shape[3]
    queries = neighbours.shape[2]
    context = rows - queries
    hc, hq = context // 2, queries // 2
    width = w_qkv.shape[2] // 3
    c = lax.axis_index("hl")
    scale = HD ** (-0.5)

    small = gather_rows(jnp.concatenate([emb_weight, vectors], axis=1))
    emb, vec = small[:, :feats], small[:, feats:].T
    wq, wo, wu, wd = [], [], [], []
    for l in range(depth):
        packed = gather_rows(jnp.concatenate([w_qkv[l], w_out[l]], axis=1))
        wq.append(packed[:, : 3 * width])
        wo.append(packed[:, 3 * width :])
        wu.append(gather_rows(w_up[l]))
        wd.append(gather_rows(w_down[l]))

    def gain(col):
        return vec[col][None, :]

    tables = []
    for m in range(micros):
        feat = features[m, 0]
        feat = halves(roll_half(feat[:context], c), roll_half(feat[context:], c))
        t_ctx = roll_half(targets[m, 0][:context], c)
        t_qry = roll_half(targets[m, 0][context:], c)
        t_in = halves(t_ctx[:, None], jnp.zeros((queries, 1), jnp.float32))
        neigh = roll_half(neighbours[m, 0], c)
        live = roll_half(nbr_mask[m, 0], c)
        flag = roll_half(flags[m, 0], c).astype(jnp.float32)
        mask = neighbour_mask(neigh, live, context, c)
        x = dot(feat, emb, 1, 1) + t_in * gain(2 * depth + 1)
        tables.append(dict(feat=feat, t_in=t_in, t_qry=t_qry, flag=flag, mask=mask, x=x))
    full_mask = [
        halves(jnp.ones((context, context), jnp.int32), t["mask"])[None] > 0 for t in tables
    ]
    qry_mask = [t["mask"][None] > 0 for t in tables]

    saved = [[None] * depth for _ in range(micros)]
    xs = [t["x"] for t in tables]
    for l in range(depth):
        last = l == depth - 1
        for m in range(micros):
            x = xs[m]
            nh, rstd = norm_stats(x)
            n = nh * gain(l)
            nq = qry_of(n, hc, hq) if last else n
            nc = ctx_of(n, hc, hq)
            q = split_heads(dot(nq, wq[l][:, :width], 1, 0))
            kv = dot(nc, wq[l][:, width:], 1, 0)
            k, v = split_heads(kv[:, :width]), split_heads(kv[:, width:])
            s = heads_dot(q, k, 2, 2) * scale
            s = jnp.where(qry_mask[m] if last else full_mask[m], s, -1e30)
            p = softmax_rows(s)
            o = merge_heads(heads_dot(p, v, 2, 1))
            total = head_sum(dot(o, wo[l], 1, 1))
            base = qry_of(x, hc, hq) if last else x
            x1 = base + total
            saved[m][l] = dict(nh=nh, rstd=rstd, nq=nq, nc=nc, q=q, k=k, v=v, p=p, o=o)
            xs[m] = x1
        for m in range(micros):
            x1 = xs[m]
            nh, rstd = norm_stats(x1)
            n = nh * gain(depth + l)
            u = dot(n, wu[l], 1, 0)
            g = gelu(u)
            xs[m] = x1 + head_sum(dot(g, wd[l], 1, 1))
            saved[m][l].update(nh2=nh, rstd2=rstd, n2=n, u=u, g=g)

    grads = [dict() for _ in range(depth)]
    g_vec = [jnp.zeros((vec.shape[1],), jnp.float32) for _ in range(vec.shape[0])]

    def add(store, key, value):
        store[key] = value if key not in store else store[key] + value

    share = 1.0 / (lax.axis_size("hh") * lax.axis_size("hl"))
    loss_sum = jnp.zeros((), jnp.float32)
    dxs = []
    for m in range(micros):
        t = tables[m]
        nh, rstd = norm_stats(xs[m])
        nf = nh * gain(2 * depth)
        r = gain(2 * depth + 2)
        err = jnp.sum(nf * r, axis=1) - t["t_qry"]
        loss_sum = loss_sum + jnp.sum(t["flag"] * err * err)
        dpred = (2.0 * t["flag"] * err)[:, None]
        g_vec[2 * depth + 2] += share * jnp.sum(nf * dpred, axis=0)
        dy = dpred * r
        g_vec[2 * depth] += share * jnp.sum(dy * nh, axis=0)
        dxs.append(norm_back(dy * gain(2 * depth), nh, rstd))

    for l in reversed(range(depth)):
        last = l == depth - 1
        for m in range(micros):
            k_ = saved[m][l]
            dy = dxs[m]
            dg = dot(dy, wd[l], 1, 0)
            add(grads[l], "down", dot(dy, k_["g"], 0, 0))
            du = dg * gelu_slope(k_["u"])
            add(grads[l], "up", dot(k_["n2"], du, 0, 0))
            dn = head_sum(dot(du, wu[l], 1, 1))
            g_vec[depth + l] += share * jnp.sum(dn * k_["nh2"], axis=0)
            dxs[m] = dy + norm_back(dn * gain(depth + l), k_["nh2"], k_["rstd2"])
        for m in range(micros):
            k_ = saved[m][l]
            dy = dxs[m]
            q, k, v, p, o = k_["q"], k_["k"], k_["v"], k_["p"], k_["o"]
            do = dot(dy, wo[l], 1, 0)
            add(grads[l], "out", dot(dy, o, 0, 0))
            doh = split_heads(do)
            dp = heads_dot(doh, v, 2, 2)
            rowsum = jnp.sum(split_heads(do * o), axis=-1, keepdims=True)
            ds = p * (dp - rowsum) * scale
            dv = merge_heads(heads_dot(p, doh, 1, 1))
            dq = merge_heads(heads_dot(ds, k, 2, 1))
            dk = merge_heads(heads_dot(ds, q, 1, 1))
            dkv = jnp.concatenate([dk, dv], axis=1)
            add(
                grads[l],
                "qkv",
                jnp.concatenate([dot(k_["nq"], dq, 0, 0), dot(k_["nc"], dkv, 0, 0)], axis=1),
            )
            dn_q = dot(dq, wq[l][:, :width], 1, 1)
            dn_c = dot(dkv, wq[l][:, width:], 1, 1)
            if last:
                dn = halves(dn_c, dn_q)
                dres = halves(jnp.zeros((context, dy.shape[1]), jnp.float32), dy)
            else:
                dn = dn_q + halves(dn_c, jnp.zeros((queries, dy.shape[1]), jnp.float32))
                dres = dy
            if l > 0:
                dn = head_sum(dn)
                g_vec[l] += share * jnp.sum(dn * k_["nh"], axis=0)
                dxs[m] = dres + norm_back(dn * gain(l), k_["nh"], k_["rstd"])
            else:
                g_vec[l] += jnp.sum(dn * k_["nh"], axis=0)
                dxs[m] = share * dres + norm_back(dn * gain(l), k_["nh"], k_["rstd"])
    g_emb = 0.0
    for m in range(micros):
        t = tables[m]
        g_emb = g_emb + dot(dxs[m], t["feat"], 0, 0)
        g_vec[2 * depth + 1] += jnp.sum(dxs[m] * t["t_in"], axis=0)

    own_small = scatter_rows(jnp.concatenate([g_emb, jnp.stack(g_vec, axis=1)], axis=1))
    own_small = own_small + swap(own_small, "hl")
    own_small = own_small + swap(own_small, "hh")
    own = [[], [], [], []]
    for l in range(depth):
        packed = scatter_rows(jnp.concatenate([grads[l]["qkv"], grads[l]["out"]], axis=1))
        own[0].append(packed[:, : 3 * width])
        own[1].append(packed[:, 3 * width :])
        own[2].append(scatter_rows(grads[l]["up"]))
        own[3].append(scatter_rows(grads[l]["down"]))
    owned = [jnp.stack(o) for o in own] + [own_small[:, :feats], own_small[:, feats:]]

    squares = share * jnp.sum(own_small * own_small)
    for o in owned[:4]:
        squares = squares + jnp.sum(o * o)
    counted = share * jnp.sum(flags.astype(jnp.float32))
    sums = lax.psum(jnp.stack([squares, share * loss_sum, counted]), AXES)
    counted = jnp.maximum(sums[2], 1.0)
    loss = sums[1] / counted
    grad_norm = jnp.sqrt(sums[0]) / counted
    factor = CLIP_AT / jnp.maximum(grad_norm, CLIP_AT) / counted
    steps_taken = step_count[0].astype(jnp.float32)
    weights = (w_qkv, w_out, w_up, w_down, emb_weight, vectors)
    firsts = (m_qkv, m_out, m_up, m_down, m_emb, m_vectors)
    seconds = (v_qkv, v_out, v_up, v_down, v_emb, v_vectors)
    new_w, new_m, new_v = [], [], []
    for i in range(6):
        rate = LR_VECTOR if i == 5 else LR_MATRIX
        decay = 0.0 if i == 5 else DECAY
        result = adamw(weights[i], owned[i] * factor, firsts[i], seconds[i], rate, decay, steps_taken)
        new_w.append(result[0])
        new_m.append(result[1])
        new_v.append(result[2])
    return (loss, grad_norm, *new_w, *new_m, *new_v)


def solution(mesh):
    dp, head = mesh.shape["dp"], mesh.shape["head"]
    fine = Mesh(mesh.devices.reshape(dp // 2, 2, head // 2, 2), AXES)
    rows, cols = ("dh", "dl"), ("hh", "hl")
    data = (
        P(None, rows, None, None),
        P(None, rows, None),
        P(None, rows, None, None),
        P(None, rows, None, None),
        P(None, rows, None),
        P(),
    )
    params = (P(None, rows, cols),) * 4 + (P(rows, None),) * 2
    return jax.shard_map(
        on_device,
        mesh=fine,
        in_specs=data + params * 3,
        out_specs=(P(), P()) + params * 3,
        check_vma=False,
    )
```

time: 2050 us -> 944 us (0.46)
  waiting for transfers between devices: 1130 us -> 452 us
  matrix products: 449 us -> 187 us
  blocking collectives: 166 us -> 55.5 us
  other arithmetic: 185 us -> 98.1 us
  starting transfers between devices: 1.28 us -> 30.4 us
    psum x9 -> x0, waiting for transfers between devices: 992 us -> none  [the longest x1 388 us: on_device(): lax.psum((totals[0], totals[1], totals[2], totals[3], totals[4], totals[5...]
    ppermute x0 -> x58, waiting for transfers between devices: none -> 438 us  [swap(): return lax.ppermute(values, axis, SWAP)]
    dot_general x80 -> x88, matrix products: 449 us -> 187 us  [the longest x64 129 us: dot(): lax.dot_general(a, b, (((ca,), (cb,)), ((), ())), precision=HIGH, preferr...]
    all_gather x4 -> x6, waiting for transfers between devices: 139 us -> 0.04 us  [gather_rows(): near = lax.all_gather(block, 'dh', axis=0, tiled=True)]
    reduce_max x16 -> x0, other arithmetic: 74.4 us -> none  [merge_block(): return (jnp.maximum(picks, jnp.max(hits, axis=1)), None)]
    psum x3 -> x1, blocking collectives: 101 us -> 39.2 us  [on_device(): sums = lax.psum(jnp.stack([squares, share * loss_sum, counted]), AXES)]
    all_gather x2 -> x1, blocking collectives: 65.3 us -> 16.3 us  [gather_rows(): near = lax.all_gather(block, 'dh', axis=0, tiled=True)]
    ppermute x0 -> x58, starting transfers between devices: none -> 28.9 us  [swap(): return lax.ppermute(values, axis, SWAP)]
  transfers between devices with their start and end apart: 13 -> 71, of which waited for: 11 -> 36; matrix products, arithmetic and copies ran while one was open for 15% -> 29% of each run, Pallas kernels for 0% -> 0%
where the time goes in v1:
time: 944 us; the launch traced here: 933 us
  waiting for transfers between devices  452 us (48%)
  matrix products  187 us (20%)
  other arithmetic  98.1 us (10%)
  local copies, waits for them, and re-layouts  80.7 us (9%)
  blocking collectives  55.5 us (6%)
  starting transfers between devices  30.4 us (3%)
  between operations  29.8 us (3%)
    ppermute x58, waiting for transfers between devices, swap(): return lax.ppermute(values, axis, SWAP)  438 us
    dot_general x64, matrix products, dot(): lax.dot_general(a, b, (((ca,), (cb,)), ((), ())), precision=HIGH, preferr...  129 us
    dot_general x24, matrix products, heads_dot(): lax.dot_general(a, b, (((ca,), (cb,)), ((0,), (0,))), precision=HIGH, pre...  58 us
    unnamed x648, local copies, waits for them, and re-layouts  45.1 us
    psum x1, blocking collectives, on_device(): sums = lax.psum(jnp.stack([squares, share * loss_sum, counted]), AXES)  39.2 us
    ppermute x58, starting transfers between devices, swap(): return lax.ppermute(values, axis, SWAP)  28.9 us
  transfers between devices with their start and end apart: 71, of which 36 were waited for; matrix products, arithmetic and copies ran while one was open for 29% of the time, Pallas kernels for 0%

profile of v1, /device:TPU:0, one launch (start us, length us, event | category | flops | bytes accessed | tf_op | source)
XLA Modules:
  0.0 932.9 jit_solution(16776174376988095147)
XLA Ops:
  12.6 16.3 %all-gather.4 = f32[4,96,135]{1,2,0:T(8,128)S(1)} all-gather(f32[1,96,135]{1,2,0:T(8,128)S(1)} %maximum_bitcast_fusion), channel_id=1, replica_groups=mesh['dh'=4,'dl'=2,'hh'=2,'hl'=2] {'dh'}, dimensions={0}, use_global_device_ids=true | all-gather | bytes 259200 | tf_op jit(solution)/shard_map/all_gather | solution.py:37
  58.8 19.7 %collective-permute-done.1 = f32[384,768]{1,0:T(8,128)S(1)} collective-permute-done((f32[384,768]{1,0:T(8,128)}, f32[384,768]{1,0:T(8,128)S(1)}, u32[]{:S(2)}, u32[]{:S(2)}) %collective-permute-start.1) | collective-permute-done | bytes 1179680 | tf_op jit(solution)/shard_map/ppermute | solution.py:26
  111.6 22.0 %collective-permute-done.29 = f32[384,768]{0,1:T(8,128)} collective-permute-done((f32[384,768]{0,1:T(8,128)S(1)}, f32[384,768]{0,1:T(8,128)}, u32[]{:S(2)}, u32[]{:S(2)}) %collective-permute-start.29) | collective-permute-done | bytes 1179680 | tf_op jit(solution)/shard_map/ppermute | solution.py:26
  140.3 17.8 %collective-permute-done.3 = f32[384,768]{0,1:T(8,128)} collective-permute-done((f32[384,768]{0,1:T(8,128)}, f32[384,768]{0,1:T(8,128)}, u32[]{:S(2)}, u32[]{:S(2)}) %collective-permute-start.3) | collective-permute-done | bytes 1179680 | tf_op jit(solution)/shard_map/ppermute | solution.py:26
  168.8 21.2 %collective-permute-done.6 = f32[384,768]{1,0:T(8,128)S(1)} collective-permute-done((f32[384,768]{1,0:T(8,128)}, f32[384,768]{1,0:T(8,128)S(1)}, u32[]{:S(2)}, u32[]{:S(2)}) %collective-permute-start.6) | collective-permute-done | bytes 1179680 | tf_op jit(solution)/shard_map/ppermute | solution.py:26
  210.0 24.0 %collective-permute-done.32 = f32[384,768]{0,1:T(8,128)} collective-permute-done((f32[384,768]{0,1:T(8,128)}, f32[384,768]{0,1:T(8,128)}, u32[]{:S(2)}, u32[]{:S(2)}) %collective-permute-start.32) | collective-permute-done | bytes 1179680 | tf_op jit(solution)/shard_map/ppermute | solution.py:26
  242.1 16.3 %collective-permute-done.8 = f32[384,768]{0,1:T(8,128)} collective-permute-done((f32[384,768]{0,1:T(8,128)S(1)}, f32[384,768]{0,1:T(8,128)}, u32[]{:S(2)}, u32[]{:S(2)}) %collective-permute-start.8) | collective-permute-done | bytes 1179680 | tf_op jit(solution)/shard_map/ppermute | solution.py:26
  288.9 7.0 collective-permute-done.12
  304.1 10.0 %collective-permute-done.14 = f32[384,768]{1,0:T(8,128)S(1)} collective-permute-done((f32[384,768]{1,0:T(8,128)}, f32[384,768]{1,0:T(8,128)S(1)}, u32[]{:S(2)}, u32[]{:S(2)}) %collective-permute-start.14) | collective-permute-done | bytes 1179680 | tf_op jit(solution)/shard_map/ppermute | solution.py:26
  315.6 22.9 %collective-permute-done.15 = f32[384,768]{1,0:T(8,128)S(1)} collective-permute-done((f32[384,768]{1,0:T(8,128)}, f32[384,768]{1,0:T(8,128)S(1)}, u32[]{:S(2)}, u32[]{:S(2)}) %collective-permute-start.15) | collective-permute-done | bytes 1179680 | tf_op jit(solution)/shard_map/ppermute | solution.py:26
  346.5 9.7 %collective-permute-done.17 = f32[128,768]{0,1:T(8,128)S(1)} collective-permute-done((f32[128,768]{0,1:T(8,128)S(1)}, f32[128,768]{0,1:T(8,128)S(1)}, u32[]{:S(2)}, u32[]{:S(2)}) %collective-permute-start.17) | collective-permute-done | bytes 393248 | tf_op jit(solution)/shard_map/ppermute | solution.py:26
  357.1 7.1 collective-permute-done.38
  378.9 9.8 %collective-permute-done.41 = f32[128,768]{0,1:T(8,128)S(1)} collective-permute-done((f32[128,768]{0,1:T(8,128)S(1)}, f32[128,768]{0,1:T(8,128)S(1)}, u32[]{:S(2)}, u32[]{:S(2)}) %collective-permute-start.41) | collective-permute-done | bytes 393248 | tf_op jit(solution)/shard_map/ppermute | solution.py:26
  388.8 7.5 collective-permute-done.20
  431.3 25.9 %collective-permute-done.23 = f32[384,768]{0,1:T(8,128)S(1)} collective-permute-done((f32[384,768]{0,1:T(8,128)S(1)}, f32[384,768]{0,1:T(8,128)S(1)}, u32[]{:S(2)}, u32[]{:S(2)}) %collective-permute-start.23) | collective-permute-done | bytes 1179680 | tf_op jit(solution)/shard_map/ppermute | solution.py:26
  457.4 24.3 %collective-permute-done.44 = f32[384,768]{0,1:T(8,128)S(1)} collective-permute-done((f32[384,768]{0,1:T(8,128)S(1)}, f32[384,768]{0,1:T(8,128)S(1)}, u32[]{:S(2)}, u32[]{:S(2)}) %collective-permute-start.44) | collective-permute-done | bytes 1179680 | tf_op jit(solution)/shard_map/ppermute | solution.py:26
  512.4 21.9 %collective-permute-done.26 = f32[384,768]{0,1:T(8,128)S(1)} collective-permute-done((f32[384,768]{0,1:T(8,128)S(1)}, f32[384,768]{0,1:T(8,128)S(1)}, u32[]{:S(2)}, u32[]{:S(2)}) %collective-permute-start.26) | collective-permute-done | bytes 1179680 | tf_op jit(solution)/shard_map/ppermute | solution.py:26
  538.4 20.7 %collective-permute-done.47 = f32[384,768]{0,1:T(8,128)S(1)} collective-permute-done((f32[384,768]{0,1:T(8,128)S(1)}, f32[384,768]{0,1:T(8,128)S(1)}, u32[]{:S(2)}, u32[]{:S(2)}) %collective-permute-start.47) | collective-permute-done | bytes 1179680 | tf_op jit(solution)/shard_map/ppermute | solution.py:26
  572.7 6.5 fusion.277
  579.3 5.9 multiply_multiply_fusion
  595.5 5.9 fusion.281
  601.5 6.0 multiply_multiply_fusion.1
  633.4 7.0 collective-permute-done.49
  655.1 27.0 %collective-permute-done.57 = f32[384,768]{1,0:T(8,128)S(1)} collective-permute-done((f32[384,768]{1,0:T(8,128)S(1)}, f32[384,768]{1,0:T(8,128)S(1)}, u32[]{:S(2)}, u32[]{:S(2)}) %collective-permute-start.57) | collective-permute-done | bytes 1179680 | tf_op jit(solution)/shard_map/ppermute | solution.py:26
  683.3 5.8 fusion.80
  693.2 26.3 %collective-permute-done.56 = f32[384,768]{1,0:T(8,128)S(1)} collective-permute-done((f32[384,768]{1,0:T(8,128)S(1)}, f32[384,768]{1,0:T(8,128)S(1)}, u32[]{:S(2)}, u32[]{:S(2)}) %collective-permute-start.56) | collective-permute-done | bytes 1179680 | tf_op jit(solution)/shard_map/ppermute | solution.py:26
  726.4 25.5 %collective-permute-done.55 = f32[384,768]{1,0:T(8,128)S(1)} collective-permute-done((f32[384,768]{1,0:T(8,128)S(1)}, f32[384,768]{1,0:T(8,128)S(1)}, u32[]{:S(2)}, u32[]{:S(2)}) %collective-permute-start.55) | collective-permute-done | bytes 1179680 | tf_op jit(solution)/shard_map/ppermute | solution.py:26
  753.1 5.8 fusion.26
  762.9 24.7 %collective-permute-done.54 = f32[384,768]{1,0:T(8,128)S(1)} collective-permute-done((f32[384,768]{1,0:T(8,128)S(1)}, f32[384,768]{1,0:T(8,128)S(1)}, u32[]{:S(2)}, u32[]{:S(2)}) %collective-permute-start.54) | collective-permute-done | bytes 1179680 | tf_op jit(solution)/shard_map/ppermute | solution.py:26
  801.8 24.0 %collective-permute-done.52 = f32[384,768]{0,1:T(8,128)S(1)} collective-permute-done((f32[384,768]{0,1:T(8,128)S(1)}, f32[384,768]{0,1:T(8,128)S(1)}, u32[]{:S(2)}, u32[]{:S(2)}) %collective-permute-start.52) | collective-permute-done | bytes 1179680 | tf_op jit(solution)/shard_map/ppermute | solution.py:26
  842.6 13.9 %reduce-scatter.24.cloned.1.call-done = f32[96,768]{1,0:T(8,128)} async-done(((f32[384,768]{1,0:T(8,128)}), f32[96,768]{1,0:T(8,128)}) %reduce-scatter.24.cloned.1.call-update) | async-done | bytes 294928
  864.1 39.2 %psum.7 = f32[3]{0:T(128)S(1)} all-reduce(f32[3]{0:T(128)S(1)} %pad_maximum_fusion.84), channel_id=1, replica_groups=mesh['dh'=4,'dl'=2,'hh'=2,'hl'=2] {'dh','dl','hh','hl'}, use_global_device_ids=true, to_apply=%region_85.86 | all-reduce | flops 3 | bytes 24 | tf_op jit(solution)/shard_map/psum | solution.py:322
  (1112 shorter events, 375.5 us)
Async XLA Ops:
  7.2 46.2 %all-gather.12.cloned.1.call-start = ((), (), s32[]{:S(2)}) async-start(), calls=%async_computation.7 | async-start | bytes 1474560 | tf_op jit(solution)/shard_map/all_gather | solution.py:37
  11.6 124.5 %all-gather.16.cloned.1.call-start = ((), (), s32[]{:S(2)}) async-start(), calls=%async_computation.13 | async-start | bytes 1474560 | tf_op jit(solution)/shard_map/all_gather | solution.py:37
  31.6 107.0 %all-gather.18.cloned.1.call-start = ((), (), s32[]{:S(2)}) async-start(), calls=%async_computation.14 | async-start | bytes 1474560 | tf_op jit(solution)/shard_map/all_gather | solution.py:37
  104.7 29.0 %collective-permute-start.29 = (f32[384,768]{0,1:T(8,128)S(1)}, f32[384,768]{0,1:T(8,128)}, u32[]{:S(2)}, u32[]{:S(2)}) collective-permute-start(f32[384,768]{0,1:T(8,128)S(1)} %slice_add_fusion.6), channel_id=1, source_target_pairs={{0,2},{2,0},{1,3},{3,1},{4,6},{6,4},{5,7},{7,5},{8,10},{10,8},{9,1... | collective-permute-start | bytes 3538952 | tf_op jit(solution)/shard_map/ppermute | solution.py:26
  107.1 102.4 %all-gather.14.cloned.1.call-start = ((), (), s32[]{:S(2)}) async-start(), calls=%async_computation.8 | async-start | bytes 1474560 | tf_op jit(solution)/shard_map/all_gather | solution.py:37
  110.1 47.9 %collective-permute-start.3 = (f32[384,768]{0,1:T(8,128)}, f32[384,768]{0,1:T(8,128)}, u32[]{:S(2)}, u32[]{:S(2)}) collective-permute-start(f32[384,768]{0,1:T(8,128)} %slice_add_fusion.9), channel_id=1, source_target_pairs={{0,2},{2,0},{1,3},{3,1},{4,6},{6,4},{5,7},{7,5},{8,10},{10,8},{9,1... | collective-permute-start | bytes 3538952 | tf_op jit(solution)/shard_map/ppermute | solution.py:26
  136.1 29.0 %collective-permute-start.5 = (f32[384,768]{1,0:T(8,128)}, f32[384,768]{1,0:T(8,128)S(1)}, u32[]{:S(2)}, u32[]{:S(2)}) collective-permute-start(f32[384,768]{1,0:T(8,128)} %bitcast.295), channel_id=1, source_target_pairs={{0,4},{4,0},{1,5},{5,1},{2,6},{6,2},{3,7},{7,3},{8,12},{12,8},{9,1... | collective-permute-start | bytes 3538952 | tf_op jit(solution)/shard_map/ppermute | solution.py:26
  138.4 146.7 %all-gather.20.cloned.1.call-start = ((), (), s32[]{:S(2)}) async-start(), calls=%async_computation.15 | async-start | bytes 1474560 | tf_op jit(solution)/shard_map/all_gather | solution.py:37
  138.7 51.3 %collective-permute-start.6 = (f32[384,768]{1,0:T(8,128)}, f32[384,768]{1,0:T(8,128)S(1)}, u32[]{:S(2)}, u32[]{:S(2)}) collective-permute-start(f32[384,768]{1,0:T(8,128)} %bitcast.401), channel_id=1, source_target_pairs={{0,4},{4,0},{1,5},{5,1},{2,6},{6,2},{3,7},{7,3},{8,12},{12,8},{9,1... | collective-permute-start | bytes 3538952 | tf_op jit(solution)/shard_map/ppermute | solution.py:26
  159.8 33.7 %collective-permute-start.4 = (f32[384,768]{0,1:T(8,128)S(1)}, f32[384,768]{0,1:T(8,128)S(1)}, u32[]{:S(2)}, u32[]{:S(2)}) collective-permute-start(f32[384,768]{0,1:T(8,128)S(1)} %add.548), channel_id=1, source_target_pairs={{0,1},{1,0},{2,3},{3,2},{4,5},{5,4},{6,7},{7,6},{8,9},{9,8},{10,11... | collective-permute-start | bytes 3538952 | tf_op jit(solution)/shard_map/ppermute | solution.py:26
  204.8 29.1 %collective-permute-start.32 = (f32[384,768]{0,1:T(8,128)}, f32[384,768]{0,1:T(8,128)}, u32[]{:S(2)}, u32[]{:S(2)}) collective-permute-start(f32[384,768]{0,1:T(8,128)} %slice_add_fusion.5), channel_id=1, source_target_pairs={{0,2},{2,0},{1,3},{3,1},{4,6},{6,4},{5,7},{7,5},{8,10},{10,8},{9,1... | collective-permute-start | bytes 3538952 | tf_op jit(solution)/shard_map/ppermute | solution.py:26
  206.4 79.3 %all-gather.22.cloned.1.call-start = ((), (), s32[]{:S(2)}) async-start(), calls=%async_computation.16 | async-start | bytes 1474560 | tf_op jit(solution)/shard_map/all_gather | solution.py:37
  208.2 50.2 %collective-permute-start.8 = (f32[384,768]{0,1:T(8,128)S(1)}, f32[384,768]{0,1:T(8,128)}, u32[]{:S(2)}, u32[]{:S(2)}) collective-permute-start(f32[384,768]{0,1:T(8,128)S(1)} %slice_add_fusion.8), channel_id=1, source_target_pairs={{0,2},{2,0},{1,3},{3,1},{4,6},{6,4},{5,7},{7,5},{8,10},{10,8},{9,1... | collective-permute-start | bytes 3538952 | tf_op jit(solution)/shard_map/ppermute | solution.py:26
  209.5 50.4 %collective-permute-start.10 = (f32[384,768]{1,0:T(8,128)}, f32[384,768]{1,0:T(8,128)}, u32[]{:S(2)}, u32[]{:S(2)}) collective-permute-start(f32[384,768]{1,0:T(8,128)} %all-gather.14.cloned.1.call-done), channel_id=1, source_target_pairs={{0,4},{4,0},{1,5},{5,1},{2,6},{6,2},{3,7},{7,3},{8,12},{12,8},{9,1... | collective-permute-start | bytes 3538952 | tf_op jit(solution)/shard_map/ppermute | solution.py:26
  236.8 594.1 %reduce-scatter.22.cloned.1.call-start = ((), (), s32[]{:S(2)}) async-start(), calls=%async_computation.17 | async-start | bytes 491520 | tf_op jit(solution)/shard_map/reduce_scatter | solution.py:44
  285.1 29.0 %collective-permute-start.14 = (f32[384,768]{1,0:T(8,128)}, f32[384,768]{1,0:T(8,128)S(1)}, u32[]{:S(2)}, u32[]{:S(2)}) collective-permute-start(f32[384,768]{1,0:T(8,128)} %bitcast.300), channel_id=1, source_target_pairs={{0,4},{4,0},{1,5},{5,1},{2,6},{6,2},{3,7},{7,3},{8,12},{12,8},{9,1... | collective-permute-start | bytes 3538952 | tf_op jit(solution)/shard_map/ppermute | solution.py:26
  285.6 52.9 %collective-permute-start.15 = (f32[384,768]{1,0:T(8,128)}, f32[384,768]{1,0:T(8,128)S(1)}, u32[]{:S(2)}, u32[]{:S(2)}) collective-permute-start(f32[384,768]{1,0:T(8,128)} %bitcast.406), channel_id=1, source_target_pairs={{0,4},{4,0},{1,5},{5,1},{2,6},{6,2},{3,7},{7,3},{8,12},{12,8},{9,1... | collective-permute-start | bytes 3538952 | tf_op jit(solution)/shard_map/ppermute | solution.py:26
  303.7 36.3 %collective-permute-start.36 = (f32[128,768]{0,1:T(8,128)S(1)}, f32[128,768]{0,1:T(8,128)S(1)}, u32[]{:S(2)}, u32[]{:S(2)}) collective-permute-start(f32[128,768]{0,1:T(8,128)S(1)} %add.595), channel_id=1, source_target_pairs={{0,1},{1,0},{2,3},{3,2},{4,5},{5,4},{6,7},{7,6},{8,9},{9,8},{10,11... | collective-permute-start | bytes 1179656 | tf_op jit(solution)/shard_map/ppermute | solution.py:26
  428.3 28.9 %collective-permute-start.23 = (f32[384,768]{0,1:T(8,128)S(1)}, f32[384,768]{0,1:T(8,128)S(1)}, u32[]{:S(2)}, u32[]{:S(2)}) collective-permute-start(f32[384,768]{0,1:T(8,128)S(1)} %maximum_add_fusion.6), channel_id=1, source_target_pairs={{0,2},{2,0},{1,3},{3,1},{4,6},{6,4},{5,7},{7,5},{8,10},{10,8},{9,1... | collective-permute-start | bytes 3538952 | tf_op jit(solution)/shard_map/ppermute | solution.py:26
  430.7 51.0 %collective-permute-start.44 = (f32[384,768]{0,1:T(8,128)S(1)}, f32[384,768]{0,1:T(8,128)S(1)}, u32[]{:S(2)}, u32[]{:S(2)}) collective-permute-start(f32[384,768]{0,1:T(8,128)S(1)} %maximum_add_fusion.7), channel_id=1, source_target_pairs={{0,2},{2,0},{1,3},{3,1},{4,6},{6,4},{5,7},{7,5},{8,10},{10,8},{9,1... | collective-permute-start | bytes 3538952 | tf_op jit(solution)/shard_map/ppermute | solution.py:26
  505.5 28.9 %collective-permute-start.26 = (f32[384,768]{0,1:T(8,128)S(1)}, f32[384,768]{0,1:T(8,128)S(1)}, u32[]{:S(2)}, u32[]{:S(2)}) collective-permute-start(f32[384,768]{0,1:T(8,128)S(1)} %slice_add_fusion.7), channel_id=1, source_target_pairs={{0,2},{2,0},{1,3},{3,1},{4,6},{6,4},{5,7},{7,5},{8,10},{10,8},{9,1... | collective-permute-start | bytes 3538952 | tf_op jit(solution)/shard_map/ppermute | solution.py:26
  509.1 49.9 %collective-permute-start.47 = (f32[384,768]{0,1:T(8,128)S(1)}, f32[384,768]{0,1:T(8,128)S(1)}, u32[]{:S(2)}, u32[]{:S(2)}) collective-permute-start(f32[384,768]{0,1:T(8,128)S(1)} %slice_add_fusion.4), channel_id=1, source_target_pairs={{0,2},{2,0},{1,3},{3,1},{4,6},{6,4},{5,7},{7,5},{8,10},{10,8},{9,1... | collective-permute-start | bytes 3538952 | tf_op jit(solution)/shard_map/ppermute | solution.py:26
  537.8 106.2 %collective-permute-start.53 = (f32[384,768]{0,1:T(8,128)}, f32[384,768]{0,1:T(8,128)}, u32[]{:S(2)}, u32[]{:S(2)}) collective-permute-start(f32[384,768]{0,1:T(8,128)} %pad_maximum_fusion.28), channel_id=1, source_target_pairs={{0,4},{4,0},{1,5},{5,1},{2,6},{6,2},{3,7},{7,3},{8,12},{12,8},{9,1... | collective-permute-start | bytes 3538952 | tf_op jit(solution)/shard_map/ppermute | solution.py:26
  643.9 191.5 %reduce-scatter.26.cloned.1.call-start = ((), (), s32[]{:S(2)}) async-start(), calls=%async_computation.19 | async-start | bytes 1474560
  649.4 188.3 %reduce-scatter.20.cloned.1.call-start = ((), (), s32[]{:S(2)}) async-start(), calls=%async_computation.12 | async-start | bytes 1474560 | tf_op jit(solution)/shard_map/reduce_scatter | solution.py:44
  654.5 27.6 %collective-permute-start.57 = (f32[384,768]{1,0:T(8,128)S(1)}, f32[384,768]{1,0:T(8,128)S(1)}, u32[]{:S(2)}, u32[]{:S(2)}) collective-permute-start(f32[384,768]{1,0:T(8,128)S(1)} %slice.911), channel_id=1, source_target_pairs={{0,4},{4,0},{1,5},{5,1},{2,6},{6,2},{3,7},{7,3},{8,12},{12,8},{9,1... | collective-permute-start | bytes 3538952 | tf_op jit(solution)/shard_map/ppermute | solution.py:26
  683.3 154.4 %reduce-scatter.18.cloned.1.call-start = ((), (), s32[]{:S(2)}) async-start(), calls=%async_computation.11 | async-start | bytes 1474560 | tf_op jit(solution)/shard_map/reduce_scatter | solution.py:44
  692.6 26.9 %collective-permute-start.56 = (f32[384,768]{1,0:T(8,128)S(1)}, f32[384,768]{1,0:T(8,128)S(1)}, u32[]{:S(2)}, u32[]{:S(2)}) collective-permute-start(f32[384,768]{1,0:T(8,128)S(1)} %slice.909), channel_id=1, source_target_pairs={{0,4},{4,0},{1,5},{5,1},{2,6},{6,2},{3,7},{7,3},{8,12},{12,8},{9,1... | collective-permute-start | bytes 3538952 | tf_op jit(solution)/shard_map/ppermute | solution.py:26
  720.8 118.8 %reduce-scatter.16.cloned.1.call-start = ((), (), s32[]{:S(2)}) async-start(), calls=%async_computation.10 | async-start | bytes 1474560 | tf_op jit(solution)/shard_map/reduce_scatter | solution.py:44
  725.9 26.0 %collective-permute-start.55 = (f32[384,768]{1,0:T(8,128)S(1)}, f32[384,768]{1,0:T(8,128)S(1)}, u32[]{:S(2)}, u32[]{:S(2)}) collective-permute-start(f32[384,768]{1,0:T(8,128)S(1)} %slice.907), channel_id=1, source_target_pairs={{0,4},{4,0},{1,5},{5,1},{2,6},{6,2},{3,7},{7,3},{8,12},{12,8},{9,1... | collective-permute-start | bytes 3538952 | tf_op jit(solution)/shard_map/ppermute | solution.py:26
  753.1 86.5 %reduce-scatter.14.cloned.1.call-start = ((), (), s32[]{:S(2)}) async-start(), calls=%async_computation.9 | async-start | bytes 1474560 | tf_op jit(solution)/shard_map/reduce_scatter | solution.py:44
  788.9 67.6 %reduce-scatter.24.cloned.1.call-start = ((), (), s32[]{:S(2)}) async-start(), calls=%async_computation.18 | async-start | bytes 1474560
  (349 other events, 3083.8 us)
Sparse Core Ops, SparseCore 0:
  11.7 34.4 all-gather.11
  48.4 29.3 all-gather.15
  107.2 29.8 all-gather.17
  139.2 31.1 all-gather.13
  206.5 29.8 all-gather.19
  237.8 30.0 all-gather.21
  644.0 20.0 reduce-scatter.21
  666.6 27.4 reduce-scatter.25
  696.5 27.8 reduce-scatter.19
  726.7 27.8 reduce-scatter.17
  757.0 27.8 reduce-scatter.15
  789.0 28.7 reduce-scatter.13
  827.7 28.8 reduce-scatter.23

commit v2 on v1

v2 whole, which is shorter than its diff:
```python
import functools

import jax
import jax.numpy as jnp
from jax import lax
from jax.experimental import pallas as pl
from jax.experimental.pallas import tpu as pltpu
from jax.sharding import Mesh, PartitionSpec as P

HD = 64
LR_MATRIX = 0.03
LR_VECTOR = 0.2
DECAY = 0.1
CLIP_AT = 0.02
EPS = 1e-05
SWAP = ((0, 1), (1, 0))
AXES = ("dh", "dl", "hh", "hl")
F32, BF16 = jnp.float32, jnp.bfloat16
ANY = pl.BlockSpec(memory_space=pl.ANY)
SMEM = pl.BlockSpec(memory_space=pltpu.SMEM)
VMEM = pl.BlockSpec(memory_space=pltpu.VMEM)
QSCALE = HD ** (-0.5)
COST = 20


def swap(values, axis):
    return lax.ppermute(values, axis, SWAP)


def head_sum(mine, theirs, before=None):
    first, second = (swap(t, "hl") for t in theirs)
    a = mine + jnp.concatenate([after(first, before), second], axis=0)
    c = swap(a, "hl")
    b = swap(a, "hh")
    return a, b, c, swap(b, "hl")


def gather_rows(block):
    near = lax.all_gather(block, "dh", axis=0, tiled=True)
    return near, swap(near, "dl")


def everyone_sum(values):
    values = jnp.broadcast_to(jnp.pad(values, (0, 128 - values.shape[0]))[None], (8, 128))
    for axis in ("hl", "hh", "dl"):
        values = values + swap(values, axis)
    size = lax.axis_size("dh")
    if size & (size - 1):
        return lax.psum(values, "dh")[0]
    step = 1
    while step < size:
        values = values + lax.ppermute(values, "dh", [(i, i ^ step) for i in range(size)])
        step *= 2
    return values[0]


def near_rows(near, far):
    return near + swap(far, "dl")


def scatter_near(near):
    return lax.psum_scatter(near, "dh", scatter_dimension=0, tiled=True)


def after(value, *others):
    others = [o for o in others if o is not None]
    return lax.optimization_barrier((value, *others))[0] if others else value


def split(a):
    hi = a.astype(BF16)
    return hi, (a - hi.astype(F32)).astype(BF16)


def dg(a, b, ca, cb):
    return lax.dot_general(a, b, (((ca,), (cb,)), ((), ())), preferred_element_type=F32)


def mm(a, b, ca, cb):
    return (dg(a[1], b[0], ca, cb) + dg(a[0], b[1], ca, cb)) + dg(a[0], b[0], ca, cb)


def norm_stats(x):
    centre = x - jnp.mean(x, axis=-1, keepdims=True)
    rstd = lax.rsqrt(jnp.mean(centre * centre, axis=-1, keepdims=True) + EPS)
    return centre * rstd, rstd


def norm_back(dn, nh, rstd):
    return rstd * (
        dn - jnp.mean(dn, axis=-1, keepdims=True) - nh * jnp.mean(dn * nh, axis=-1, keepdims=True)
    )


def gelu_parts(u):
    t = jnp.tanh(0.7978845608 * (u + 0.044715 * u * u * u))
    value = 0.5 * u * (1.0 + t)
    slope = 0.5 * (1.0 + t) + 0.5 * u * (1.0 - t * t) * 0.7978845608 * (1.0 + 3.0 * 0.044715 * u * u)
    return value, slope


def lanes(shape, low):
    at = lax.broadcasted_iota(jnp.int32, shape, 1)
    return (at >= low) & (at < low + HD)


def keep(pair, low):
    held = lanes(pair[0].shape, low)
    zero = jnp.zeros(pair[0].shape, BF16)
    return jnp.where(held, pair[0], zero), jnp.where(held, pair[1], zero)


class Copies:
    def __init__(self, sems):
        self.sems, self.count, self.open = sems, 0, []

    def start(self, src, dst):
        copy = pltpu.make_async_copy(src, dst, self.sems.at[self.count])
        self.count += 1
        copy.start()
        self.open.append(copy)
        return copy

    def wait(self, *copies):
        for copy in copies:
            copy.wait()
            self.open = [other for other in self.open if other is not copy]

    def wait_all(self):
        self.wait(*list(self.open))


def load_pair(copies, near, far, dst):
    half = near.shape[0]
    return (
        copies.start(near, dst.at[pl.ds(0, half)]),
        copies.start(far, dst.at[pl.ds(half, half)]),
    )


def send_parts(copies, part, half, mine, theirs):
    quarter = half // 2
    for i, piece in enumerate(theirs):
        copies.start(part.at[pl.ds(half + i * quarter, quarter)], piece)
    if mine is not None:
        copies.start(part.at[pl.ds(0, half)], mine)


def row(vec_ref, index):
    return vec_ref[pl.ds(index, 1), :]


def run(kernel, name, inputs, specs, outs, scratch, sems, flops, moved, aliases=None):
    return pl.pallas_call(
        kernel,
        name=name,
        out_shape=[jax.ShapeDtypeStruct(s, F32) for s in outs],
        in_specs=specs,
        out_specs=[ANY] * len(outs),
        scratch_shapes=list(scratch) + [pltpu.SemaphoreType.DMA((sems,))],
        input_output_aliases=aliases or {},
        compiler_params=pltpu.CompilerParams(vmem_limit_bytes=56 << 20),
        cost_estimate=pl.CostEstimate(flops=flops // COST, bytes_accessed=moved // COST, transcendentals=0),
    )(*inputs)


class Sizes:
    def __init__(self, d, context, queries, depth, width, feats, share):
        self.d, self.context, self.queries = d, context, queries
        self.depth, self.width, self.feats, self.share = depth, width, feats, share
        self.hc, self.hq = context // 2, queries // 2
        self.half = self.hc + self.hq
        self.rows = context + queries
        self.heads = width // HD
        self.k = slice(0, 256)
        self.v = slice(128, 384)
        self.q = slice(384, 640)
        self.o = slice(512, 768)
        self.kv = slice(0, 384)


def load_feats(copies, z, c_ref, feat, dst):
    c = c_ref[0]
    made = []
    for i in range(2):
        side = c if i == 0 else 1 - c
        made.append(
            copies.start(
                feat.at[pl.ds(pl.multiple_of(side * z.hc, z.hc), z.hc)],
                dst.at[pl.ds(i * z.half, z.hc)],
            )
        )
        made.append(
            copies.start(
                feat.at[pl.ds(pl.multiple_of(z.context + side * z.hq, z.hq), z.hq)],
                dst.at[pl.ds(i * z.half + z.hc, z.hq)],
            )
        )
    return made


def split_into(hi, lo, value):
    a, b = split(value)
    hi[...] = a
    lo[...] = b


def scores(z, qh, kh, h, mask, masked_from):
    s = mm(keep(qh, h * HD), kh, 1, 1)
    if masked_from == 0:
        return jnp.where(mask > 0, s, -1e30)
    low = jnp.where(mask > 0, s[masked_from:], -1e30)
    return jnp.concatenate([s[:masked_from], low], axis=0)


def attn_fwd_kernel(z, l, first, last, *refs):
    if first:
        (c_ref, t_in, vec, feat, emb, wn, wf, mask) = refs[:8]
        refs = refs[8:]
    else:
        (vec, xp, pa, pb, pc, pd, wn, wf, mask) = refs[:9]
        refs = refs[9:]
    x_out, q_out, kv_out, o_out, lse_out, mine, *theirs = refs[:8]
    (xb, wb, wh, wl, qb, kvb, ob, lseb, part, maskb, *rest, sems) = refs[8:]
    copies = Copies(sems)
    if first:
        featb, embb = rest
        cf = load_feats(copies, z, c_ref, feat, featb)
        ce = copies.start(emb, embb)
    else:
        (add,) = rest
        cx = copies.start(xp, xb)
        ca = [
            copies.start(p, add.at[pl.ds(i * z.half, z.half)]) for i, p in enumerate((pa, pb, pc, pd))
        ]
    cw = load_pair(copies, wn, wf, wb)
    cm = copies.start(mask, maskb)
    if first:
        copies.wait(*cf, ce)
        embs = split(embb[...])
    else:
        copies.wait(cx, *ca)
    gain = row(vec, l)
    normed = []
    outs = []
    for i in range(2):
        here = pl.ds(i * z.half, z.half)
        if first:
            x = mm(split(featb[here, :]), embs, 1, 1) + t_in[here, :] * row(vec, 2 * z.depth + 1)
        else:
            x = xb[here, :] + (
                add[pl.ds(2 * i * z.half, z.half), :] + add[pl.ds((2 * i + 1) * z.half, z.half), :]
            )
        xb[here, :] = x
        outs.append(copies.start(xb.at[here], x_out.at[here]))
    copies.wait(*cw)
    split_into(wh, wl, wb[...])
    for i in range(2):
        here = pl.ds(i * z.half, z.half)
        nh, _ = norm_stats(xb[here, :])
        n = split(nh * gain)
        nc = (n[0][: z.hc], n[1][: z.hc])
        nq = (n[0][z.hc :], n[1][z.hc :]) if last else n
        qrows = pl.ds(i * z.hq, z.hq) if last else here
        qb[qrows, :] = mm(nq, (wh[:, z.q], wl[:, z.q]), 1, 0) * QSCALE
        kvb[pl.ds(i * z.hc, z.hc), :] = mm(nc, (wh[:, z.kv], wl[:, z.kv]), 1, 0)
    copies.start(qb, q_out)
    copies.start(kvb, kv_out)
    copies.wait(cm)
    kh = split(kvb[:, z.k])
    vh = split(kvb[:, z.v])
    vm = [keep(vh, HD + h * HD) for h in range(z.heads)]
    tiles = [(0, 2 * z.hq)] if last else [(z.half, z.half), (0, z.half)]
    for start, size in tiles:
        here = pl.ds(start, size)
        qh = split(qb[here, :])
        m_tile = maskb[...] if last else maskb[pl.ds((start // z.half) * z.hq, z.hq), :]
        o = jnp.zeros((size, 256), F32)
        lse = jnp.zeros((size, 128), F32)
        at = lax.broadcasted_iota(jnp.int32, (size, 128), 1)
        for h in range(z.heads):
            s = scores(z, qh, kh, h, m_tile, 0 if last else z.hc)
            top = jnp.max(s, axis=-1, keepdims=True)
            e = jnp.exp(s - top)
            total = jnp.sum(e, axis=-1, keepdims=True)
            o = o + mm(split(e), vm[h], 1, 0) * (1.0 / total)
            lse = jnp.where(at == h, top + jnp.log(total), lse)
        ob[here, :] = o
        lseb[here, :] = lse
        part[here, :] = mm(split(o), (wh[:, z.o], wl[:, z.o]), 1, 1)
        if start > 0:
            send_parts(copies, part, z.half, None, theirs)
    if last:
        send_parts(copies, part, z.hq, mine, theirs)
    else:
        copies.start(part.at[pl.ds(0, z.half)], mine)
    copies.start(ob, o_out)
    copies.start(lseb, lse_out)
    copies.wait_all()


def attn_fwd(z, l, last, inputs):
    first = l == 0
    rq = z.queries if last else z.rows
    scratch = [
        pltpu.VMEM((z.rows, z.d), F32),
        pltpu.VMEM((z.d, z.d), F32),
        pltpu.VMEM((z.d, z.d), BF16),
        pltpu.VMEM((z.d, z.d), BF16),
        pltpu.VMEM((rq, 256), F32),
        pltpu.VMEM((z.context, 384), F32),
        pltpu.VMEM((rq, 256), F32),
        pltpu.VMEM((rq, 128), F32),
        pltpu.VMEM((rq, z.d), F32),
        pltpu.VMEM((z.queries, z.context), F32),
    ]
    if first:
        scratch += [pltpu.VMEM((z.rows, z.feats), F32), pltpu.VMEM((z.d, z.feats), F32)]
        specs = [SMEM, VMEM, VMEM] + [ANY] * 5
    else:
        scratch += [pltpu.VMEM((4 * z.half, z.d), F32)]
        specs = [VMEM] + [ANY] * 8
    outs = [
        (z.rows, z.d),
        (rq, 256),
        (z.context, 384),
        (rq, 256),
        (rq, 128),
        (rq // 2, z.d),
        (rq // 4, z.d),
        (rq // 4, z.d),
    ]
    return run(
        functools.partial(attn_fwd_kernel, z, l, first, last),
        f"attn_fwd{l}",
        inputs,
        specs,
        outs,
        scratch,
        24,
        3 * 2 * (2 * rq * z.d * 256 + z.context * z.d * 384 + 6 * rq * z.context * 256),
        16 << 20,
    )


def ffn_fwd_kernel(z, l, last, *refs):
    (vec, xp, pa, pb, pc, pd, un, uf, dn, df) = refs[:10]
    x_out, u_out, mine, *theirs = refs[10:15]
    (xb, add, wb, wh, wl, vb, vh, vl, ub, part, sems) = refs[15:]
    copies = Copies(sems)
    half = z.hq if last else z.half
    if last:
        cx = [
            copies.start(xp.at[pl.ds(z.hc, z.hq)], xb.at[pl.ds(0, z.hq)]),
            copies.start(xp.at[pl.ds(z.half + z.hc, z.hq)], xb.at[pl.ds(z.hq, z.hq)]),
        ]
    else:
        cx = [copies.start(xp, xb)]
    ca = [copies.start(p, add.at[pl.ds(i * half, half)]) for i, p in enumerate((pa, pb, pc, pd))]
    cu = load_pair(copies, un, uf, wb)
    cd = load_pair(copies, dn, df, vb)
    copies.wait(*cx, *ca)
    gain = row(vec, z.depth + l)
    for i in range(2):
        here = pl.ds(i * half, half)
        xb[here, :] = xb[here, :] + (
            add[pl.ds(2 * i * half, half), :] + add[pl.ds((2 * i + 1) * half, half), :]
        )
    copies.start(xb, x_out)
    copies.wait(*cu)
    split_into(wh, wl, wb[...])
    copies.wait(*cd)
    split_into(vh, vl, vb[...])
    tiles = [(0, 2 * half)] if last else [(half, half), (0, half)]
    for start, size in tiles:
        here = pl.ds(start, size)
        nh, _ = norm_stats(xb[here, :])
        u = mm(split(nh * gain), (wh[...], wl[...]), 1, 0)
        ub[here, :] = u
        copies.start(ub.at[here], u_out.at[here])
        g, _ = gelu_parts(u)
        part[here, :] = mm(split(g), (vh[...], vl[...]), 1, 1)
        if start > 0:
            send_parts(copies, part, half, None, theirs)
    if last:
        send_parts(copies, part, half, mine, theirs)
    else:
        copies.start(part.at[pl.ds(0, half)], mine)
    copies.wait_all()


def ffn_fwd(z, l, last, inputs):
    r = z.queries if last else z.rows
    big = lambda t=F32: pltpu.VMEM((z.d, z.d), t)
    tall = lambda: pltpu.VMEM((r, z.d), F32)
    return run(
        functools.partial(ffn_fwd_kernel, z, l, last),
        f"ffn_fwd{l}",
        inputs,
        [VMEM] + [ANY] * 9,
        [(r, z.d), (r, z.d), (r // 2, z.d), (r // 4, z.d), (r // 4, z.d)],
        [tall(), pltpu.VMEM((2 * r, z.d), F32), big(), big(BF16), big(BF16), big(), big(BF16), big(BF16), tall(), tall()],
        20,
        3 * 4 * r * z.d * z.d,
        24 << 20,
    )


def ffn_bwd_kernel(z, l, last, accumulate, *refs):
    if last:
        (vec, side, xm, pa, pb, pc, pd, u_in, un, uf, dn, df) = refs[:12]
        refs = refs[12:]
    else:
        (vec, res, xn, xm, pa, pb, pc, pd, u_in, un, uf, dn, df) = refs[:13]
        refs = refs[13:]
    if accumulate:
        olds, refs = refs[:4], refs[4:]
    dy_out, mine, *theirs, gv, gun, guf, gdn, gdf = refs[:9]
    (xb, add, wb, wh, wl, vb, vh, vl, ub, dyb, dyh, dyl, gh, gl, part, gub, gdb, gvb, *rest, sems) = refs[9:]
    copies = Copies(sems)
    r = z.queries if last else z.rows
    half = r // 2
    ca = [copies.start(p, add.at[pl.ds(i * half, half)]) for i, p in enumerate((pa, pb, pc, pd))]
    cx = [copies.start(xm, xb)]
    if not last:
        (xnb,) = rest
        ca.append(copies.start(xn, xnb))
        for i in range(2):
            ca.append(copies.start(res.at[pl.ds(i * z.hq, z.hq)], dyb.at[pl.ds(i * z.half + z.hc, z.hq)]))
    cd = load_pair(copies, dn, df, vb)
    cu_in = copies.start(u_in, ub)
    cu = load_pair(copies, un, uf, wb)
    if accumulate:
        co = (*load_pair(copies, olds[0], olds[1], gub), *load_pair(copies, olds[2], olds[3], gdb))
    gvb[...] = jnp.zeros_like(gvb)
    copies.wait(*ca, *cx)
    for i in range(2):
        here = pl.ds(i * half, half)
        total = add[pl.ds(2 * i * half, half), :] + add[pl.ds((2 * i + 1) * half, half), :]
        if last:
            x4 = xb[here, :] + total
            nh, rstd = norm_stats(x4)
            r_head = row(vec, 2 * z.depth + 2)
            gain = row(vec, 2 * z.depth)
            nf = nh * gain
            flag = side[here, 0:1]
            err = jnp.sum(nf * r_head, axis=-1, keepdims=True) - side[here, 1:2]
            dpred = 2.0 * flag * err
            dnf = dpred * r_head
            dy = norm_back(dnf * gain, nh, rstd)
            gvb[pl.ds(2 * z.depth + 2, 1), :] += z.share * jnp.sum(nf * dpred, axis=0, keepdims=True)
            gvb[pl.ds(2 * z.depth, 1), :] += z.share * jnp.sum(dnf * nh, axis=0, keepdims=True)
            gvb[pl.ds(7, 1), :] += jnp.broadcast_to(
                jnp.sum(flag * err * err, axis=0, keepdims=True), (1, z.d)
            )
        else:
            gain = row(vec, l + 1)
            nh, rstd = norm_stats(xnb[here, :])
            dy = norm_back(total * gain, nh, rstd)
            dy = jnp.concatenate([dy[: z.hc], dy[z.hc :] + dyb[pl.ds(i * z.half + z.hc, z.hq), :]], axis=0)
            gvb[pl.ds(l + 1, 1), :] += z.share * jnp.sum(total * nh, axis=0, keepdims=True)
        dyb[here, :] = dy
        a, b = split(dy)
        dyh[here, :] = a
        dyl[here, :] = b
    copies.start(dyb, dy_out)
    copies.start(gvb, gv)
    copies.wait(*cd)
    split_into(vh, vl, vb[...])
    copies.wait(*cu)
    split_into(wh, wl, wb[...])
    copies.wait(cu_in)
    gain = row(vec, z.depth + l)
    tiles = [(0, r)] if last else [(half, half), (0, half)]
    for start, size in tiles:
        here = pl.ds(start, size)
        dh = mm((dyh[here, :], dyl[here, :]), (vh[...], vl[...]), 1, 0)
        g, slope = gelu_parts(ub[here, :])
        a, b = split(g)
        gh[here, :] = a
        gl[here, :] = b
        ub[here, :] = dh * slope
        part[here, :] = mm(split(ub[here, :]), (wh[...], wl[...]), 1, 1)
        if start > 0:
            send_parts(copies, part, half, None, theirs)
    if last:
        send_parts(copies, part, half, mine, theirs)
    else:
        copies.start(part.at[pl.ds(0, half)], mine)
    if accumulate:
        copies.wait(*co)
    new = mm((dyh[...], dyl[...]), (gh[...], gl[...]), 0, 0)
    gdb[...] = gdb[...] + new if accumulate else new
    d_half = z.d // 2
    copies.start(gdb.at[pl.ds(0, d_half)], gdn)
    copies.start(gdb.at[pl.ds(d_half, d_half)], gdf)
    nh, _ = norm_stats(xb[...])
    new = mm(split(nh * gain), split(ub[...]), 0, 0)
    gub[...] = gub[...] + new if accumulate else new
    copies.start(gub.at[pl.ds(0, d_half)], gun)
    copies.start(gub.at[pl.ds(d_half, d_half)], guf)
    copies.wait_all()


def ffn_bwd(z, l, last, inputs, olds):
    r = z.queries if last else z.rows
    big = lambda t=F32: pltpu.VMEM((z.d, z.d), t)
    tall = lambda t=F32: pltpu.VMEM((r, z.d), t)
    scratch = [tall(), pltpu.VMEM((2 * r, z.d), F32), big(), big(BF16), big(BF16), big(), big(BF16), big(BF16)]
    scratch += [tall(), tall(), tall(BF16), tall(BF16), tall(BF16), tall(BF16), tall(), big(), big()]
    scratch += [pltpu.VMEM((8, z.d), F32)]
    specs = [VMEM] + ([VMEM] if last else [ANY]) + [ANY] * (len(inputs) - 2)
    if not last:
        scratch += [tall()]
    h = z.d // 2
    outs = [(r, z.d), (r // 2, z.d), (r // 4, z.d), (r // 4, z.d), (8, z.d)] + [(h, z.d)] * 4
    aliases = None
    if olds is not None:
        aliases = {len(inputs) + i: 5 + i for i in range(4)}
        inputs = list(inputs) + list(olds)
        specs = specs + [ANY] * 4
    return run(
        functools.partial(ffn_bwd_kernel, z, l, last, olds is not None),
        f"ffn_bwd{l}",
        inputs,
        specs,
        outs,
        scratch,
        36,
        3 * 8 * r * z.d * z.d,
        32 << 20,
        aliases,
    )


def attn_bwd_kernel(z, l, first, last, accumulate, *refs):
    (vec, dyp, xm, pa, pb, pc, pd, wn, wf, x_in, q_in, kv_in, o_in, lse_in, mask) = refs[:15]
    refs = refs[15:]
    if first:
        (c_ref, t_in, feat) = refs[:3]
        refs = refs[3:]
    if accumulate:
        olds, refs = refs[: 3 if first else 2], refs[3 if first else 2 :]
    if first:
        gv, gn, gf, emb_out = refs[:4]
        refs = refs[4:]
    else:
        dy_out, mine, *theirs, gv, gn, gf = refs[:7]
        refs = refs[7:]
    (dyb, xmb, add, wb, wh, wl, xb, qb, kvb, ob, lseb, maskb, dyh, dyl, dqb, dkb, dvb, gb, gvb, *rest, sems) = refs
    copies = Copies(sems)
    rq = z.queries if last else z.rows
    half = rq // 2
    ca = [copies.start(p, add.at[pl.ds(i * half, half)]) for i, p in enumerate((pa, pb, pc, pd))]
    ca += [copies.start(dyp, dyb), copies.start(xm, xmb)]
    cw = load_pair(copies, wn, wf, wb)
    cq = [copies.start(q_in, qb), copies.start(kv_in, kvb), copies.start(o_in, ob)]
    cq += [copies.start(lse_in, lseb), copies.start(mask, maskb)]
    cx = [copies.start(x_in, xb)]
    if first:
        featb, geb = rest
        cx += load_feats(copies, z, c_ref, feat, featb)
    if accumulate:
        co = list(load_pair(copies, olds[0], olds[1], gb))
        if first:
            co.append(copies.start(olds[2], geb))
    gvb[...] = jnp.zeros_like(gvb)
    copies.wait(*ca)
    gain2 = row(vec, z.depth + l)
    for i in range(2):
        here = pl.ds(i * half, half)
        total = add[pl.ds(2 * i * half, half), :] + add[pl.ds((2 * i + 1) * half, half), :]
        nh, rstd = norm_stats(xmb[here, :])
        dy = dyb[here, :] + norm_back(total * gain2, nh, rstd)
        gvb[pl.ds(z.depth + l, 1), :] += z.share * jnp.sum(total * nh, axis=0, keepdims=True)
        dyb[here, :] = dy
        a, b = split(dy)
        dyh[here, :] = a
        dyl[here, :] = b
    if not first:
        copies.start(dyb, dy_out)
    copies.wait(*cw)
    split_into(wh, wl, wb[...])
    copies.wait(*cq)
    kh = split(kvb[:, z.k])
    vh = split(kvb[:, z.v])
    km = [keep(kh, h * HD) for h in range(z.heads)]
    dkb[...] = jnp.zeros_like(dkb)
    dvb[...] = jnp.zeros_like(dvb)
    tiles = [(0, rq)] if last else [(half, half), (0, half)]
    for start, size in tiles:
        here = pl.ds(start, size)
        do = mm((dyh[here, :], dyl[here, :]), (wh[:, z.o], wl[:, z.o]), 1, 0)
        doh = split(do)
        prod = do * ob[here, :]
        qh = split(qb[here, :])
        m_tile = maskb[...] if last else maskb[pl.ds((start // half) * z.hq, z.hq), :]
        dq = jnp.zeros((size, 256), F32)
        for h in range(z.heads):
            qm = keep(qh, h * HD)
            dm = keep(doh, HD + h * HD)
            s = scores(z, qh, kh, h, m_tile, 0 if last else z.hc)
            p = jnp.exp(s - lseb[here, h : h + 1])
            delta = jnp.sum(
                jnp.where(lanes(prod.shape, HD + h * HD), prod, 0.0), axis=-1, keepdims=True
            )
            dp = mm(dm, vh, 1, 1)
            ds = split(p * (dp - delta))
            dq = dq + mm(ds, km[h], 1, 0)
            dkb[...] += mm(ds, qm, 0, 0)
            dvb[...] += mm(split(p), dm, 0, 0)
        dqb[here, :] = dq * QSCALE
    kvb[:, 0:128] = dkb[:, 0:128]
    kvb[:, 128:256] = dkb[:, 128:256] + dvb[:, 0:128]
    kvb[:, 256:384] = dvb[:, 128:256]
    if accumulate:
        copies.wait(*co)
    g_out = mm((dyh[...], dyl[...]), split(ob[...]), 0, 0)
    copies.wait(*cx)
    gain = row(vec, l)
    dnb = add
    g_q = jnp.zeros((z.d, 256), F32)
    g_kv = jnp.zeros((z.d, 384), F32)
    ge = 0.0
    for i in (1, 0):
        here = pl.ds(i * z.half, z.half)
        nh, rstd = norm_stats(xb[here, :])
        n = split(nh * gain)
        nc = (n[0][: z.hc], n[1][: z.hc])
        nq = (n[0][z.hc :], n[1][z.hc :]) if last else n
        qrows = pl.ds(i * z.hq, z.hq) if last else here
        dq = split(dqb[qrows, :])
        dkv = split(kvb[pl.ds(i * z.hc, z.hc), :])
        g_q = g_q + mm(nq, dq, 0, 0)
        g_kv = g_kv + mm(nc, dkv, 0, 0)
        dn_q = mm(dq, (wh[:, z.q], wl[:, z.q]), 1, 1)
        dn_c = mm(dkv, (wh[:, z.kv], wl[:, z.kv]), 1, 1)
        if last:
            dn = jnp.concatenate([dn_c, dn_q], axis=0)
        else:
            dn = jnp.concatenate([dn_q[: z.hc] + dn_c, dn_q[z.hc :]], axis=0)
        if first:
            gvb[pl.ds(l, 1), :] += jnp.sum(dn * nh, axis=0, keepdims=True)
            dx = z.share * dyb[here, :] + norm_back(dn * gain, nh, rstd)
            gvb[pl.ds(2 * z.depth + 1, 1), :] += jnp.sum(dx * t_in[here, :], axis=0, keepdims=True)
            ge = ge + mm(split(dx), split(featb[here, :]), 0, 0)
        else:
            dnb[pl.ds(i * z.half, z.half), :] = dn
            if i > 0:
                send_parts(copies, dnb, z.half, None, theirs)
            else:
                copies.start(dnb.at[here], mine)
    copies.start(gvb, gv)
    new = [
        g_kv,
        g_q[:, 0:128],
        g_q[:, 128:256] + g_out[:, 0:128],
        g_out[:, 128:256],
    ]
    at = 0
    for piece in new:
        cols = slice(at, at + piece.shape[1])
        gb[:, cols] = gb[:, cols] + piece if accumulate else piece
        at += piece.shape[1]
    d_half = z.d // 2
    copies.start(gb.at[pl.ds(0, d_half)], gn)
    copies.start(gb.at[pl.ds(d_half, d_half)], gf)
    if first:
        geb[...] = geb[...] + ge if accumulate else ge
        copies.start(geb, emb_out)
    copies.wait_all()


def attn_bwd(z, l, last, inputs, firsts, olds):
    first = l == 0
    rq = z.queries if last else z.rows
    big = lambda t=F32: pltpu.VMEM((z.d, z.d), t)
    tall = lambda t=F32: pltpu.VMEM((rq, z.d), t)
    scratch = [tall(), tall(), pltpu.VMEM((2 * z.rows, z.d), F32), big(), big(BF16), big(BF16)]
    scratch += [pltpu.VMEM((z.rows, z.d), F32), pltpu.VMEM((rq, 256), F32), pltpu.VMEM((z.context, 384), F32)]
    scratch += [pltpu.VMEM((rq, 256), F32), pltpu.VMEM((rq, 128), F32), pltpu.VMEM((z.queries, z.context), F32)]
    scratch += [tall(BF16), tall(BF16), pltpu.VMEM((rq, 256), F32)]
    scratch += [pltpu.VMEM((z.context, 256), F32), pltpu.VMEM((z.context, 256), F32), big(), pltpu.VMEM((8, z.d), F32)]
    specs = [VMEM] + [ANY] * 14
    h = z.d // 2
    outs = [(8, z.d), (h, z.d), (h, z.d)]
    inputs = list(inputs)
    if first:
        inputs += list(firsts)
        specs += [SMEM, VMEM, ANY]
        scratch += [pltpu.VMEM((z.rows, z.feats), F32), pltpu.VMEM((z.d, z.feats), F32)]
        outs += [(z.d, z.feats)]
        grads = [1, 2, 3]
    else:
        outs = [(rq, z.d), (z.half, z.d), (z.half // 2, z.d), (z.half // 2, z.d)] + outs
        grads = [5, 6]
    aliases = None
    if olds is not None:
        aliases = {len(inputs) + i: g for i, g in enumerate(grads)}
        inputs += list(olds)
        specs += [ANY] * len(olds)
    return run(
        functools.partial(attn_bwd_kernel, z, l, first, last, olds is not None),
        f"attn_bwd{l}",
        inputs,
        specs,
        outs,
        scratch,
        32,
        3 * 2 * (4 * rq * z.d * 256 + 2 * z.context * z.d * 384 + 15 * rq * z.context * 256),
        24 << 20,
        aliases,
    )


def roll_half(x, c):
    half = x.shape[0] // 2
    return jnp.where(c == 0, x, jnp.concatenate([x[half:], x[:half]], axis=0))


def interleave(ctx, qry):
    hc, hq = ctx.shape[0] // 2, qry.shape[0] // 2
    return jnp.concatenate([ctx[:hc], qry[:hq], ctx[hc:], qry[hq:]], axis=0)


def neighbour_mask(neigh, live, context_rows, c):
    words = context_rows // 32
    col = jnp.bitwise_xor(neigh, c * (context_rows // 2))
    bit = jnp.left_shift(live, jnp.bitwise_and(col, 31))
    at = jnp.right_shift(col, 5)
    index = jnp.arange(words, dtype=jnp.int32)[None, :, None]
    word = jnp.sum(jnp.where(at[:, None, :] == index, bit[:, None, :], 0), axis=-1)
    spread = jnp.broadcast_to(word[:, :, None], word.shape + (32,)).reshape(word.shape[0], context_rows)
    shift = jnp.bitwise_and(jnp.arange(context_rows, dtype=jnp.int32), 31)
    return jnp.bitwise_and(jnp.right_shift(spread, shift[None, :]), 1).astype(F32)


def adamw(weight, grad, first, second, rate, decay, steps_taken):
    first_new = 0.9 * first + 0.1 * grad
    second_new = 0.999 * second + 0.001 * grad * grad
    first_hat = first_new / (1.0 - jnp.power(0.9, steps_taken))
    second_hat = second_new / (1.0 - jnp.power(0.999, steps_taken))
    weight_new = weight - rate * (first_hat / (jnp.sqrt(second_hat) + 1e-08) + decay * weight)
    return (weight_new, first_new, second_new)


def on_device(
    features,
    targets,
    neighbours,
    nbr_mask,
    flags,
    step_count,
    w_qkv,
    w_out,
    w_up,
    w_down,
    emb_weight,
    vectors,
    m_qkv,
    m_out,
    m_up,
    m_down,
    m_emb,
    m_vectors,
    v_qkv,
    v_out,
    v_up,
    v_down,
    v_emb,
    v_vectors,
):
    depth, d_rows = w_qkv.shape[:2]
    micros, _, rows, feats = features.shape
    queries = neighbours.shape[2]
    context = rows - queries
    width = w_qkv.shape[2] // 3
    d = d_rows * lax.axis_size("dh") * lax.axis_size("dl")
    share = 1.0 / (lax.axis_size("hh") * lax.axis_size("hl"))
    z = Sizes(d, context, queries, depth, width, feats, share)
    c = lax.axis_index("hl")
    c_arr = jnp.full((1,), c, jnp.int32)

    near, far = gather_rows(jnp.concatenate([emb_weight, vectors], axis=1))
    small = jnp.concatenate([near, far], axis=0)
    emb = small[:, :feats]
    vec = jnp.pad(small[:, feats:].T, ((0, 1), (0, 0)))
    def rows_near(block):
        return lax.all_gather(block, "dh", axis=0, tiled=True)

    blocks = []
    for l in range(depth):
        parts = [w_qkv[l][:, width:], w_qkv[l][:, :width], w_out[l]]
        blocks += [jnp.concatenate(parts, axis=1), w_up[l], w_down[l]]

    tables = []
    for m in range(micros):
        t_ctx = roll_half(targets[m, 0][:context], c)
        t_qry = roll_half(targets[m, 0][context:], c)
        t_in = interleave(t_ctx, jnp.zeros((queries,), F32))[:, None]
        flag = roll_half(flags[m, 0], c).astype(F32)
        mask = neighbour_mask(roll_half(neighbours[m, 0], c), roll_half(nbr_mask[m, 0], c), context, c)
        tables.append(dict(feat=features[m, 0], t_in=t_in, side=jnp.stack([flag, t_qry], axis=1), mask=mask))

    held = [vec]

    def beside(kernel, *transfers, ahead=(), strict=False):
        gate = after(held[0], *ahead)
        moved = [t() for t in transfers]
        outs = list(kernel(gate))
        moved = [after(x, outs[0]) for x in moved]
        held[0] = after(vec, *moved)
        if strict:
            outs[-1] = after(outs[-1], *moved)
        return (outs, *moved)

    def sent(pieces):
        held[0] = after(held[0], pieces[0])
        came[0] = pieces[1]
        return pieces

    came = [None]
    near, far = [None] * len(blocks), [None] * len(blocks)

    def gather(i):
        return lambda: rows_near(blocks[i])

    def cross(i, part=None):
        if part is None:
            return lambda: swap(near[i], "dl")
        half = near[i].shape[0] // 2
        return lambda: swap(near[i][part * half : (part + 1) * half], "dl")

    def both(i):
        return near[i], far[i]

    saved = [[None] * depth for _ in range(micros)]
    state = [None] * micros

    def attn_forward(l, m, *transfers, ahead=(), strict=False):
        t, last = tables[m], l == depth - 1

        def call(gate):
            if l == 0:
                inputs = (c_arr, t["t_in"], gate, t["feat"], emb, *both(3 * l), t["mask"])
            else:
                inputs = (gate, *state[m], *both(3 * l), t["mask"])
            return attn_fwd(z, l, last, inputs)

        (x, q, kv, o, lse, mine, *theirs), *moved = beside(call, *transfers, ahead=ahead, strict=strict)
        saved[m][l] = dict(x=x, q=q, kv=kv, o=o, lse=lse)
        state[m] = (x, *sent(head_sum(mine, theirs, came[0])))
        return moved

    def ffn_forward(l, m, *transfers, ahead=()):
        def call(gate):
            return ffn_fwd(z, l, l == depth - 1, (gate, *state[m], *both(3 * l + 1), *both(3 * l + 2)))

        (x1, u, mine, *theirs), *moved = beside(call, *transfers, ahead=ahead)
        saved[m][l].update(x1=x1, u=u)
        state[m] = (x1, *sent(head_sum(mine, theirs, came[0])))
        return moved

    near[0] = rows_near(blocks[0])
    far[0] = swap(near[0], "dl")
    near[1] = rows_near(blocks[1])
    far[1], near[2] = attn_forward(0, 0, cross(1), gather(2), ahead=(near[1],))
    near[3] = rows_near(blocks[3])
    (far[2],) = attn_forward(0, 1, cross(2), strict=True)
    (near[4],) = ffn_forward(0, 0, gather(4))
    far[3], near[5] = ffn_forward(0, 1, cross(3), gather(5))
    far[4] = swap(near[4], "dl")
    (top,) = attn_forward(1, 0, cross(5, 0))
    (low,) = attn_forward(1, 1, cross(5, 1))
    far[5] = jnp.concatenate([top, low], axis=0)
    ffn_forward(1, 0)
    ffn_forward(1, 1)

    g_attn, g_ffn = [None] * depth, [None] * depth
    g_vecs = []
    cot = [None] * micros

    def ffn_backward(l, m, *transfers):
        k, last = saved[m][l], l == depth - 1

        def call(gate):
            weights = (k["u"], *both(3 * l + 1), *both(3 * l + 2))
            if last:
                inputs = (gate, tables[m]["side"], k["x1"], *state[m][1:], *weights)
            else:
                res, pieces = cot[m]
                inputs = (gate, res, saved[m][l + 1]["x"], k["x1"], *pieces, *weights)
            return ffn_bwd(z, l, last, inputs, g_ffn[l])

        (dy, mine, t0, t1, gv, *g_ffn[l]), *moved = beside(call, *transfers)
        g_vecs.append(gv)
        cot[m] = (dy, sent(head_sum(mine, (t0, t1), came[0])))
        return moved

    def attn_backward(l, m, *transfers):
        k, t, last = saved[m][l], tables[m], l == depth - 1

        def call(gate):
            dy, pieces = cot[m]
            inputs = (gate, dy, k["x1"], *pieces, *both(3 * l), k["x"], k["q"], k["kv"], k["o"], k["lse"], t["mask"])
            firsts = (c_arr, t["t_in"], t["feat"]) if l == 0 else ()
            return attn_bwd(z, l, last, inputs, firsts, g_attn[l])

        outs, *moved = beside(call, *transfers)
        if l == 0:
            gv, *g_attn[l] = outs
        else:
            dy, mine, t0, t1, gv, *g_attn[l] = outs
            cot[m] = (dy, sent(head_sum(mine, (t0, t1), came[0])))
        g_vecs.append(gv)
        return moved

    def cross_far(pair):
        return lambda: swap(pair[1], "dl")

    def reduce(part):
        return lambda: scatter_near(part)

    ffn_backward(1, 0)
    ffn_backward(1, 1)
    up1, down1 = g_ffn[1][:2], g_ffn[1][2:]
    attn_backward(1, 0)
    (got,) = attn_backward(1, 1, cross_far(up1))
    own_up1 = up1[0] + got
    packed1 = g_attn[1][:2]
    got, own_up1 = ffn_backward(0, 0, cross_far(down1), reduce(own_up1))
    own_down1 = down1[0] + got
    got, own_down1 = ffn_backward(0, 1, cross_far(packed1), reduce(own_down1))
    own_packed1 = packed1[0] + got
    up0, down0 = g_ffn[0][:2], g_ffn[0][2:]
    own_up0 = near_rows(*up0)
    held[0] = after(held[0], own_up0)
    got, own_up0, own_packed1 = attn_backward(0, 0, cross_far(down0), reduce(own_up0), reduce(own_packed1))
    own_down0 = down0[0] + got
    (own_down0,) = attn_backward(0, 1, reduce(own_down0))
    packed0 = g_attn[0][:2]
    own_packed0 = near_rows(packed0[0], after(packed0[1], own_down0))
    crossed = own_packed0
    own_packed0 = scatter_near(own_packed0)
    own = [[own_packed0, own_packed1], [own_up0, own_up1], [own_down0, own_down1]]

    owned = [
        jnp.stack([jnp.concatenate([o[:, 2 * width : 3 * width], o[:, : 2 * width]], axis=1) for o in own[0]]),
        jnp.stack([o[:, 3 * width :] for o in own[0]]),
        jnp.stack(own[1]),
        jnp.stack(own[2]),
    ]
    g_vec = sum(g_vecs[1:], g_vecs[0])
    n_vec = vectors.shape[1]
    loss_local = g_vec[n_vec, 0]
    g_small = jnp.concatenate([g_attn[0][2], g_vec[:n_vec].T], axis=1)
    own_small = scatter_near(near_rows(g_small[: d // 2], g_small[d // 2 :]))
    own_small = own_small + swap(own_small, "hl")
    own_small = own_small + swap(own_small, "hh")
    owned += [own_small[:, :feats], own_small[:, feats:]]

    squares = share * jnp.sum(own_small * own_small)
    for o in owned[:4]:
        squares = squares + jnp.sum(o * o)
    counted = share * jnp.sum(flags.astype(F32))
    sums = everyone_sum(jnp.stack([squares, share * loss_local, counted]))
    counted = jnp.maximum(sums[2], 1.0)
    loss = sums[1] / counted
    grad_norm = jnp.sqrt(sums[0]) / counted
    factor = CLIP_AT / jnp.maximum(grad_norm, CLIP_AT) / counted
    steps_taken = step_count[0].astype(F32)
    weights = (w_qkv, w_out, w_up, w_down, emb_weight, vectors)
    firsts = (m_qkv, m_out, m_up, m_down, m_emb, m_vectors)
    seconds = (v_qkv, v_out, v_up, v_down, v_emb, v_vectors)
    new_w, new_m, new_v = [], [], []
    for i in range(6):
        rate = LR_VECTOR if i == 5 else LR_MATRIX
        decay = 0.0 if i == 5 else DECAY
        result = adamw(weights[i], owned[i] * factor, firsts[i], seconds[i], rate, decay, steps_taken)
        new_w.append(result[0])
        new_m.append(result[1])
        new_v.append(result[2])
    return (loss, grad_norm, *new_w, *new_m, *new_v)


def solution(mesh):
    dp, head = mesh.shape["dp"], mesh.shape["head"]
    fine = Mesh(mesh.devices.reshape(dp // 2, 2, head // 2, 2), AXES)
    rows, cols = ("dh", "dl"), ("hh", "hl")
    data = (
        P(None, rows, None, None),
        P(None, rows, None),
        P(None, rows, None, None),
        P(None, rows, None, None),
        P(None, rows, None),
        P(),
    )
    params = (P(None, rows, cols),) * 4 + (P(rows, None),) * 2
    return jax.shard_map(
        on_device,
        mesh=fine,
        in_specs=data + params * 3,
        out_specs=(P(), P()) + params * 3,
        check_vma=False,
    )
```

time: 944 us -> 756 us (0.80)
  Pallas kernels: 0 us -> 268 us
  matrix products: 187 us -> 0 us
  waiting for transfers between devices: 452 us -> 287 us
  local copies, waits for them, and re-layouts: 80.7 us -> 36.6 us
  other arithmetic: 98.1 us -> 55.9 us
  blocking collectives: 55.5 us -> 16.3 us
  starting transfers between devices: 30.4 us -> 55.8 us
    pallas_call x0 -> x16, Pallas kernels: none -> 268 us  [run(): pl.pallas_call(kernel, name=name, out_shape=[jax.ShapeDtypeStruct(s, F32)...]
    ppermute x58 -> x90, waiting for transfers between devices: 438 us -> 200 us  [swap(): return lax.ppermute(values, axis, SWAP)]
    dot_general x88 -> x0, matrix products: 187 us -> none  [the longest x64 129 us: dot(): lax.dot_general(a, b, (((ca,), (cb,)), ((), ())), precision=HIGH, preferr...]
    all_gather x6, waiting for transfers between devices: 0.04 us -> 43.8 us  [rows_near(): return lax.all_gather(block, 'dh', axis=0, tiled=True)]
    psum x1 -> x0, blocking collectives: 39.2 us -> none  [on_device(): sums = lax.psum(jnp.stack([squares, share * loss_sum, counted]), AXES)]
    reduce_scatter x5 -> x7, waiting for transfers between devices: 0.06 us -> 37.3 us  [scatter_near(): return lax.psum_scatter(near, 'dh', scatter_dimension=0, tiled=True)]
    reduce_sum x39 -> x2, other arithmetic: 40.2 us -> 9.31 us  [the longest x1 8.7 us: neighbour_mask(): jnp.sum(jnp.where(at[:, None, :] == index, bit[:, None, :], 0), axis=-1)]
    ppermute x58 -> x90, starting transfers between devices: 28.9 us -> 53.1 us  [swap(): return lax.ppermute(values, axis, SWAP)]
  transfers between devices with their start and end apart: 71 -> 105, of which waited for: 36 -> 44; matrix products, arithmetic and copies ran while one was open for 29% -> 7% of each run, Pallas kernels for 0% -> 36%
where the time goes in v2:
time: 756 us; the launch traced here: 745 us
  waiting for transfers between devices  287 us (38%)
  Pallas kernels  268 us (35%)
  other arithmetic  55.9 us (7%)
  starting transfers between devices  55.8 us (7%)
  local copies, waits for them, and re-layouts  36.6 us (5%)
  between operations  25.6 us (3%)
  blocking collectives  16.3 us (2%)
    pallas_call x16, Pallas kernels, run(): pl.pallas_call(kernel, name=name, out_shape=[jax.ShapeDtypeStruct(s, F32)...  268 us
    ppermute x90, waiting for transfers between devices, swap(): return lax.ppermute(values, axis, SWAP)  200 us
    ppermute x90, starting transfers between devices, swap(): return lax.ppermute(values, axis, SWAP)  53.1 us
    all_gather x6, waiting for transfers between devices, rows_near(): return lax.all_gather(block, 'dh', axis=0, tiled=True)  43.8 us
    reduce_scatter x7, waiting for transfers between devices, scatter_near(): return lax.psum_scatter(near, 'dh', scatter_dimension=0, tiled=True)  37.3 us
    unnamed x220, local copies, waits for them, and re-layouts  21.7 us
    add x14, other arithmetic, head_sum(): a = mine + jnp.concatenate([after(first, before), second], axis=0)  18.7 us
    all_gather x1, blocking collectives, gather_rows(): near = lax.all_gather(block, 'dh', axis=0, tiled=True)  16.3 us
  transfers between devices with their start and end apart: 105, of which 44 were waited for; matrix products, arithmetic and copies ran while one was open for 7% of the time, Pallas kernels for 36%

profile of v2, /device:TPU:0, one launch (start us, length us, event | category | flops | bytes accessed | tf_op | source)
XLA Modules:
  0.0 745.0 jit_solution(554148930311603727)
XLA Ops:
  11.8 16.3 %all-gather.4 = f32[4,96,135]{1,2,0:T(8,128)S(1)} all-gather(f32[1,96,135]{1,2,0:T(8,128)S(1)} %maximum_bitcast_fusion.2), channel_id=1, replica_groups=mesh['dh'=4,'dl'=2,'hh'=2,'hl'=2] {'dh'}, dimensions={0}, use_global_device_ids=true | all-gather | bytes 259200 | tf_op jit(solution)/shard_map/all_gather | solution.py:39
  31.3 8.7 %select_reduce_fusion = (s32[256,16]{1,0:T(8,128)S(1)}, s32[256,16]{1,0:T(8,128)S(1)}) fusion(s32[256,256]{1,0:T(8,128)S(1)} %get-tuple-element.478, s32[256,256]{1,0:T(8,128)S(1)} %broadcast_shift-right-arithmetic_fusion, s32[256,256]{1,0:T(8,128)S(1)} %get-tuple-element.479, s32[256,256]{1,0:T(8,128)S(1)} %get-tuple-element.480), kind=kLoop, calls=%fused_computation | loop fusion | flops 6283264 | bytes 1081344 | tf_op jit(solution)/shard_map/reduce_sum | solution.py:732
  51.6 25.3 %all-gather.22.cloned.1.call-done = f32[1,384,768]{2,1,0:T(8,128)} async-done(((f32[1,96,768]{2,1,0:T(8,128)}), f32[1,384,768]{2,1,0:T(8,128)}) %all-gather.22.cloned.1.call-update) | async-done | bytes 1179664 | tf_op jit(solution)/shard_map/all_gather | solution.py:789
  78.0 14.9 %attn_fwd0.2 = (f32[768,768]{1,0:T(8,128)}, f32[768,256]{1,0:T(8,128)}, f32[512,384]{1,0:T(8,128)}, f32[768,256]{1,0:T(8,128)}, f32[768,128]{1,0:T(8,128)}, /*in...) custom-call(s32[1]{0:T(128)} %bitcast.5.refs_0_.refs_15_, f32[768,1]{1,0:T(8,128)} %broadcast_in_dim.62.refs_1_.refs_16_, ...), custom_call_target="tpu_custom_call" | custom-call | flops 317089376 | bytes 838860 | tf_op jit(solution)/shard_map/attn_fwd0/pallas_call | solution.py:154
  94.9 13.8 %all-gather.20.cloned.1.call-done = f32[1,384,768]{2,1,0:T(8,128)} async-done(((f32[1,96,768]{2,1,0:T(8,128)}), f32[1,384,768]{2,1,0:T(8,128)}) %all-gather.20.cloned.1.call-update) | async-done | bytes 1179664 | tf_op jit(solution)/shard_map/all_gather | solution.py:789
  122.3 14.9 %attn_fwd0.3 = (f32[768,768]{1,0:T(8,128)}, f32[768,256]{1,0:T(8,128)}, f32[512,384]{1,0:T(8,128)}, f32[768,256]{1,0:T(8,128)}, f32[768,128]{1,0:T(8,128)}, /*in...) custom-call(s32[1]{0:T(128)} %bitcast.5.refs_0_.refs_15_, f32[768,1]{1,0:T(8,128)} %broadcast_in_dim.63.refs_1_.refs_16_, ...), custom_call_target="tpu_custom_call" | custom-call | flops 317089376 | bytes 838860 | tf_op jit(solution)/shard_map/attn_fwd0/pallas_call | solution.py:154
  137.3 9.4 %collective-permute-done.2.refs_9_.refs_12_ = f32[384,768]{1,0:T(8,128)S(1)} collective-permute-done((f32[384,768]{1,0:T(8,128)}, f32[384,768]{1,0:T(8,128)S(1)}, u32[]{:S(2)}, u32[]{:S(2)}) %collective-permute-start.2) | collective-permute-done | bytes 1179680 | tf_op jit(solution)/shard_map/ppermute | solution.py:27
  153.9 15.2 %ffn_fwd0.2 = (f32[768,768]{1,0:T(8,128)}, f32[768,768]{1,0:T(8,128)}, f32[384,768]{1,0:T(8,128)}, f32[192,768]{1,0:T(8,128)}, f32[192,768]{1,0:T(8,128)}) custom-call(f32[8,768]{1,0:T(8,128)} %pad.8.refs_2_.refs_0_, f32[768,768]{1,0:T(8,128)} %get-tuple-element.189.refs_1_.refs_9_, f32[384,768]{1,0:T(8,128)} %maximum_add_fusion.refs_2_, ...), custom_call_target="tpu_custom_call" | custom-call | flops 271790912 | bytes 1258291 | tf_op jit(solution)/shard_map/ffn_fwd0/pallas_call | solution.py:154
  170.0 8.5 %collective-permute-done.12.refs_3_ = f32[384,768]{1,0:T(8,128)} collective-permute-done((f32[384,768]{1,0:T(8,128)S(1)}, f32[384,768]{1,0:T(8,128)}, u32[]{:S(2)}, u32[]{:S(2)}) %collective-permute-start.12) | collective-permute-done | bytes 1179680 | tf_op jit(solution)/shard_map/ppermute | solution.py:27
  185.6 15.3 %ffn_fwd0.3 = (f32[768,768]{1,0:T(8,128)}, f32[768,768]{1,0:T(8,128)}, f32[384,768]{1,0:T(8,128)}, f32[192,768]{1,0:T(8,128)}, f32[192,768]{1,0:T(8,128)}) custom-call(f32[8,768]{1,0:T(8,128)} %pad.8.refs_2_.refs_0_, f32[768,768]{1,0:T(8,128)} %get-tuple-element.197.refs_1_.refs_9_, f32[384,768]{1,0:T(8,128)} %copy-done.15, ...), custom_call_target="tpu_custom_call" | custom-call | flops 271790912 | bytes 1258291 | tf_op jit(solution)/shard_map/ffn_fwd0/pallas_call | solution.py:154
  203.2 8.4 %collective-permute-done.20.refs_3_ = f32[384,768]{1,0:T(8,128)} collective-permute-done((f32[384,768]{1,0:T(8,128)S(1)}, f32[384,768]{1,0:T(8,128)}, u32[]{:S(2)}, u32[]{:S(2)}) %collective-permute-start.20) | collective-permute-done | bytes 1179680 | tf_op jit(solution)/shard_map/ppermute | solution.py:27
  216.5 24.2 %collective-permute-done.25.refs_3_ = f32[384,768]{1,0:T(8,128)} collective-permute-done((f32[384,768]{1,0:T(8,128)S(1)}, f32[384,768]{1,0:T(8,128)}, u32[]{:S(2)}, u32[]{:S(2)}) %collective-permute-start.25) | collective-permute-done | bytes 1179680 | tf_op jit(solution)/shard_map/ppermute | solution.py:27
  243.1 10.5 %attn_fwd1.2 = (f32[768,768]{1,0:T(8,128)}, f32[256,256]{1,0:T(8,128)}, f32[512,384]{1,0:T(8,128)}, f32[256,256]{1,0:T(8,128)}, f32[256,128]{1,0:T(8,128)}, /*in...) custom-call(f32[8,768]{1,0:T(8,128)} %pad.8.refs_2_.refs_0_, ...), custom_call_target="tpu_custom_call" | custom-call | flops 135895456 | bytes 838860 | tf_op jit(solution)/shard_map/attn_fwd1/pallas_call | solution.py:154
  257.5 13.0 %collective-permute-done.17 = f32[192,768]{1,0:T(8,128)S(1)} collective-permute-done((f32[192,768]{1,0:T(8,128)S(1)}, f32[192,768]{1,0:T(8,128)S(1)}, u32[]{:S(2)}, u32[]{:S(2)}) %collective-permute-start.17) | collective-permute-done | bytes 589856 | tf_op jit(solution)/shard_map/ppermute | solution.py:27
  272.0 10.6 %attn_fwd1.3 = (f32[768,768]{1,0:T(8,128)}, f32[256,256]{1,0:T(8,128)}, f32[512,384]{1,0:T(8,128)}, f32[256,256]{1,0:T(8,128)}, f32[256,128]{1,0:T(8,128)}, /*in...) custom-call(f32[8,768]{1,0:T(8,128)} %pad.8.refs_2_.refs_0_, ...), custom_call_target="tpu_custom_call" | custom-call | flops 135895456 | bytes 838860 | tf_op jit(solution)/shard_map/attn_fwd1/pallas_call | solution.py:154
  286.4 21.2 %collective-permute-done.16 = f32[192,768]{1,0:T(8,128)S(1)} collective-permute-done((f32[192,768]{1,0:T(8,128)S(1)}, f32[192,768]{1,0:T(8,128)S(1)}, u32[]{:S(2)}, u32[]{:S(2)}) %collective-permute-start.16) | collective-permute-done | bytes 589856 | tf_op jit(solution)/shard_map/ppermute | solution.py:27
  309.9 9.2 %ffn_fwd1.2 = (f32[256,768]{1,0:T(8,128)}, f32[256,768]{1,0:T(8,128)}, f32[128,768]{1,0:T(8,128)}, f32[64,768]{1,0:T(8,128)}, f32[64,768]{1,0:T(8,128)}) custom-call(f32[8,768]{1,0:T(8,128)} %pad.8.refs_2_.refs_0_, f32[768,768]{1,0:T(8,128)} %get-tuple-element.223.refs_1_.refs_9_.refs_2_, f32[128,768]{1,0:T(8,128)} %copy-done.34, f32[128,768]{1,0:T(8,128)} %copy-done.69, ...), custom_call_target="tpu_custom_call" | custom-call | flops 90596968 | bytes 1258291 | tf_op jit(solution)/shard_map/ffn_fwd1/pallas_call | solution.py:154
  324.3 9.0 %ffn_fwd1.3 = (f32[256,768]{1,0:T(8,128)}, f32[256,768]{1,0:T(8,128)}, f32[128,768]{1,0:T(8,128)}, f32[64,768]{1,0:T(8,128)}, f32[64,768]{1,0:T(8,128)}) custom-call(f32[8,768]{1,0:T(8,128)} %pad.8.refs_2_.refs_0_, f32[768,768]{1,0:T(8,128)} %get-tuple-element.231.refs_1_.refs_9_.refs_2_, f32[128,768]{1,0:T(8,128)} %copy-done.33, f32[128,768]{1,0:T(8,128)} %copy-done.68, ...), custom_call_target="tpu_custom_call" | custom-call | flops 90596968 | bytes 1258291 | tf_op jit(solution)/shard_map/ffn_fwd1/pallas_call | solution.py:154
  339.6 11.1 %ffn_bwd1.2 = (f32[256,768]{1,0:T(8,128)}, f32[128,768]{1,0:T(8,128)}, f32[64,768]{1,0:T(8,128)}, f32[64,768]{1,0:T(8,128)}, f32[8,768]{1,0:T(8,128)}, /*index=5...) custom-call(f32[8,768]{1,0:T(8,128)} %pad.8.refs_2_.refs_0_, ...), custom_call_target="tpu_custom_call" | custom-call | flops 181193936 | bytes 1677721 | tf_op jit(solution)/shard_map/ffn_bwd1/pallas_call | solution.py:154
  356.1 12.3 %ffn_bwd1.3 = (f32[256,768]{1,0:T(8,128)}, f32[128,768]{1,0:T(8,128)}, f32[64,768]{1,0:T(8,128)}, f32[64,768]{1,0:T(8,128)}, f32[8,768]{1,0:T(8,128)}, /*index=5...) custom-call(f32[8,768]{1,0:T(8,128)} %pad.8.refs_2_.refs_0_, ...), custom_call_target="tpu_custom_call", output_to_operand_aliasing={{5}: (12, {}), {6}: (13, {}), {7}: (14, {}), {8}: (15, {})} | custom-call | flops 181193936 | bytes 1677721 | tf_op jit(solution)/shard_map/ffn_bwd1/pallas_call | solution.py:154
  373.0 15.6 %attn_bwd1.2 = (f32[256,768]{1,0:T(8,128)}, f32[384,768]{1,0:T(8,128)}, f32[192,768]{1,0:T(8,128)}, f32[192,768]{1,0:T(8,128)}, f32[8,768]{1,0:T(8,128)}, /*index=5*/f32[384,768]{1,0:T(8,128)}, f32[384,768]{1,0:T(8,128)}) custom-call(f32[8,768]{1,0:T(8,128)} %pad.8.refs_2_.refs_0_, f32[256,768]{1,0:T(8,128)} %get-tuple-element.269.refs_1_, ...), custom_call_target="tpu_custom_call" | custom-call | flops 301989888 | bytes 1258291 | tf_op jit(solution)/shard_map/attn_bwd1/pallas_call | solution.py:154
  390.6 9.7 %collective-permute-done.58.refs_4_ = f32[128,768]{1,0:T(8,128)S(1)} collective-permute-done((f32[128,768]{1,0:T(8,128)S(1)}, f32[128,768]{1,0:T(8,128)S(1)}, u32[]{:S(2)}, u32[]{:S(2)}) %collective-permute-start.58) | collective-permute-done | bytes 393248 | tf_op jit(solution)/shard_map/ppermute | solution.py:27
  404.3 16.2 %attn_bwd1.3 = (f32[256,768]{1,0:T(8,128)}, f32[384,768]{1,0:T(8,128)}, f32[192,768]{1,0:T(8,128)}, f32[192,768]{1,0:T(8,128)}, f32[8,768]{1,0:T(8,128)}, /*index=5*/f32[384,768]{1,0:T(8,128)}, f32[384,768]{1,0:T(8,128)}) custom-call(f32[8,768]{1,0:T(8,128)} %pad.8.refs_2_.refs_0_, ...), custom_call_target="tpu_custom_call", output_to_operand_aliasing={{5}: (15, {}), {6}: (16, {})} | custom-call | flops 301989888 | bytes 1258291 | tf_op jit(solution)/shard_map/attn_bwd1/pallas_call | solution.py:154
  421.9 8.3 %collective-permute-done.63.refs_5_ = f32[384,768]{1,0:T(8,128)S(1)} collective-permute-done((f32[384,768]{1,0:T(8,128)S(1)}, f32[384,768]{1,0:T(8,128)S(1)}, u32[]{:S(2)}, u32[]{:S(2)}) %collective-permute-start.63) | collective-permute-done | bytes 1179680 | tf_op jit(solution)/shard_map/ppermute | solution.py:27
  439.1 22.2 %ffn_bwd0.2 = (f32[768,768]{1,0:T(8,128)}, f32[384,768]{1,0:T(8,128)}, f32[192,768]{1,0:T(8,128)}, f32[192,768]{1,0:T(8,128)}, f32[8,768]{1,0:T(8,128)}, /*index...) custom-call(f32[8,768]{1,0:T(8,128)} %pad.8.refs_2_.refs_0_, ...), custom_call_target="tpu_custom_call" | custom-call | flops 543581824 | bytes 1677721 | tf_op jit(solution)/shard_map/ffn_bwd0/pallas_call | solution.py:154
  472.7 23.9 %ffn_bwd0.3 = (f32[768,768]{1,0:T(8,128)}, f32[384,768]{1,0:T(8,128)}, f32[192,768]{1,0:T(8,128)}, f32[192,768]{1,0:T(8,128)}, f32[8,768]{1,0:T(8,128)}, /*index...) custom-call(f32[8,768]{1,0:T(8,128)} %pad.8.refs_2_.refs_0_, ...), custom_call_target="tpu_custom_call", output_to_operand_aliasing={{5}: (13, {}), {6}: (14, {}), {7}: (15, {}), {8}: (16, {})} | custom-call | flops 543581824 | bytes 1677721 | tf_op jit(solution)/shard_map/ffn_bwd0/pallas_call | solution.py:154
  501.8 25.6 %collective-permute-done.77 = f32[384,768]{1,0:T(8,128)S(1)} collective-permute-done((f32[384,768]{1,0:T(8,128)S(1)}, f32[384,768]{1,0:T(8,128)S(1)}, u32[]{:S(2)}, u32[]{:S(2)}) %collective-permute-start.77) | collective-permute-done | bytes 1179680 | tf_op jit(solution)/shard_map/ppermute | solution.py:27
  537.8 33.2 %attn_bwd0.2 = (f32[8,768]{1,0:T(8,128)}, f32[384,768]{1,0:T(8,128)}, f32[384,768]{1,0:T(8,128)}, f32[768,128]{1,0:T(8,128)}) custom-call(f32[8,768]{1,0:T(8,128)} %pad.8.refs_2_.refs_0_, f32[768,768]{1,0:T(8,128)} %get-tuple-element.296.refs_1_, f32[768,768]{1,0:T(8,128)} %get-tuple-element.206.refs_1_.refs_3_.refs_2_, f32[384,768]{1,0:T(8,128)} %copy-done.9, ...), custom_call_target="tpu_custom_call" | custom-call | flops 724775744 | bytes 1258291 | tf_op jit(solution)/shard_map/attn_bwd0/pallas_call | solution.py:154
  579.6 33.6 %attn_bwd0.3 = (f32[8,768]{1,0:T(8,128)}, f32[384,768]{1,0:T(8,128)}, f32[384,768]{1,0:T(8,128)}, f32[768,128]{1,0:T(8,128)}) custom-call(f32[8,768]{1,0:T(8,128)} %pad.8.refs_2_.refs_0_, f32[768,768]{1,0:T(8,128)} %get-tuple-element.313.refs_1_, ...), custom_call_target="tpu_custom_call", output_to_operand_aliasing={{1}: (18, {}), {2}: (19, {}), {3}: (20, {})} | custom-call | flops 724775744 | bytes 1258291 | tf_op jit(solution)/shard_map/attn_bwd0/pallas_call | solution.py:154
  617.4 32.6 %collective-permute-done.83 = f32[384,135]{1,0:T(8,128)S(1)} collective-permute-done((f32[384,135]{1,0:T(8,128)S(1)}, f32[384,135]{1,0:T(8,128)S(1)}, u32[]{:S(2)}, u32[]{:S(2)}) %collective-permute-start.83) | collective-permute-done | bytes 207392 | tf_op jit(solution)/shard_map/ppermute | solution.py:27
  653.6 15.9 %reduce-scatter.16.cloned.1.call-done = f32[96,135]{1,0:T(8,128)} async-done(((f32[384,135]{1,0:T(8,128)}), f32[96,135]{1,0:T(8,128)}) %reduce-scatter.16.cloned.1.call-update) | async-done | bytes 51856 | tf_op jit(solution)/shard_map/reduce_scatter | solution.py:62
  678.2 21.4 %reduce-scatter.20.cloned.1.call-done = f32[96,768]{1,0:T(8,128)} async-done(((f32[384,768]{1,0:T(8,128)}), f32[96,768]{1,0:T(8,128)}) %reduce-scatter.20.cloned.1.call-update) | async-done | bytes 294928 | tf_op jit(solution)/shard_map/reduce_scatter | solution.py:62
  (539 shorter events, 189.3 us)
Async XLA Ops:
  7.2 38.2 %all-gather.12.cloned.1.call-start = ((), (), s32[]{:S(2)}) async-start(), calls=%async_computation.7 | async-start | bytes 1474560 | tf_op jit(solution)/shard_map/all_gather | solution.py:789
  10.7 66.2 %all-gather.22.cloned.1.call-start = ((), (), s32[]{:S(2)}) async-start(), calls=%async_computation.19 | async-start | bytes 1474560 | tf_op jit(solution)/shard_map/all_gather | solution.py:789
  11.7 97.0 %all-gather.20.cloned.1.call-start = ((), (), s32[]{:S(2)}) async-start(), calls=%async_computation.18 | async-start | bytes 1474560 | tf_op jit(solution)/shard_map/all_gather | solution.py:789
  30.9 153.7 %all-gather.18.cloned.1.call-start = ((), (), s32[]{:S(2)}) async-start(), calls=%async_computation.17 | async-start | bytes 1474560 | tf_op jit(solution)/shard_map/all_gather | solution.py:789
  45.4 31.5 %collective-permute-start.1 = (f32[384,768]{1,0:T(8,128)}, f32[384,768]{1,0:T(8,128)S(1)}, u32[]{:S(2)}, u32[]{:S(2)}) collective-permute-start(f32[384,768]{1,0:T(8,128)} %all-gather.12.cloned.1.call-done.refs_5_.refs_7_), channel_id=1, source_target_pairs={{0,4},{4,0},{1,5},{5,1},{2,6},{6,2},{3,7},{7,3},{8,12},{12,8},{9,1... | collective-permute-start | bytes 3538952 | tf_op jit(solution)/shard_map/ppermute | solution.py:27
  93.5 28.8 %collective-permute-start.3 = (f32[384,768]{1,0:T(8,128)S(1)}, f32[384,768]{1,0:T(8,128)S(1)}, u32[]{:S(2)}, u32[]{:S(2)}) collective-permute-start(f32[384,768]{1,0:T(8,128)S(1)} %bitcast.118), channel_id=1, source_target_pairs={{0,4},{4,0},{1,5},{5,1},{2,6},{6,2},{3,7},{7,3},{8,12},{12,8},{9,1... | collective-permute-start | bytes 3538952 | tf_op jit(solution)/shard_map/ppermute | solution.py:27
  108.7 38.0 %collective-permute-start.2 = (f32[384,768]{1,0:T(8,128)}, f32[384,768]{1,0:T(8,128)S(1)}, u32[]{:S(2)}, u32[]{:S(2)}) collective-permute-start(f32[384,768]{1,0:T(8,128)} %bitcast.119), channel_id=1, source_target_pairs={{0,4},{4,0},{1,5},{5,1},{2,6},{6,2},{3,7},{7,3},{8,12},{12,8},{9,1... | collective-permute-start | bytes 3538952 | tf_op jit(solution)/shard_map/ppermute | solution.py:27
  113.0 34.4 %collective-permute-start.7 = (f32[384,768]{1,0:T(8,128)}, f32[384,768]{1,0:T(8,128)}, u32[]{:S(2)}, u32[]{:S(2)}) collective-permute-start(f32[384,768]{1,0:T(8,128)} %maximum_add_fusion.refs_2_), channel_id=1, source_target_pairs={{0,2},{2,0},{1,3},{3,1},{4,6},{6,4},{5,7},{7,5},{8,10},{10,8},{9,1... | collective-permute-start | bytes 3538952 | tf_op jit(solution)/shard_map/ppermute | solution.py:27
  146.7 67.8 %all-gather.14.cloned.1.call-start = ((), (), s32[]{:S(2)}) async-start(), calls=%async_computation.8 | async-start | bytes 1474560 | tf_op jit(solution)/shard_map/all_gather | solution.py:789
  179.4 62.7 %all-gather.16.cloned.1.call-start = ((), (), s32[]{:S(2)}) async-start(), calls=%async_computation.16 | async-start | bytes 1474560 | tf_op jit(solution)/shard_map/all_gather | solution.py:789
  183.0 28.6 %collective-permute-start.20 = (f32[384,768]{1,0:T(8,128)S(1)}, f32[384,768]{1,0:T(8,128)}, u32[]{:S(2)}, u32[]{:S(2)}) collective-permute-start(f32[384,768]{1,0:T(8,128)S(1)} %maximum_add_fusion.2.refs_2_), channel_id=1, source_target_pairs={{0,2},{2,0},{1,3},{3,1},{4,6},{6,4},{5,7},{7,5},{8,10},{10,8},{9,1... | collective-permute-start | bytes 3538952 | tf_op jit(solution)/shard_map/ppermute | solution.py:27
  201.5 264.4 %reduce-scatter.8.cloned.1.call-start = ((), (), s32[]{:S(2)}) async-start(), calls=%async_computation.9 | async-start | bytes 1474560 | tf_op jit(solution)/shard_map/reduce_scatter | solution.py:62
  216.5 55.5 %collective-permute-start.27 = (f32[384,768]{1,0:T(8,128)S(1)}, f32[384,768]{1,0:T(8,128)}, u32[]{:S(2)}, u32[]{:S(2)}) collective-permute-start(f32[384,768]{1,0:T(8,128)S(1)} %maximum_add_fusion.3.refs_2_), channel_id=1, source_target_pairs={{0,1},{1,0},{2,3},{3,2},{4,5},{5,4},{6,7},{7,6},{8,9},{9,8},{10,11... | collective-permute-start | bytes 3538952 | tf_op jit(solution)/shard_map/ppermute | solution.py:27
  240.8 31.2 %collective-permute-start.28 = (f32[384,768]{1,0:T(8,128)}, f32[384,768]{1,0:T(8,128)}, u32[]{:S(2)}, u32[]{:S(2)}) collective-permute-start(f32[384,768]{1,0:T(8,128)} %collective-permute-done.25.refs_3_), channel_id=1, source_target_pairs={{0,1},{1,0},{2,3},{3,2},{4,5},{5,4},{6,7},{7,6},{8,9},{9,8},{10,11... | collective-permute-start | bytes 3538952 | tf_op jit(solution)/shard_map/ppermute | solution.py:27
  255.8 51.8 %collective-permute-start.34 = (f32[384,768]{1,0:T(8,128)S(1)}, f32[384,768]{1,0:T(8,128)S(1)}, u32[]{:S(2)}, u32[]{:S(2)}) collective-permute-start(f32[384,768]{1,0:T(8,128)S(1)} %bitcast.128), channel_id=1, source_target_pairs={{0,4},{4,0},{1,5},{5,1},{2,6},{6,2},{3,7},{7,3},{8,12},{12,8},{9,1... | collective-permute-start | bytes 3538952 | tf_op jit(solution)/shard_map/ppermute | solution.py:27
  270.5 37.1 %collective-permute-start.16 = (f32[192,768]{1,0:T(8,128)S(1)}, f32[192,768]{1,0:T(8,128)S(1)}, u32[]{:S(2)}, u32[]{:S(2)}) collective-permute-start(f32[192,768]{1,0:T(8,128)S(1)} %get-tuple-element.477), channel_id=1, source_target_pairs={{0,4},{4,0},{1,5},{5,1},{2,6},{6,2},{3,7},{7,3},{8,12},{12,8},{9,1... | collective-permute-start | bytes 1769480 | tf_op jit(solution)/shard_map/ppermute | solution.py:27
  285.7 35.1 %collective-permute-start.36 = (f32[128,768]{1,0:T(8,128)S(1)}, f32[128,768]{1,0:T(8,128)S(1)}, u32[]{:S(2)}, u32[]{:S(2)}) collective-permute-start(f32[128,768]{1,0:T(8,128)S(1)} %maximum_add_fusion.9.refs_2_), channel_id=1, source_target_pairs={{0,2},{2,0},{1,3},{3,1},{4,6},{6,4},{5,7},{7,5},{8,10},{10,8},{9,1... | collective-permute-start | bytes 1179656 | tf_op jit(solution)/shard_map/ppermute | solution.py:27
  369.5 51.0 %collective-permute-start.51 = (f32[384,768]{1,0:T(8,128)}, f32[384,768]{1,0:T(8,128)S(1)}, u32[]{:S(2)}, u32[]{:S(2)}) collective-permute-start(f32[384,768]{1,0:T(8,128)} %get-tuple-element.263), channel_id=1, source_target_pairs={{0,4},{4,0},{1,5},{5,1},{2,6},{6,2},{3,7},{7,3},{8,12},{12,8},{9,1... | collective-permute-start | bytes 3538952 | tf_op jit(solution)/shard_map/ppermute | solution.py:27
  401.9 28.3 %collective-permute-start.63 = (f32[384,768]{1,0:T(8,128)S(1)}, f32[384,768]{1,0:T(8,128)S(1)}, u32[]{:S(2)}, u32[]{:S(2)}) collective-permute-start(f32[384,768]{1,0:T(8,128)S(1)} %maximum_add_fusion.4.refs_4_), channel_id=1, source_target_pairs={{0,2},{2,0},{1,3},{3,1},{4,6},{6,4},{5,7},{7,5},{8,10},{10,8},{9,1... | collective-permute-start | bytes 3538952 | tf_op jit(solution)/shard_map/ppermute | solution.py:27
  421.7 116.1 %reduce-scatter.10.cloned.1.call-start = ((), (), s32[]{:S(2)}) async-start(), calls=%async_computation.10 | async-start | bytes 1474560 | tf_op jit(solution)/shard_map/reduce_scatter | solution.py:62
  430.2 31.1 %collective-permute-start.50 = (f32[384,768]{1,0:T(8,128)}, f32[384,768]{1,0:T(8,128)S(1)}, u32[]{:S(2)}, u32[]{:S(2)}) collective-permute-start(f32[384,768]{1,0:T(8,128)} %get-tuple-element.262), channel_id=1, source_target_pairs={{0,4},{4,0},{1,5},{5,1},{2,6},{6,2},{3,7},{7,3},{8,12},{12,8},{9,1... | collective-permute-start | bytes 3538952 | tf_op jit(solution)/shard_map/ppermute | solution.py:27
  462.5 111.8 %reduce-scatter.14.cloned.1.call-start = ((), (), s32[]{:S(2)}) async-start(), calls=%async_computation.12 | async-start | bytes 1474560 | tf_op jit(solution)/shard_map/reduce_scatter | solution.py:62
  464.3 32.3 %collective-permute-start.73 = (f32[384,768]{1,0:T(8,128)}, f32[384,768]{1,0:T(8,128)}, u32[]{:S(2)}, u32[]{:S(2)}) collective-permute-start(f32[384,768]{1,0:T(8,128)} %get-tuple-element.312), channel_id=1, source_target_pairs={{0,4},{4,0},{1,5},{5,1},{2,6},{6,2},{3,7},{7,3},{8,12},{12,8},{9,1... | collective-permute-start | bytes 3538952 | tf_op jit(solution)/shard_map/ppermute | solution.py:27
  499.2 75.1 %reduce-scatter.12.cloned.1.call-start = ((), (), s32[]{:S(2)}) async-start(), calls=%async_computation.11 | async-start | bytes 1474560 | tf_op jit(solution)/shard_map/reduce_scatter | solution.py:62
  500.4 28.3 %collective-permute-start.75 = (f32[384,768]{1,0:T(8,128)S(1)}, f32[384,768]{1,0:T(8,128)}, u32[]{:S(2)}, u32[]{:S(2)}) collective-permute-start(f32[384,768]{1,0:T(8,128)S(1)} %maximum_add_fusion.6.refs_3_), channel_id=1, source_target_pairs={{0,2},{2,0},{1,3},{3,1},{4,6},{6,4},{5,7},{7,5},{8,10},{10,8},{9,1... | collective-permute-start | bytes 3538952 | tf_op jit(solution)/shard_map/ppermute | solution.py:27
  528.5 84.8 %reduce-scatter.18.cloned.1.call-start = ((), (), s32[]{:S(2)}) async-start(), calls=%async_computation.14 | async-start | bytes 1474560 | tf_op jit(solution)/shard_map/reduce_scatter | solution.py:62
  529.8 41.3 %collective-permute-start.72 = (f32[384,768]{1,0:T(8,128)S(1)}, f32[384,768]{1,0:T(8,128)}, u32[]{:S(2)}, u32[]{:S(2)}) collective-permute-start(f32[384,768]{1,0:T(8,128)S(1)} %copy-done.38), channel_id=1, source_target_pairs={{0,4},{4,0},{1,5},{5,1},{2,6},{6,2},{3,7},{7,3},{8,12},{12,8},{9,1... | collective-permute-start | bytes 3538952 | tf_op jit(solution)/shard_map/ppermute | solution.py:27
  536.3 37.5 %collective-permute-start.80 = (f32[384,768]{1,0:T(8,128)S(1)}, f32[384,768]{1,0:T(8,128)}, u32[]{:S(2)}, u32[]{:S(2)}) collective-permute-start(f32[384,768]{1,0:T(8,128)S(1)} %maximum_add_fusion.7.refs_3_), channel_id=1, source_target_pairs={{0,2},{2,0},{1,3},{3,1},{4,6},{6,4},{5,7},{7,5},{8,10},{10,8},{9,1... | collective-permute-start | bytes 3538952 | tf_op jit(solution)/shard_map/ppermute | solution.py:27
  573.5 96.0 %reduce-scatter.16.cloned.1.call-start = ((), (), s32[]{:S(2)}) async-start(), calls=%async_computation.13 | async-start | bytes 491520 | tf_op jit(solution)/shard_map/reduce_scatter | solution.py:62
  613.3 37.8 %collective-permute-start.86 = (f32[384,768]{1,0:T(8,128)}, f32[384,768]{1,0:T(8,128)S(1)}, u32[]{:S(2)}, u32[]{:S(2)}) collective-permute-start(f32[384,768]{1,0:T(8,128)} %get-tuple-element.355), channel_id=1, source_target_pairs={{0,4},{4,0},{1,5},{5,1},{2,6},{6,2},{3,7},{7,3},{8,12},{12,8},{9,1... | collective-permute-start | bytes 3538952 | tf_op jit(solution)/shard_map/ppermute | solution.py:27
  616.4 33.7 %collective-permute-start.83 = (f32[384,135]{1,0:T(8,128)S(1)}, f32[384,135]{1,0:T(8,128)S(1)}, u32[]{:S(2)}, u32[]{:S(2)}) collective-permute-start(f32[384,135]{1,0:T(8,128)S(1)} %pad_maximum_fusion.3), channel_id=1, source_target_pairs={{0,4},{4,0},{1,5},{5,1},{2,6},{6,2},{3,7},{7,3},{8,12},{12,8},{9,1... | collective-permute-start | bytes 622088 | tf_op jit(solution)/shard_map/ppermute | solution.py:27
  650.8 48.7 %reduce-scatter.20.cloned.1.call-start = ((), (), s32[]{:S(2)}) async-start(), calls=%async_computation.15 | async-start | bytes 1474560 | tf_op jit(solution)/shard_map/reduce_scatter | solution.py:62
  (180 other events, 2023.8 us)
Sparse Core Ops, SparseCore 0:
  10.8 34.5 all-gather.11
  47.6 29.3 all-gather.21
  79.1 29.5 all-gather.19
  146.8 29.7 all-gather.17
  179.5 29.7 all-gather.13
  210.7 29.5 all-gather.15
  421.8 26.9 reduce-scatter.7
  462.6 27.0 reduce-scatter.9
  499.3 27.7 reduce-scatter.13
  529.3 27.8 reduce-scatter.11
  573.6 27.1 reduce-scatter.17
  651.0 18.5 reduce-scatter.15
  672.0 27.5 reduce-scatter.19

commit v3 on v2

--- a/solution.py
+++ b/solution.py
@@ -28,11 +28,11 @@
 
 
 def head_sum(mine, theirs, before=None):
+    if before is not None and before.shape[0] < mine.shape[0]:
+        theirs, before = [after(t, before) for t in theirs], None
     first, second = (swap(t, "hl") for t in theirs)
     a = mine + jnp.concatenate([after(first, before), second], axis=0)
-    c = swap(a, "hl")
-    b = swap(a, "hh")
-    return a, b, c, swap(b, "hl")
+    return [a, swap(a, "hh"), swap(a, "hl")]
 
 
 def gather_rows(block):
@@ -144,6 +144,22 @@
         copies.start(part.at[pl.ds(half + i * quarter, quarter)], piece)
     if mine is not None:
         copies.start(part.at[pl.ds(0, half)], mine)
+
+
+def load_weight(copies, arrays, dst, z_ref=None):
+    if len(arrays) == 2:
+        return load_pair(copies, arrays[0], arrays[1], dst)
+    rows = dst.shape[0] // 8
+    made = []
+    for i in range(8):
+        if len(arrays) == 1:
+            src = arrays[0].at[pl.ds(((i % 4) * 2 + i // 4) * rows, rows)]
+            at = i * rows
+        else:
+            src = arrays[i]
+            at = pl.multiple_of((i // 4 * 4 + jnp.bitwise_xor(z_ref[1], i % 4)) * rows, 8)
+        made.append(copies.start(src, dst.at[pl.ds(at, rows)]))
+    return tuple(made)
 
 
 def row(vec_ref, index):
@@ -213,12 +229,13 @@
     return jnp.concatenate([s[:masked_from], low], axis=0)
 
 
-def attn_fwd_kernel(z, l, first, last, *refs):
+def attn_fwd_kernel(z, l, first, last, blocks, *refs):
+    c_ref = None
     if first:
-        (c_ref, t_in, vec, feat, emb, wn, wf, mask) = refs[:8]
-        refs = refs[8:]
-    else:
-        (vec, xp, pa, pb, pc, pd, wn, wf, mask) = refs[:9]
+        (c_ref, t_in, vec, feat, emb, *weights, mask) = refs[: 6 + blocks]
+        refs = refs[6 + blocks :]
+    else:
+        (vec, xp, pa, pb, pc, pd, *weights, mask) = refs[:9]
         refs = refs[9:]
     x_out, q_out, kv_out, o_out, lse_out, mine, *theirs = refs[:8]
     (xb, wb, wh, wl, qb, kvb, ob, lseb, part, maskb, *rest, sems) = refs[8:]
@@ -233,7 +250,7 @@
         ca = [
             copies.start(p, add.at[pl.ds(i * z.half, z.half)]) for i, p in enumerate((pa, pb, pc, pd))
         ]
-    cw = load_pair(copies, wn, wf, wb)
+    cw = load_weight(copies, weights, wb, c_ref)
     cm = copies.start(mask, maskb)
     if first:
         copies.wait(*cf, ce)
@@ -299,7 +316,7 @@
     copies.wait_all()
 
 
-def attn_fwd(z, l, last, inputs):
+def attn_fwd(z, l, last, blocks, inputs):
     first = l == 0
     rq = z.queries if last else z.rows
     scratch = [
@@ -316,7 +333,7 @@
     ]
     if first:
         scratch += [pltpu.VMEM((z.rows, z.feats), F32), pltpu.VMEM((z.d, z.feats), F32)]
-        specs = [SMEM, VMEM, VMEM] + [ANY] * 5
+        specs = [SMEM, VMEM, VMEM] + [ANY] * (3 + blocks)
     else:
         scratch += [pltpu.VMEM((4 * z.half, z.d), F32)]
         specs = [VMEM] + [ANY] * 8
@@ -331,22 +348,24 @@
         (rq // 4, z.d),
     ]
     return run(
-        functools.partial(attn_fwd_kernel, z, l, first, last),
+        functools.partial(attn_fwd_kernel, z, l, first, last, blocks),
         f"attn_fwd{l}",
         inputs,
         specs,
         outs,
         scratch,
-        24,
+        48,
         3 * 2 * (2 * rq * z.d * 256 + z.context * z.d * 384 + 6 * rq * z.context * 256),
         16 << 20,
     )
 
 
-def ffn_fwd_kernel(z, l, last, *refs):
-    (vec, xp, pa, pb, pc, pd, un, uf, dn, df) = refs[:10]
-    x_out, u_out, mine, *theirs = refs[10:15]
-    (xb, add, wb, wh, wl, vb, vh, vl, ub, part, sems) = refs[15:]
+def ffn_fwd_kernel(z, l, last, blocks, *refs):
+    (vec, xp, pa, pb, pc, pd, *weights) = refs[: 6 + sum(blocks)]
+    refs = refs[6 + sum(blocks) :]
+    ups, downs = weights[: blocks[0]], weights[blocks[0] :]
+    x_out, u_out, mine, *theirs = refs[:5]
+    (xb, add, wb, wh, wl, vb, vh, vl, ub, part, sems) = refs[5:]
     copies = Copies(sems)
     half = z.hq if last else z.half
     if last:
@@ -357,8 +376,8 @@
     else:
         cx = [copies.start(xp, xb)]
     ca = [copies.start(p, add.at[pl.ds(i * half, half)]) for i, p in enumerate((pa, pb, pc, pd))]
-    cu = load_pair(copies, un, uf, wb)
-    cd = load_pair(copies, dn, df, vb)
+    cu = load_weight(copies, ups, wb)
+    cd = load_weight(copies, downs, vb)
     copies.wait(*cx, *ca)
     gain = row(vec, z.depth + l)
     for i in range(2):
@@ -389,30 +408,32 @@
     copies.wait_all()
 
 
-def ffn_fwd(z, l, last, inputs):
+def ffn_fwd(z, l, last, blocks, inputs):
     r = z.queries if last else z.rows
     big = lambda t=F32: pltpu.VMEM((z.d, z.d), t)
     tall = lambda: pltpu.VMEM((r, z.d), F32)
     return run(
-        functools.partial(ffn_fwd_kernel, z, l, last),
+        functools.partial(ffn_fwd_kernel, z, l, last, blocks),
         f"ffn_fwd{l}",
         inputs,
-        [VMEM] + [ANY] * 9,
+        [VMEM] + [ANY] * (5 + sum(blocks)),
         [(r, z.d), (r, z.d), (r // 2, z.d), (r // 4, z.d), (r // 4, z.d)],
         [tall(), pltpu.VMEM((2 * r, z.d), F32), big(), big(BF16), big(BF16), big(), big(BF16), big(BF16), tall(), tall()],
-        20,
+        48,
         3 * 4 * r * z.d * z.d,
         24 << 20,
     )
 
 
-def ffn_bwd_kernel(z, l, last, accumulate, *refs):
+def ffn_bwd_kernel(z, l, last, accumulate, blocks, *refs):
+    held = sum(blocks)
     if last:
-        (vec, side, xm, pa, pb, pc, pd, u_in, un, uf, dn, df) = refs[:12]
-        refs = refs[12:]
-    else:
-        (vec, res, xn, xm, pa, pb, pc, pd, u_in, un, uf, dn, df) = refs[:13]
-        refs = refs[13:]
+        (vec, side, xm, pa, pb, pc, pd, u_in, *weights) = refs[: 8 + held]
+        refs = refs[8 + held :]
+    else:
+        (vec, res, xn, xm, pa, pb, pc, pd, u_in, *weights) = refs[: 9 + held]
+        refs = refs[9 + held :]
+    ups, downs = weights[: blocks[0]], weights[blocks[0] :]
     if accumulate:
         olds, refs = refs[:4], refs[4:]
     dy_out, mine, *theirs, gv, gun, guf, gdn, gdf = refs[:9]
@@ -427,9 +448,9 @@
         ca.append(copies.start(xn, xnb))
         for i in range(2):
             ca.append(copies.start(res.at[pl.ds(i * z.hq, z.hq)], dyb.at[pl.ds(i * z.half + z.hc, z.hq)]))
-    cd = load_pair(copies, dn, df, vb)
+    cd = load_weight(copies, downs, vb)
     cu_in = copies.start(u_in, ub)
-    cu = load_pair(copies, un, uf, wb)
+    cu = load_weight(copies, ups, wb)
     if accumulate:
         co = (*load_pair(copies, olds[0], olds[1], gub), *load_pair(copies, olds[2], olds[3], gdb))
     gvb[...] = jnp.zeros_like(gvb)
@@ -502,7 +523,7 @@
     copies.wait_all()
 
 
-def ffn_bwd(z, l, last, inputs, olds):
+def ffn_bwd(z, l, last, blocks, inputs, olds):
     r = z.queries if last else z.rows
     big = lambda t=F32: pltpu.VMEM((z.d, z.d), t)
     tall = lambda t=F32: pltpu.VMEM((r, z.d), t)
@@ -520,50 +541,46 @@
         inputs = list(inputs) + list(olds)
         specs = specs + [ANY] * 4
     return run(
-        functools.partial(ffn_bwd_kernel, z, l, last, olds is not None),
+        functools.partial(ffn_bwd_kernel, z, l, last, olds is not None, blocks),
         f"ffn_bwd{l}",
         inputs,
         specs,
         outs,
         scratch,
-        36,
+        48,
         3 * 8 * r * z.d * z.d,
         32 << 20,
         aliases,
     )
 
 
-def attn_bwd_kernel(z, l, first, last, accumulate, *refs):
-    (vec, dyp, xm, pa, pb, pc, pd, wn, wf, x_in, q_in, kv_in, o_in, lse_in, mask) = refs[:15]
-    refs = refs[15:]
+def attn_bwd_kernel(z, l, first, last, accumulate, blocks, *refs):
+    (vec, dyp, xm, pa, pb, pc, pd, *weights) = refs[: 7 + blocks]
+    (x_in, q_in, kv_in, o_in, lse_in, mask) = refs[7 + blocks : 13 + blocks]
+    refs = refs[13 + blocks :]
+    c_ref = None
     if first:
-        (c_ref, t_in, feat) = refs[:3]
-        refs = refs[3:]
+        c_ref, refs = refs[0], refs[1:]
     if accumulate:
-        olds, refs = refs[: 3 if first else 2], refs[3 if first else 2 :]
+        olds, refs = refs[:2], refs[2:]
     if first:
-        gv, gn, gf, emb_out = refs[:4]
-        refs = refs[4:]
+        dy_out, dq_out, dkv_out, gv, gn, gf = refs[:6]
+        refs = refs[6:]
     else:
         dy_out, mine, *theirs, gv, gn, gf = refs[:7]
         refs = refs[7:]
-    (dyb, xmb, add, wb, wh, wl, xb, qb, kvb, ob, lseb, maskb, dyh, dyl, dqb, dkb, dvb, gb, gvb, *rest, sems) = refs
+    (dyb, xmb, add, wb, wh, wl, xb, qb, kvb, ob, lseb, maskb, dyh, dyl, dqb, dkb, dvb, gb, gvb, sems) = refs
     copies = Copies(sems)
     rq = z.queries if last else z.rows
     half = rq // 2
     ca = [copies.start(p, add.at[pl.ds(i * half, half)]) for i, p in enumerate((pa, pb, pc, pd))]
     ca += [copies.start(dyp, dyb), copies.start(xm, xmb)]
-    cw = load_pair(copies, wn, wf, wb)
+    cw = load_weight(copies, weights, wb, c_ref)
     cq = [copies.start(q_in, qb), copies.start(kv_in, kvb), copies.start(o_in, ob)]
     cq += [copies.start(lse_in, lseb), copies.start(mask, maskb)]
     cx = [copies.start(x_in, xb)]
-    if first:
-        featb, geb = rest
-        cx += load_feats(copies, z, c_ref, feat, featb)
     if accumulate:
         co = list(load_pair(copies, olds[0], olds[1], gb))
-        if first:
-            co.append(copies.start(olds[2], geb))
     gvb[...] = jnp.zeros_like(gvb)
     copies.wait(*ca)
     gain2 = row(vec, z.depth + l)
@@ -577,8 +594,7 @@
         a, b = split(dy)
         dyh[here, :] = a
         dyl[here, :] = b
-    if not first:
-        copies.start(dyb, dy_out)
+    copies.start(dyb, dy_out)
     copies.wait(*cw)
     split_into(wh, wl, wb[...])
     copies.wait(*cq)
@@ -613,6 +629,9 @@
     kvb[:, 0:128] = dkb[:, 0:128]
     kvb[:, 128:256] = dkb[:, 128:256] + dvb[:, 0:128]
     kvb[:, 256:384] = dvb[:, 128:256]
+    if first:
+        copies.start(dqb, dq_out)
+        copies.start(kvb, dkv_out)
     if accumulate:
         copies.wait(*co)
     g_out = mm((dyh[...], dyl[...]), split(ob[...]), 0, 0)
@@ -621,7 +640,6 @@
     dnb = add
     g_q = jnp.zeros((z.d, 256), F32)
     g_kv = jnp.zeros((z.d, 384), F32)
-    ge = 0.0
     for i in (1, 0):
         here = pl.ds(i * z.half, z.half)
         nh, rstd = norm_stats(xb[here, :])
@@ -633,23 +651,19 @@
         dkv = split(kvb[pl.ds(i * z.hc, z.hc), :])
         g_q = g_q + mm(nq, dq, 0, 0)
         g_kv = g_kv + mm(nc, dkv, 0, 0)
+        if first:
+            continue
         dn_q = mm(dq, (wh[:, z.q], wl[:, z.q]), 1, 1)
         dn_c = mm(dkv, (wh[:, z.kv], wl[:, z.kv]), 1, 1)
         if last:
             dn = jnp.concatenate([dn_c, dn_q], axis=0)
         else:
             dn = jnp.concatenate([dn_q[: z.hc] + dn_c, dn_q[z.hc :]], axis=0)
-        if first:
-            gvb[pl.ds(l, 1), :] += jnp.sum(dn * nh, axis=0, keepdims=True)
-            dx = z.share * dyb[here, :] + norm_back(dn * gain, nh, rstd)
-            gvb[pl.ds(2 * z.depth + 1, 1), :] += jnp.sum(dx * t_in[here, :], axis=0, keepdims=True)
-            ge = ge + mm(split(dx), split(featb[here, :]), 0, 0)
+        dnb[pl.ds(i * z.half, z.half), :] = dn
+        if i > 0:
+            send_parts(copies, dnb, z.half, None, theirs)
         else:
-            dnb[pl.ds(i * z.half, z.half), :] = dn
-            if i > 0:
-                send_parts(copies, dnb, z.half, None, theirs)
-            else:
-                copies.start(dnb.at[here], mine)
+            copies.start(dnb.at[here], mine)
     copies.start(gvb, gv)
     new = [
         g_kv,
@@ -665,13 +679,10 @@
     d_half = z.d // 2
     copies.start(gb.at[pl.ds(0, d_half)], gn)
     copies.start(gb.at[pl.ds(d_half, d_half)], gf)
-    if first:
-        geb[...] = geb[...] + ge if accumulate else ge
-        copies.start(geb, emb_out)
     copies.wait_all()
 
 
-def attn_bwd(z, l, last, inputs, firsts, olds):
+def attn_bwd(z, l, last, blocks, inputs, firsts, olds):
     first = l == 0
     rq = z.queries if last else z.rows
     big = lambda t=F32: pltpu.VMEM((z.d, z.d), t)
@@ -681,16 +692,15 @@
     scratch += [pltpu.VMEM((rq, 256), F32), pltpu.VMEM((rq, 128), F32), pltpu.VMEM((z.queries, z.context), F32)]
     scratch += [tall(BF16), tall(BF16), pltpu.VMEM((rq, 256), F32)]
     scratch += [pltpu.VMEM((z.context, 256), F32), pltpu.VMEM((z.context, 256), F32), big(), pltpu.VMEM((8, z.d), F32)]
-    specs = [VMEM] + [ANY] * 14
+    specs = [VMEM] + [ANY] * (12 + blocks)
     h = z.d // 2
     outs = [(8, z.d), (h, z.d), (h, z.d)]
     inputs = list(inputs)
     if first:
         inputs += list(firsts)
-        specs += [SMEM, VMEM, ANY]
-        scratch += [pltpu.VMEM((z.rows, z.feats), F32), pltpu.VMEM((z.d, z.feats), F32)]
-        outs += [(z.d, z.feats)]
-        grads = [1, 2, 3]
+        specs += [SMEM]
+        outs = [(rq, z.d), (rq, 256), (z.context, 384)] + outs
+        grads = [4, 5]
     else:
         outs = [(rq, z.d), (z.half, z.d), (z.half // 2, z.d), (z.half // 2, z.d)] + outs
         grads = [5, 6]
@@ -700,15 +710,80 @@
         inputs += list(olds)
         specs += [ANY] * len(olds)
     return run(
-        functools.partial(attn_bwd_kernel, z, l, first, last, olds is not None),
+        functools.partial(attn_bwd_kernel, z, l, first, last, olds is not None, blocks),
         f"attn_bwd{l}",
         inputs,
         specs,
         outs,
         scratch,
-        32,
+        48,
         3 * 2 * (4 * rq * z.d * 256 + 2 * z.context * z.d * 384 + 15 * rq * z.context * 256),
         24 << 20,
+        aliases,
+    )
+
+
+def embed_bwd_kernel(z, accumulate, blocks, *refs):
+    (c_ref, t_in, vec, feat, x_in, dy, dq, dkv, *weights) = refs[: 8 + blocks]
+    refs = refs[8 + blocks :]
+    if accumulate:
+        old, refs = refs[0], refs[1:]
+    gv, emb_out = refs[:2]
+    (xb, dyb, dqb, kvb, wb, wh, wl, featb, geb, gvb, sems) = refs[2:]
+    copies = Copies(sems)
+    cw = load_weight(copies, weights, wb, c_ref)
+    cd = [copies.start(dq, dqb), copies.start(dkv, kvb)]
+    cx = [copies.start(x_in, xb), copies.start(dy, dyb)]
+    cx += load_feats(copies, z, c_ref, feat, featb)
+    if accumulate:
+        co = copies.start(old, geb)
+    gvb[...] = jnp.zeros_like(gvb)
+    copies.wait(*cw)
+    split_into(wh, wl, wb[...])
+    copies.wait(*cd)
+    copies.wait(*cx)
+    gain = row(vec, 0)
+    ge = 0.0
+    for i in range(2):
+        here = pl.ds(i * z.half, z.half)
+        nh, rstd = norm_stats(xb[here, :])
+        dn_q = mm(split(dqb[here, :]), (wh[:, z.q], wl[:, z.q]), 1, 1)
+        dn_c = mm(split(kvb[pl.ds(i * z.hc, z.hc), :]), (wh[:, z.kv], wl[:, z.kv]), 1, 1)
+        dn = jnp.concatenate([dn_q[: z.hc] + dn_c, dn_q[z.hc :]], axis=0)
+        gvb[pl.ds(0, 1), :] += jnp.sum(dn * nh, axis=0, keepdims=True)
+        dx = z.share * dyb[here, :] + norm_back(dn * gain, nh, rstd)
+        gvb[pl.ds(2 * z.depth + 1, 1), :] += jnp.sum(dx * t_in[here, :], axis=0, keepdims=True)
+        ge = ge + mm(split(dx), split(featb[here, :]), 0, 0)
+    copies.start(gvb, gv)
+    if accumulate:
+        copies.wait(co)
+        ge = geb[...] + ge
+    geb[...] = ge
+    copies.start(geb, emb_out)
+    copies.wait_all()
+
+
+def embed_bwd(z, blocks, inputs, old):
+    big = lambda t=F32: pltpu.VMEM((z.d, z.d), t)
+    scratch = [pltpu.VMEM((z.rows, z.d), F32), pltpu.VMEM((z.rows, z.d), F32), pltpu.VMEM((z.rows, 256), F32)]
+    scratch += [pltpu.VMEM((z.context, 384), F32), big(), big(BF16), big(BF16)]
+    scratch += [pltpu.VMEM((z.rows, z.feats), F32), pltpu.VMEM((z.d, z.feats), F32), pltpu.VMEM((8, z.d), F32)]
+    specs = [SMEM, VMEM, VMEM] + [ANY] * (5 + blocks)
+    aliases = None
+    if old is not None:
+        aliases = {len(inputs): 1}
+        inputs = list(inputs) + [old]
+        specs = specs + [ANY]
+    return run(
+        functools.partial(embed_bwd_kernel, z, old is not None, blocks),
+        "embed_bwd",
+        inputs,
+        specs,
+        [(8, z.d), (z.d, z.feats)],
+        scratch,
+        48,
+        3 * 2 * (z.rows * z.d * 256 + z.context * z.d * 384 + z.rows * z.d * z.feats),
+        12 << 20,
         aliases,
     )
 
@@ -779,9 +854,26 @@
     share = 1.0 / (lax.axis_size("hh") * lax.axis_size("hl"))
     z = Sizes(d, context, queries, depth, width, feats, share)
     c = lax.axis_index("hl")
-    c_arr = jnp.full((1,), c, jnp.int32)
-
-    near, far = gather_rows(jnp.concatenate([emb_weight, vectors], axis=1))
+    c_arr = jnp.stack([c, lax.axis_index("dh")]).astype(jnp.int32)
+
+    zi = lax.axis_index("dh")
+    line = lax.axis_size("dh")
+    near_by = line == 4
+
+    def hop(value, step):
+        return lax.ppermute(value, "dh", [(i, i ^ step) for i in range(line)])
+
+    own_rows = jnp.concatenate([emb_weight, vectors], axis=1)
+    if near_by:
+        b0, b1, b2, b3 = [own_rows] + [hop(own_rows, m) for m in (1, 2, 3)]
+        odd, high = jnp.bitwise_and(zi, 1) == 1, zi >= 2
+        b0, b1 = jnp.where(odd, b1, b0), jnp.where(odd, b0, b1)
+        b2, b3 = jnp.where(odd, b3, b2), jnp.where(odd, b2, b3)
+        near = [jnp.where(high, b2, b0), jnp.where(high, b3, b1), jnp.where(high, b0, b2), jnp.where(high, b1, b3)]
+        near = jnp.concatenate(near, axis=0)
+        far = swap(near, "dl")
+    else:
+        near, far = gather_rows(own_rows)
     small = jnp.concatenate([near, far], axis=0)
     emb = small[:, :feats]
     vec = jnp.pad(small[:, feats:].T, ((0, 1), (0, 0)))
@@ -802,7 +894,7 @@
         mask = neighbour_mask(roll_half(neighbours[m, 0], c), roll_half(nbr_mask[m, 0], c), context, c)
         tables.append(dict(feat=features[m, 0], t_in=t_in, side=jnp.stack([flag, t_qry], axis=1), mask=mask))
 
-    held = [vec]
+    held, pending = [vec], []
 
     def beside(kernel, *transfers, ahead=(), strict=False):
         gate = after(held[0], *ahead)
@@ -810,6 +902,9 @@
         outs = list(kernel(gate))
         moved = [after(x, outs[0]) for x in moved]
         held[0] = after(vec, *moved)
+        for pieces in pending:
+            pieces.append(swap(after(pieces[1], outs[0]), "hl"))
+        pending.clear()
         if strict:
             outs[-1] = after(outs[-1], *moved)
         return (outs, *moved)
@@ -817,6 +912,7 @@
     def sent(pieces):
         held[0] = after(held[0], pieces[0])
         came[0] = pieces[1]
+        pending.append(pieces)
         return pieces
 
     came = [None]
@@ -832,7 +928,10 @@
         return lambda: swap(near[i][part * half : (part + 1) * half], "dl")
 
     def both(i):
-        return near[i], far[i]
+        return near[i] if isinstance(near[i], tuple) else (near[i], far[i])
+
+    def held_blocks(*indices):
+        return tuple(len(both(i)) for i in indices)
 
     saved = [[None] * depth for _ in range(micros)]
     state = [None] * micros
@@ -842,37 +941,40 @@
 
         def call(gate):
             if l == 0:
-                inputs = (c_arr, t["t_in"], gate, t["feat"], emb, *both(3 * l), t["mask"])
+                inputs = (c_arr, t["t_in"], gate, t["feat"], emb, *both(0), t["mask"])
             else:
-                inputs = (gate, *state[m], *both(3 * l), t["mask"])
-            return attn_fwd(z, l, last, inputs)
+                inputs = (gate, state[m][0], *state[m][1], *both(3 * l), t["mask"])
+            return attn_fwd(z, l, last, *held_blocks(3 * l), inputs)
 
         (x, q, kv, o, lse, mine, *theirs), *moved = beside(call, *transfers, ahead=ahead, strict=strict)
         saved[m][l] = dict(x=x, q=q, kv=kv, o=o, lse=lse)
-        state[m] = (x, *sent(head_sum(mine, theirs, came[0])))
+        state[m] = (x, sent(head_sum(mine, theirs, came[0])))
         return moved
 
-    def ffn_forward(l, m, *transfers, ahead=()):
+    def ffn_forward(l, m, *transfers, ahead=(), strict=False):
         def call(gate):
-            return ffn_fwd(z, l, l == depth - 1, (gate, *state[m], *both(3 * l + 1), *both(3 * l + 2)))
-
-        (x1, u, mine, *theirs), *moved = beside(call, *transfers, ahead=ahead)
+            inputs = (gate, state[m][0], *state[m][1], *both(3 * l + 1), *both(3 * l + 2))
+            return ffn_fwd(z, l, l == depth - 1, held_blocks(3 * l + 1, 3 * l + 2), inputs)
+
+        (x1, u, mine, *theirs), *moved = beside(call, *transfers, ahead=ahead, strict=strict)
         saved[m][l].update(x1=x1, u=u)
-        state[m] = (x1, *sent(head_sum(mine, theirs, came[0])))
+        state[m] = (x1, sent(head_sum(mine, theirs, came[0])))
         return moved
 
-    near[0] = rows_near(blocks[0])
-    far[0] = swap(near[0], "dl")
+    if near_by:
+        first = [blocks[0]] + [hop(blocks[0], m) for m in (1, 2, 3)]
+        near[0] = tuple(first + [swap(block, "dl") for block in first])
+        near[2] = (rows_near(jnp.concatenate([blocks[2], swap(blocks[2], "dl")], axis=0)),)
+    else:
+        near[0] = gather_rows(blocks[0])
+        near[2] = gather_rows(blocks[2])
     near[1] = rows_near(blocks[1])
-    far[1], near[2] = attn_forward(0, 0, cross(1), gather(2), ahead=(near[1],))
-    near[3] = rows_near(blocks[3])
-    (far[2],) = attn_forward(0, 1, cross(2), strict=True)
-    (near[4],) = ffn_forward(0, 0, gather(4))
-    far[3], near[5] = ffn_forward(0, 1, cross(3), gather(5))
-    far[4] = swap(near[4], "dl")
-    (top,) = attn_forward(1, 0, cross(5, 0))
-    (low,) = attn_forward(1, 1, cross(5, 1))
-    far[5] = jnp.concatenate([top, low], axis=0)
+    attn_forward(0, 0, ahead=(near[1],))
+    (far[1],) = attn_forward(0, 1, cross(1), strict=True)
+    (near[3],) = ffn_forward(0, 0, gather(3))
+    far[3], near[4] = ffn_forward(0, 1, cross(3), gather(4))
+    far[4], near[5] = attn_forward(1, 0, cross(4), gather(5))
+    (far[5],) = attn_forward(1, 1, cross(5), strict=True)
     ffn_forward(1, 0)
     ffn_forward(1, 1)
 
@@ -886,11 +988,11 @@
         def call(gate):
             weights = (k["u"], *both(3 * l + 1), *both(3 * l + 2))
             if last:
-                inputs = (gate, tables[m]["side"], k["x1"], *state[m][1:], *weights)
+                inputs = (gate, tables[m]["side"], k["x1"], *state[m][1], *weights)
             else:
                 res, pieces = cot[m]
                 inputs = (gate, res, saved[m][l + 1]["x"], k["x1"], *pieces, *weights)
-            return ffn_bwd(z, l, last, inputs, g_ffn[l])
+            return ffn_bwd(z, l, last, held_blocks(3 * l + 1, 3 * l + 2), inputs, g_ffn[l])
 
         (dy, mine, t0, t1, gv, *g_ffn[l]), *moved = beside(call, *transfers)
         g_vecs.append(gv)
@@ -903,12 +1005,13 @@
         def call(gate):
             dy, pieces = cot[m]
             inputs = (gate, dy, k["x1"], *pieces, *both(3 * l), k["x"], k["q"], k["kv"], k["o"], k["lse"], t["mask"])
-            firsts = (c_arr, t["t_in"], t["feat"]) if l == 0 else ()
-            return attn_bwd(z, l, last, inputs, firsts, g_attn[l])
+            firsts = (c_arr,) if l == 0 else ()
+            return attn_bwd(z, l, last, *held_blocks(3 * l), inputs, firsts, g_attn[l])
 
         outs, *moved = beside(call, *transfers)
         if l == 0:
-            gv, *g_attn[l] = outs
+            *cot[m], gv, g_near, g_far = outs
+            g_attn[l] = [g_near, g_far]
         else:
             dy, mine, t0, t1, gv, *g_attn[l] = outs
             cot[m] = (dy, sent(head_sum(mine, (t0, t1), came[0])))
@@ -933,15 +1036,31 @@
     got, own_down1 = ffn_backward(0, 1, cross_far(packed1), reduce(own_down1))
     own_packed1 = packed1[0] + got
     up0, down0 = g_ffn[0][:2], g_ffn[0][2:]
-    own_up0 = near_rows(*up0)
-    held[0] = after(held[0], own_up0)
-    got, own_up0, own_packed1 = attn_backward(0, 0, cross_far(down0), reduce(own_up0), reduce(own_packed1))
+    got, own_packed1 = attn_backward(0, 0, cross_far(up0), reduce(own_packed1))
+    own_up0 = up0[0] + got
+    got, own_up0 = attn_backward(0, 1, cross_far(down0), reduce(own_up0))
     own_down0 = down0[0] + got
-    (own_down0,) = attn_backward(0, 1, reduce(own_down0))
-    packed0 = g_attn[0][:2]
-    own_packed0 = near_rows(packed0[0], after(packed0[1], own_down0))
-    crossed = own_packed0
-    own_packed0 = scatter_near(own_packed0)
+
+    g_emb = [None]
+
+    def embed_backward(m, *transfers):
+        t = tables[m]
+
+        def call(gate):
+            inputs = (c_arr, t["t_in"], gate, t["feat"], saved[m][0]["x"], *cot[m], *both(0))
+            return embed_bwd(z, *held_blocks(0), inputs, g_emb[0])
+
+        (gv, g_emb[0]), *moved = beside(call, *transfers)
+        g_vecs.append(gv)
+        return moved
+
+    packed0 = g_attn[0]
+    got = swap(after(packed0[1], own_down0), "dl")
+    own_down0 = scatter_near(own_down0)
+    embed_backward(0)
+    embed_backward(1)
+    own_down0 = after(own_down0, g_vecs[-1])
+    own_packed0 = scatter_near(packed0[0] + after(got, g_vecs[-1]))
     own = [[own_packed0, own_packed1], [own_up0, own_up1], [own_down0, own_down1]]
 
     owned = [
@@ -950,20 +1069,26 @@
         jnp.stack(own[1]),
         jnp.stack(own[2]),
     ]
+    n_vec = vectors.shape[1]
     g_vec = sum(g_vecs[1:], g_vecs[0])
-    n_vec = vectors.shape[1]
-    loss_local = g_vec[n_vec, 0]
-    g_small = jnp.concatenate([g_attn[0][2], g_vec[:n_vec].T], axis=1)
-    own_small = scatter_near(near_rows(g_small[: d // 2], g_small[d // 2 :]))
+    loss_local = share * g_vec[n_vec, 0]
+    g_small = jnp.concatenate([g_emb[0], g_vec[:n_vec].T], axis=1)
+    own_small = near_rows(g_small[: d // 2], g_small[d // 2 :])
+    if near_by:
+        piece = lambda m: lax.dynamic_slice_in_dim(own_small, jnp.bitwise_xor(zi, m) * d_rows, d_rows, axis=0)
+        own_small = (piece(0) + hop(piece(1), 1)) + (hop(piece(2), 2) + hop(piece(3), 3))
+    else:
+        own_small = scatter_near(own_small)
     own_small = own_small + swap(own_small, "hl")
     own_small = own_small + swap(own_small, "hh")
-    owned += [own_small[:, :feats], own_small[:, feats:]]
+    own_emb, own_vec = own_small[:, :feats], own_small[:, feats:]
+    owned += [own_emb, own_vec]
 
     squares = share * jnp.sum(own_small * own_small)
     for o in owned[:4]:
         squares = squares + jnp.sum(o * o)
     counted = share * jnp.sum(flags.astype(F32))
-    sums = everyone_sum(jnp.stack([squares, share * loss_local, counted]))
+    sums = everyone_sum(jnp.stack([squares, loss_local, counted]))
     counted = jnp.maximum(sums[2], 1.0)
     loss = sums[1] / counted
     grad_norm = jnp.sqrt(sums[0]) / counted

time: 756 us -> 643 us (0.85)
  waiting for transfers between devices: 287 us -> 162 us
  starting transfers between devices: 55.8 us -> 75.2 us
  blocking collectives: 16.3 us -> 0 us
  Pallas kernels: 268 us -> 280 us
    ppermute x90 -> x92, waiting for transfers between devices: 200 us -> 128 us  [swap(): return lax.ppermute(values, axis, SWAP)]
    all_gather x6 -> x5, waiting for transfers between devices: 43.8 us -> 0.04 us  [rows_near(): return lax.all_gather(block, 'dh', axis=0, tiled=True)]
    reduce_scatter x7 -> x6, waiting for transfers between devices: 37.3 us -> 0.03 us  [scatter_near(): return lax.psum_scatter(near, 'dh', scatter_dimension=0, tiled=True)]
    ppermute x0 -> x9, waiting for transfers between devices: none -> 30.5 us  [hop(): return lax.ppermute(value, 'dh', [(i, i ^ step) for i in range(line)])]
    all_gather x1 -> x0, blocking collectives: 16.3 us -> none  [gather_rows(): near = lax.all_gather(block, 'dh', axis=0, tiled=True)]
    ppermute x0 -> x9, starting transfers between devices: none -> 14.8 us  [hop(): return lax.ppermute(value, 'dh', [(i, i ^ step) for i in range(line)])]
    pallas_call x16 -> x18, Pallas kernels: 268 us -> 280 us  [run(): pl.pallas_call(kernel, name=name, out_shape=[jax.ShapeDtypeStruct(s, F32)...]
    unnamed x220 -> x235, local copies, waits for them, and re-layouts: 21.7 us -> 17.8 us
  transfers between devices with their start and end apart: 105 -> 114, of which waited for: 44 -> 48; matrix products, arithmetic and copies ran while one was open for 7% -> 10% of each run, Pallas kernels for 36% -> 44%
where the time goes in v3:
time: 643 us; the launch traced here: 635 us
  Pallas kernels  280 us (44%)
  waiting for transfers between devices  162 us (25%)
  starting transfers between devices  75.2 us (12%)
  other arithmetic  58.7 us (9%)
  local copies, waits for them, and re-layouts  33.2 us (5%)
  between operations  25.7 us (4%)
    pallas_call x18, Pallas kernels, run(): pl.pallas_call(kernel, name=name, out_shape=[jax.ShapeDtypeStruct(s, F32)...  280 us
    ppermute x92, waiting for transfers between devices, swap(): return lax.ppermute(values, axis, SWAP)  128 us
    ppermute x92, starting transfers between devices, swap(): return lax.ppermute(values, axis, SWAP)  50.6 us
    ppermute x9, waiting for transfers between devices, hop(): return lax.ppermute(value, 'dh', [(i, i ^ step) for i in range(line)])  30.5 us
    add x14, other arithmetic, head_sum(): a = mine + jnp.concatenate([after(first, before), second], axis=0)  18.5 us
    unnamed x235, local copies, waits for them, and re-layouts  17.8 us
    ppermute x9, starting transfers between devices, hop(): return lax.ppermute(value, 'dh', [(i, i ^ step) for i in range(line)])  14.8 us
  transfers between devices with their start and end apart: 114, of which 48 were waited for; matrix products, arithmetic and copies ran while one was open for 10% of the time, Pallas kernels for 44%

profile of v3, /device:TPU:0, one launch (start us, length us, event | category | flops | bytes accessed | tf_op | source)
XLA Modules:
  0.0 634.5 jit_solution(18364094275287672659)
XLA Ops:
  25.3 8.7 %select_reduce_fusion = (s32[256,16]{1,0:T(8,128)S(1)}, s32[256,16]{1,0:T(8,128)S(1)}) fusion(s32[256,256]{1,0:T(8,128)S(1)} %get-tuple-element.524, s32[256,256]{1,0:T(8,128)S(1)} %broadcast_shift-right-arithmetic_fusion, s32[256,256]{1,0:T(8,128)S(1)} %get-tuple-element.525, s32[256,256]{1,0:T(8,128)S(1)} %get-tuple-element.526), kind=kLoop, calls=%fused_computation | loop fusion | flops 6283264 | bytes 1081344 | tf_op jit(solution)/shard_map/reduce_sum | solution.py:807
  45.5 10.3 %collective-permute-done.4.refs_6_.refs_8_.refs_9_ = f32[96,768]{1,0:T(8,128)S(1)} collective-permute-done((f32[96,768]{1,0:T(8,128)S(1)}, f32[96,768]{1,0:T(8,128)S(1)}, u32[]{:S(2)}, u32[]{:S(2)}) %collective-permute-start.4) | collective-permute-done | bytes 294944 | tf_op jit(solution)/shard_map/ppermute | solution.py:864
  57.1 8.8 %collective-permute-done.5.refs_7_.refs_9_.refs_10_ = f32[96,768]{1,0:T(8,128)S(1)} collective-permute-done((f32[96,768]{1,0:T(8,128)S(1)}, f32[96,768]{1,0:T(8,128)S(1)}, u32[]{:S(2)}, u32[]{:S(2)}) %collective-permute-start.5) | collective-permute-done | bytes 294944 | tf_op jit(solution)/shard_map/ppermute | solution.py:864
  74.9 14.9 %attn_fwd0.2 = (f32[768,768]{1,0:T(8,128)}, f32[768,256]{1,0:T(8,128)}, f32[512,384]{1,0:T(8,128)}, f32[768,256]{1,0:T(8,128)}, f32[768,128]{1,0:T(8,128)}, /*in...) custom-call(s32[2]{0:T(128)} %pad_add_fusion.refs_0_.refs_21_, f32[768,1]{1,0:T(8,128)} %broadcast_in_dim.59.refs_1_, ...), custom_call_target="tpu_custom_call" | custom-call | flops 317089376 | bytes 838860 | tf_op jit(solution)/shard_map/attn_fwd0/pallas_call | solution.py:170
  98.1 14.8 %attn_fwd0.3 = (f32[768,768]{1,0:T(8,128)}, f32[768,256]{1,0:T(8,128)}, f32[512,384]{1,0:T(8,128)}, f32[768,256]{1,0:T(8,128)}, f32[768,128]{1,0:T(8,128)}, /*in...) custom-call(s32[2]{0:T(128)} %pad_add_fusion.refs_0_.refs_21_, f32[768,1]{1,0:T(8,128)} %broadcast_in_dim.58.refs_1_, ...), custom_call_target="tpu_custom_call" | custom-call | flops 317089376 | bytes 838860 | tf_op jit(solution)/shard_map/attn_fwd0/pallas_call | solution.py:170
  126.2 15.4 %ffn_fwd0.2 = (f32[768,768]{1,0:T(8,128)}, f32[768,768]{1,0:T(8,128)}, f32[384,768]{1,0:T(8,128)}, f32[192,768]{1,0:T(8,128)}, f32[192,768]{1,0:T(8,128)}) custom-call(f32[8,768]{1,0:T(8,128)} %pad.8.refs_2_.refs_0_, f32[768,768]{1,0:T(8,128)} %get-tuple-element.226.refs_1_.refs_15_.refs_4_, f32[384,768]{1,0:T(8,128)} %copy-done.16, ...), custom_call_target="tpu_custom_call" | custom-call | flops 271790912 | bytes 1258291 | tf_op jit(solution)/shard_map/ffn_fwd0/pallas_call | solution.py:170
  142.4 10.2 %collective-permute-done.22.refs_3_ = f32[384,768]{1,0:T(8,128)} collective-permute-done((f32[384,768]{1,0:T(8,128)S(1)}, f32[384,768]{1,0:T(8,128)}, u32[]{:S(2)}, u32[]{:S(2)}) %collective-permute-start.22) | collective-permute-done | bytes 1179680 | tf_op jit(solution)/shard_map/ppermute | solution.py:27
  157.6 15.6 %ffn_fwd0.3 = (f32[768,768]{1,0:T(8,128)}, f32[768,768]{1,0:T(8,128)}, f32[384,768]{1,0:T(8,128)}, f32[192,768]{1,0:T(8,128)}, f32[192,768]{1,0:T(8,128)}) custom-call(f32[8,768]{1,0:T(8,128)} %pad.8.refs_2_.refs_0_, f32[768,768]{1,0:T(8,128)} %get-tuple-element.217.refs_1_.refs_15_.refs_4_, f32[384,768]{1,0:T(8,128)} %copy-done.20, ...), custom_call_target="tpu_custom_call" | custom-call | flops 271790912 | bytes 1258291 | tf_op jit(solution)/shard_map/ffn_fwd0/pallas_call | solution.py:170
  175.4 8.4 %collective-permute-done.27.refs_3_ = f32[384,768]{1,0:T(8,128)} collective-permute-done((f32[384,768]{1,0:T(8,128)}, f32[384,768]{1,0:T(8,128)}, u32[]{:S(2)}, u32[]{:S(2)}) %collective-permute-start.27) | collective-permute-done | bytes 1179680 | tf_op jit(solution)/shard_map/ppermute | solution.py:27
  187.7 14.3 %collective-permute-done.20.refs_7_.refs_8_ = f32[384,768]{1,0:T(8,128)S(1)} collective-permute-done((f32[384,768]{1,0:T(8,128)S(1)}, f32[384,768]{1,0:T(8,128)S(1)}, u32[]{:S(2)}, u32[]{:S(2)}) %collective-permute-start.20) | collective-permute-done | bytes 1179680 | tf_op jit(solution)/shard_map/ppermute | solution.py:27
  203.5 10.8 %attn_fwd1.2 = (f32[768,768]{1,0:T(8,128)}, f32[256,256]{1,0:T(8,128)}, f32[512,384]{1,0:T(8,128)}, f32[256,256]{1,0:T(8,128)}, f32[256,128]{1,0:T(8,128)}, /*in...) custom-call(f32[8,768]{1,0:T(8,128)} %pad.8.refs_2_.refs_0_, ...), custom_call_target="tpu_custom_call" | custom-call | flops 135895456 | bytes 838860 | tf_op jit(solution)/shard_map/attn_fwd1/pallas_call | solution.py:170
  222.4 8.7 %collective-permute-done.32.refs_7_.refs_9_ = f32[384,768]{1,0:T(8,128)S(1)} collective-permute-done((f32[384,768]{1,0:T(8,128)}, f32[384,768]{1,0:T(8,128)S(1)}, u32[]{:S(2)}, u32[]{:S(2)}) %collective-permute-start.32) | collective-permute-done | bytes 1179680 | tf_op jit(solution)/shard_map/ppermute | solution.py:27
  232.2 10.9 %attn_fwd1.3 = (f32[768,768]{1,0:T(8,128)}, f32[256,256]{1,0:T(8,128)}, f32[512,384]{1,0:T(8,128)}, f32[256,256]{1,0:T(8,128)}, f32[256,128]{1,0:T(8,128)}, /*in...) custom-call(f32[8,768]{1,0:T(8,128)} %pad.8.refs_2_.refs_0_, ...), custom_call_target="tpu_custom_call" | custom-call | flops 135895456 | bytes 838860 | tf_op jit(solution)/shard_map/attn_fwd1/pallas_call | solution.py:170
  243.2 11.7 %collective-permute-done.31.refs_9_.refs_11_ = f32[384,768]{1,0:T(8,128)S(1)} collective-permute-done((f32[384,768]{1,0:T(8,128)}, f32[384,768]{1,0:T(8,128)S(1)}, u32[]{:S(2)}, u32[]{:S(2)}) %collective-permute-start.31) | collective-permute-done | bytes 1179680 | tf_op jit(solution)/shard_map/ppermute | solution.py:27
  259.8 9.7 %ffn_fwd1.2 = (f32[256,768]{1,0:T(8,128)}, f32[256,768]{1,0:T(8,128)}, f32[128,768]{1,0:T(8,128)}, f32[64,768]{1,0:T(8,128)}, f32[64,768]{1,0:T(8,128)}) custom-call(f32[8,768]{1,0:T(8,128)} %pad.8.refs_2_.refs_0_, f32[768,768]{1,0:T(8,128)} %get-tuple-element.247.refs_1_.refs_9_.refs_2_, f32[128,768]{1,0:T(8,128)} %copy-done.38, f32[128,768]{1,0:T(8,128)} %copy-done.72, ...), custom_call_target="tpu_custom_call" | custom-call | flops 90596968 | bytes 1258291 | tf_op jit(solution)/shard_map/ffn_fwd1/pallas_call | solution.py:170
  275.6 9.3 %ffn_fwd1.3 = (f32[256,768]{1,0:T(8,128)}, f32[256,768]{1,0:T(8,128)}, f32[128,768]{1,0:T(8,128)}, f32[64,768]{1,0:T(8,128)}, f32[64,768]{1,0:T(8,128)}) custom-call(f32[8,768]{1,0:T(8,128)} %pad.8.refs_2_.refs_0_, f32[768,768]{1,0:T(8,128)} %get-tuple-element.257.refs_1_.refs_9_.refs_2_, f32[128,768]{1,0:T(8,128)} %copy-done.37, f32[128,768]{1,0:T(8,128)} %copy-done.71, ...), custom_call_target="tpu_custom_call" | custom-call | flops 90596968 | bytes 1258291 | tf_op jit(solution)/shard_map/ffn_fwd1/pallas_call | solution.py:170
  290.3 11.1 %ffn_bwd1.2 = (f32[256,768]{1,0:T(8,128)}, f32[128,768]{1,0:T(8,128)}, f32[64,768]{1,0:T(8,128)}, f32[64,768]{1,0:T(8,128)}, f32[8,768]{1,0:T(8,128)}, /*index=5...) custom-call(f32[8,768]{1,0:T(8,128)} %pad.8.refs_2_.refs_0_, ...), custom_call_target="tpu_custom_call" | custom-call | flops 181193936 | bytes 1677721 | tf_op jit(solution)/shard_map/ffn_bwd1/pallas_call | solution.py:170
  307.7 12.5 %ffn_bwd1.3 = (f32[256,768]{1,0:T(8,128)}, f32[128,768]{1,0:T(8,128)}, f32[64,768]{1,0:T(8,128)}, f32[64,768]{1,0:T(8,128)}, f32[8,768]{1,0:T(8,128)}, /*index=5...) custom-call(f32[8,768]{1,0:T(8,128)} %pad.8.refs_2_.refs_0_, ...), custom_call_target="tpu_custom_call", output_to_operand_aliasing={{5}: (12, {}), {6}: (13, {}), {7}: (14, {}), {8}: (15, {})} | custom-call | flops 181193936 | bytes 1677721 | tf_op jit(solution)/shard_map/ffn_bwd1/pallas_call | solution.py:170
  326.3 15.7 %attn_bwd1.2 = (f32[256,768]{1,0:T(8,128)}, f32[384,768]{1,0:T(8,128)}, f32[192,768]{1,0:T(8,128)}, f32[192,768]{1,0:T(8,128)}, f32[8,768]{1,0:T(8,128)}, /*index=5*/f32[384,768]{1,0:T(8,128)}, f32[384,768]{1,0:T(8,128)}) custom-call(f32[8,768]{1,0:T(8,128)} %pad.8.refs_2_.refs_0_, f32[256,768]{1,0:T(8,128)} %get-tuple-element.287.refs_1_, ...), custom_call_target="tpu_custom_call" | custom-call | flops 301989888 | bytes 1258291 | tf_op jit(solution)/shard_map/attn_bwd1/pallas_call | solution.py:170
  349.8 16.4 %attn_bwd1.3 = (f32[256,768]{1,0:T(8,128)}, f32[384,768]{1,0:T(8,128)}, f32[192,768]{1,0:T(8,128)}, f32[192,768]{1,0:T(8,128)}, f32[8,768]{1,0:T(8,128)}, /*index=5*/f32[384,768]{1,0:T(8,128)}, f32[384,768]{1,0:T(8,128)}) custom-call(f32[8,768]{1,0:T(8,128)} %pad.8.refs_2_.refs_0_, ...), custom_call_target="tpu_custom_call", output_to_operand_aliasing={{5}: (15, {}), {6}: (16, {})} | custom-call | flops 301989888 | bytes 1258291 | tf_op jit(solution)/shard_map/attn_bwd1/pallas_call | solution.py:170
  367.6 8.0 %collective-permute-done.71.refs_5_ = f32[384,768]{1,0:T(8,128)} collective-permute-done((f32[384,768]{1,0:T(8,128)S(1)}, f32[384,768]{1,0:T(8,128)}, u32[]{:S(2)}, u32[]{:S(2)}) %collective-permute-start.71) | collective-permute-done | bytes 1179680 | tf_op jit(solution)/shard_map/ppermute | solution.py:27
  383.2 22.2 %ffn_bwd0.2 = (f32[768,768]{1,0:T(8,128)}, f32[384,768]{1,0:T(8,128)}, f32[192,768]{1,0:T(8,128)}, f32[192,768]{1,0:T(8,128)}, f32[8,768]{1,0:T(8,128)}, /*index...) custom-call(f32[8,768]{1,0:T(8,128)} %pad.8.refs_2_.refs_0_, ...), custom_call_target="tpu_custom_call" | custom-call | flops 543581824 | bytes 1677721 | tf_op jit(solution)/shard_map/ffn_bwd0/pallas_call | solution.py:170
  415.9 23.9 %ffn_bwd0.3 = (f32[768,768]{1,0:T(8,128)}, f32[384,768]{1,0:T(8,128)}, f32[192,768]{1,0:T(8,128)}, f32[192,768]{1,0:T(8,128)}, f32[8,768]{1,0:T(8,128)}, /*index...) custom-call(f32[8,768]{1,0:T(8,128)} %pad.8.refs_2_.refs_0_, ...), custom_call_target="tpu_custom_call", output_to_operand_aliasing={{5}: (12, {}), {6}: (13, {}), {7}: (14, {}), {8}: (15, {})} | custom-call | flops 543581824 | bytes 1677721 | tf_op jit(solution)/shard_map/ffn_bwd0/pallas_call | solution.py:170
  451.0 27.3 %attn_bwd0.2 = (f32[768,768]{1,0:T(8,128)}, f32[768,256]{1,0:T(8,128)}, f32[512,384]{1,0:T(8,128)}, f32[8,768]{1,0:T(8,128)}, f32[384,768]{1,0:T(8,128)}, /*index=5*/f32[384,768]{1,0:T(8,128)}) custom-call(f32[8,768]{1,0:T(8,128)} %pad.8.refs_2_.refs_0_, f32[768,768]{1,0:T(8,128)} %get-tuple-element.331.refs_1_, ...), custom_call_target="tpu_custom_call" | custom-call | flops 724775744 | bytes 1258291 | tf_op jit(solution)/shard_map/attn_bwd0/pallas_call | solution.py:170
  485.8 27.5 %attn_bwd0.3 = (f32[768,768]{1,0:T(8,128)}, f32[768,256]{1,0:T(8,128)}, f32[512,384]{1,0:T(8,128)}, f32[8,768]{1,0:T(8,128)}, f32[384,768]{1,0:T(8,128)}, /*index=5*/f32[384,768]{1,0:T(8,128)}) custom-call(f32[8,768]{1,0:T(8,128)} %pad.8.refs_2_.refs_0_, f32[768,768]{1,0:T(8,128)} %get-tuple-element.349.refs_1_, ...), custom_call_target="tpu_custom_call", output_to_operand_aliasing={{4}: (22, {}), {5}: (23, {})} | custom-call | flops 724775744 | bytes 1258291 | tf_op jit(solution)/shard_map/attn_bwd0/pallas_call | solution.py:170
  517.7 10.9 %embed_bwd.2 = (f32[8,768]{1,0:T(8,128)}, f32[768,128]{1,0:T(8,128)}) custom-call(s32[2]{0:T(128)} %pad_add_fusion.refs_0_.refs_21_, f32[768,1]{1,0:T(8,128)} %broadcast_in_dim.59.refs_1_, f32[8,768]{1,0:T(8,128)} %pad.8.refs_2_.refs_0_, f32[768,128]{1,0:T(8,128)} %get-tuple-element.527.refs_3_, f32[768,768]{1,0:T(8,128)} %get-tuple-element.226.refs_1_.refs_15_.refs_4_, ...), custom_call_target="tpu_custom_call" | custom-call | flops 113246208 | bytes 629145 | tf_op jit(solution)/shard_map/embed_bwd/pallas_call | solution.py:170
  528.7 10.8 %embed_bwd.3 = (f32[8,768]{1,0:T(8,128)}, f32[768,128]{1,0:T(8,128)}) custom-call(s32[2]{0:T(128)} %pad_add_fusion.refs_0_.refs_21_, f32[768,1]{1,0:T(8,128)} %broadcast_in_dim.58.refs_1_, f32[8,768]{1,0:T(8,128)} %pad.8.refs_2_.refs_0_, f32[768,128]{1,0:T(8,128)} %get-tuple-element.528.refs_3_, ...), custom_call_target="tpu_custom_call", output_to_operand_aliasing={{1}: (16, {})} | custom-call | flops 113246208 | bytes 629145 | tf_op jit(solution)/shard_map/embed_bwd/pallas_call | solution.py:170
  539.5 5.6 collective-permute-done.97
  548.2 9.7 %collective-permute-done.91 = f32[384,135]{1,0:T(8,128)S(1)} collective-permute-done((f32[384,135]{1,0:T(8,128)S(1)}, f32[384,135]{1,0:T(8,128)S(1)}, u32[]{:S(2)}, u32[]{:S(2)}) %collective-permute-start.91) | collective-permute-done | bytes 207392 | tf_op jit(solution)/shard_map/ppermute | solution.py:27
  563.7 5.5 collective-permute-done.92
  569.2 5.8 collective-permute-done.93
  599.3 6.6 %collective-permute-start.101 = (f32[8,128]{1,0:T(8,128)S(1)}, f32[8,128]{1,0:T(8,128)S(1)}, u32[]{:S(2)}, u32[]{:S(2)}) collective-permute-start(f32[8,128]{1,0:T(8,128)S(1)} %add.289), channel_id=1, source_target_pairs={{0,8},{8,0},{16,24},{24,16},{1,9},{9,1},{17,25},{25,17},{2,10},{10... | collective-permute-start | bytes 12296 | tf_op jit(solution)/shard_map/ppermute | solution.py:52
  (574 shorter events, 206.6 us)
Async XLA Ops:
  7.2 62.5 %all-gather.13.cloned.1.call-start = ((), (), s32[]{:S(2)}) async-start(), calls=%async_computation.14 | async-start | bytes 1474560 | tf_op jit(solution)/shard_map/all_gather | solution.py:881
  9.6 30.0 %collective-permute-start = (f32[96,135]{0,1:T(8,128)}, f32[96,135]{0,1:T(8,128)}, u32[]{:S(2)}, u32[]{:S(2)}) collective-permute-start(f32[96,135]{0,1:T(8,128)} %pad_maximum_fusion.9), channel_id=1, source_target_pairs={{0,24},{8,16},{16,8},{24,0},{1,25},{9,17},{17,9},{25,1},{2,26},{10... | collective-permute-start | bytes 155528 | tf_op jit(solution)/shard_map/ppermute | solution.py:864
  17.1 109.1 %all-gather.11.cloned.1.call-start = ((), (), s32[]{:S(2)}) async-start(), calls=%async_computation.7 | async-start | bytes 2949120 | tf_op jit(solution)/shard_map/all_gather | solution.py:881
  37.2 119.3 %all-gather.9.cloned.1.call-start = ((), (), s32[]{:S(2)}) async-start(), calls=%async_computation.6 | async-start | bytes 1474560 | tf_op jit(solution)/shard_map/all_gather | solution.py:881
  40.4 29.3 %collective-permute-start.7 = (f32[96,768]{1,0:T(8,128)S(1)}, f32[96,768]{1,0:T(8,128)S(1)}, u32[]{:S(2)}, u32[]{:S(2)}) collective-permute-start(f32[96,768]{1,0:T(8,128)S(1)} %pad_maximum_fusion.5.refs_5_.refs_7_.refs_8_), channel_id=1, source_target_pairs={{0,4},{4,0},{1,5},{5,1},{2,6},{6,2},{3,7},{7,3},{8,12},{12,8},{9,1... | collective-permute-start | bytes 884744 | tf_op jit(solution)/shard_map/ppermute | solution.py:27
  94.4 28.2 %collective-permute-start.15 = (f32[384,768]{1,0:T(8,128)S(1)}, f32[384,768]{1,0:T(8,128)}, u32[]{:S(2)}, u32[]{:S(2)}) collective-permute-start(f32[384,768]{1,0:T(8,128)S(1)} %maximum_add_fusion.refs_2_), channel_id=1, source_target_pairs={{0,2},{2,0},{1,3},{3,1},{4,6},{6,4},{5,7},{7,5},{8,10},{10,8},{9,1... | collective-permute-start | bytes 3538952 | tf_op jit(solution)/shard_map/ppermute | solution.py:27
  96.9 90.8 %all-gather.17.cloned.1.call-start = ((), (), s32[]{:S(2)}) async-start(), calls=%async_computation.16 | async-start | bytes 1474560 | tf_op jit(solution)/shard_map/all_gather | solution.py:881
  124.1 28.5 %collective-permute-start.22 = (f32[384,768]{1,0:T(8,128)S(1)}, f32[384,768]{1,0:T(8,128)}, u32[]{:S(2)}, u32[]{:S(2)}) collective-permute-start(f32[384,768]{1,0:T(8,128)S(1)} %maximum_add_fusion.1.refs_2_), channel_id=1, source_target_pairs={{0,2},{2,0},{1,3},{3,1},{4,6},{6,4},{5,7},{7,5},{8,10},{10,8},{9,1... | collective-permute-start | bytes 3538952 | tf_op jit(solution)/shard_map/ppermute | solution.py:27
  125.6 89.3 %all-gather.15.cloned.1.call-start = ((), (), s32[]{:S(2)}) async-start(), calls=%async_computation.15 | async-start | bytes 1474560 | tf_op jit(solution)/shard_map/all_gather | solution.py:881
  155.1 28.7 %collective-permute-start.27 = (f32[384,768]{1,0:T(8,128)}, f32[384,768]{1,0:T(8,128)}, u32[]{:S(2)}, u32[]{:S(2)}) collective-permute-start(f32[384,768]{1,0:T(8,128)} %maximum_add_fusion.2.refs_2_), channel_id=1, source_target_pairs={{0,2},{2,0},{1,3},{3,1},{4,6},{6,4},{5,7},{7,5},{8,10},{10,8},{9,1... | collective-permute-start | bytes 3538952 | tf_op jit(solution)/shard_map/ppermute | solution.py:27
  173.8 242.1 %reduce-scatter.7.cloned.1.call-start = ((), (), s32[]{:S(2)}) async-start(), calls=%async_computation.8 | async-start | bytes 1474560 | tf_op jit(solution)/shard_map/reduce_scatter | solution.py:62
  173.9 28.2 %collective-permute-start.20 = (f32[384,768]{1,0:T(8,128)S(1)}, f32[384,768]{1,0:T(8,128)S(1)}, u32[]{:S(2)}, u32[]{:S(2)}) collective-permute-start(f32[384,768]{1,0:T(8,128)S(1)} %copy-done.4), channel_id=1, source_target_pairs={{0,4},{4,0},{1,5},{5,1},{2,6},{6,2},{3,7},{7,3},{8,12},{12,8},{9,1... | collective-permute-start | bytes 3538952 | tf_op jit(solution)/shard_map/ppermute | solution.py:27
  175.4 28.1 %collective-permute-start.29 = (f32[384,768]{1,0:T(8,128)}, f32[384,768]{1,0:T(8,128)}, u32[]{:S(2)}, u32[]{:S(2)}) collective-permute-start(f32[384,768]{1,0:T(8,128)} %maximum_add_fusion.2.refs_2_), channel_id=1, source_target_pairs={{0,1},{1,0},{2,3},{3,2},{4,5},{5,4},{6,7},{7,6},{8,9},{9,8},{10,11... | collective-permute-start | bytes 3538952 | tf_op jit(solution)/shard_map/ppermute | solution.py:27
  186.3 28.6 %collective-permute-start.34 = (f32[384,768]{1,0:T(8,128)}, f32[384,768]{1,0:T(8,128)S(1)}, u32[]{:S(2)}, u32[]{:S(2)}) collective-permute-start(f32[384,768]{1,0:T(8,128)} %maximum_add_fusion.3.refs_2_), channel_id=1, source_target_pairs={{0,2},{2,0},{1,3},{3,1},{4,6},{6,4},{5,7},{7,5},{8,10},{10,8},{9,1... | collective-permute-start | bytes 3538952 | tf_op jit(solution)/shard_map/ppermute | solution.py:27
  202.0 29.1 %collective-permute-start.32 = (f32[384,768]{1,0:T(8,128)}, f32[384,768]{1,0:T(8,128)S(1)}, u32[]{:S(2)}, u32[]{:S(2)}) collective-permute-start(f32[384,768]{1,0:T(8,128)} %bitcast.112), channel_id=1, source_target_pairs={{0,4},{4,0},{1,5},{5,1},{2,6},{6,2},{3,7},{7,3},{8,12},{12,8},{9,1... | collective-permute-start | bytes 3538952 | tf_op jit(solution)/shard_map/ppermute | solution.py:27
  214.9 40.0 %collective-permute-start.31 = (f32[384,768]{1,0:T(8,128)}, f32[384,768]{1,0:T(8,128)S(1)}, u32[]{:S(2)}, u32[]{:S(2)}) collective-permute-start(f32[384,768]{1,0:T(8,128)} %bitcast.117), channel_id=1, source_target_pairs={{0,4},{4,0},{1,5},{5,1},{2,6},{6,2},{3,7},{7,3},{8,12},{12,8},{9,1... | collective-permute-start | bytes 3538952 | tf_op jit(solution)/shard_map/ppermute | solution.py:27
  220.9 34.6 %collective-permute-start.39 = (f32[128,768]{1,0:T(8,128)S(1)}, f32[128,768]{1,0:T(8,128)S(1)}, u32[]{:S(2)}, u32[]{:S(2)}) collective-permute-start(f32[128,768]{1,0:T(8,128)S(1)} %maximum_add_fusion.8.refs_2_), channel_id=1, source_target_pairs={{0,2},{2,0},{1,3},{3,1},{4,6},{6,4},{5,7},{7,5},{8,10},{10,8},{9,1... | collective-permute-start | bytes 1179656 | tf_op jit(solution)/shard_map/ppermute | solution.py:27
  323.9 42.3 %collective-permute-start.59 = (f32[384,768]{1,0:T(8,128)S(1)}, f32[384,768]{1,0:T(8,128)S(1)}, u32[]{:S(2)}, u32[]{:S(2)}) collective-permute-start(f32[384,768]{1,0:T(8,128)S(1)} %copy-done.54), channel_id=1, source_target_pairs={{0,4},{4,0},{1,5},{5,1},{2,6},{6,2},{3,7},{7,3},{8,12},{12,8},{9,1... | collective-permute-start | bytes 3538952 | tf_op jit(solution)/shard_map/ppermute | solution.py:27
  347.4 28.2 %collective-permute-start.71 = (f32[384,768]{1,0:T(8,128)S(1)}, f32[384,768]{1,0:T(8,128)}, u32[]{:S(2)}, u32[]{:S(2)}) collective-permute-start(f32[384,768]{1,0:T(8,128)S(1)} %maximum_add_fusion.4.refs_4_), channel_id=1, source_target_pairs={{0,2},{2,0},{1,3},{3,1},{4,6},{6,4},{5,7},{7,5},{8,10},{10,8},{9,1... | collective-permute-start | bytes 3538952 | tf_op jit(solution)/shard_map/ppermute | solution.py:27
  367.4 83.6 %reduce-scatter.9.cloned.1.call-start = ((), (), s32[]{:S(2)}) async-start(), calls=%async_computation.9 | async-start | bytes 1474560 | tf_op jit(solution)/shard_map/reduce_scatter | solution.py:62
  375.6 29.9 %collective-permute-start.58 = (f32[384,768]{1,0:T(8,128)}, f32[384,768]{1,0:T(8,128)S(1)}, u32[]{:S(2)}, u32[]{:S(2)}) collective-permute-start(f32[384,768]{1,0:T(8,128)} %get-tuple-element.294), channel_id=1, source_target_pairs={{0,4},{4,0},{1,5},{5,1},{2,6},{6,2},{3,7},{7,3},{8,12},{12,8},{9,1... | collective-permute-start | bytes 3538952 | tf_op jit(solution)/shard_map/ppermute | solution.py:27
  380.3 28.1 %collective-permute-start.76 = (f32[384,768]{1,0:T(8,128)S(1)}, f32[384,768]{1,0:T(8,128)S(1)}, u32[]{:S(2)}, u32[]{:S(2)}) collective-permute-start(f32[384,768]{1,0:T(8,128)S(1)} %maximum_add_fusion.5.refs_4_), channel_id=1, source_target_pairs={{0,2},{2,0},{1,3},{3,1},{4,6},{6,4},{5,7},{7,5},{8,10},{10,8},{9,1... | collective-permute-start | bytes 3538952 | tf_op jit(solution)/shard_map/ppermute | solution.py:27
  406.7 76.0 %reduce-scatter.11.cloned.1.call-start = ((), (), s32[]{:S(2)}) async-start(), calls=%async_computation.10 | async-start | bytes 1474560 | tf_op jit(solution)/shard_map/reduce_scatter | solution.py:62
  408.3 31.5 %collective-permute-start.81 = (f32[384,768]{1,0:T(8,128)}, f32[384,768]{1,0:T(8,128)}, u32[]{:S(2)}, u32[]{:S(2)}) collective-permute-start(f32[384,768]{1,0:T(8,128)} %get-tuple-element.348), channel_id=1, source_target_pairs={{0,4},{4,0},{1,5},{5,1},{2,6},{6,2},{3,7},{7,3},{8,12},{12,8},{9,1... | collective-permute-start | bytes 3538952 | tf_op jit(solution)/shard_map/ppermute | solution.py:27
  414.5 28.2 %collective-permute-start.83 = (f32[384,768]{1,0:T(8,128)S(1)}, f32[384,768]{1,0:T(8,128)}, u32[]{:S(2)}, u32[]{:S(2)}) collective-permute-start(f32[384,768]{1,0:T(8,128)S(1)} %maximum_add_fusion.6.refs_3_), channel_id=1, source_target_pairs={{0,2},{2,0},{1,3},{3,1},{4,6},{6,4},{5,7},{7,5},{8,10},{10,8},{9,1... | collective-permute-start | bytes 3538952 | tf_op jit(solution)/shard_map/ppermute | solution.py:27
  442.4 75.3 %reduce-scatter.13.cloned.1.call-start = ((), (), s32[]{:S(2)}) async-start(), calls=%async_computation.11 | async-start | bytes 1474560 | tf_op jit(solution)/shard_map/reduce_scatter | solution.py:62
  443.7 34.6 %collective-permute-start.80 = (f32[384,768]{1,0:T(8,128)S(1)}, f32[384,768]{1,0:T(8,128)}, u32[]{:S(2)}, u32[]{:S(2)}) collective-permute-start(f32[384,768]{1,0:T(8,128)S(1)} %copy-done.41), channel_id=1, source_target_pairs={{0,4},{4,0},{1,5},{5,1},{2,6},{6,2},{3,7},{7,3},{8,12},{12,8},{9,1... | collective-permute-start | bytes 3538952 | tf_op jit(solution)/shard_map/ppermute | solution.py:27
  450.2 30.7 %collective-permute-start.87 = (f32[384,768]{1,0:T(8,128)S(1)}, f32[384,768]{1,0:T(8,128)}, u32[]{:S(2)}, u32[]{:S(2)}) collective-permute-start(f32[384,768]{1,0:T(8,128)S(1)} %maximum_add_fusion.7.refs_3_), channel_id=1, source_target_pairs={{0,2},{2,0},{1,3},{3,1},{4,6},{6,4},{5,7},{7,5},{8,10},{10,8},{9,1... | collective-permute-start | bytes 3538952 | tf_op jit(solution)/shard_map/ppermute | solution.py:27
  480.8 101.9 %reduce-scatter.17.cloned.1.call-start = ((), (), s32[]{:S(2)}) async-start(), calls=%async_computation.13 | async-start | bytes 1474560 | tf_op jit(solution)/shard_map/reduce_scatter | solution.py:62
  482.1 31.3 %collective-permute-start.90 = (f32[384,768]{1,0:T(8,128)S(1)}, f32[384,768]{1,0:T(8,128)}, u32[]{:S(2)}, u32[]{:S(2)}) collective-permute-start(f32[384,768]{1,0:T(8,128)S(1)} %copy-done.42), channel_id=1, source_target_pairs={{0,4},{4,0},{1,5},{5,1},{2,6},{6,2},{3,7},{7,3},{8,12},{12,8},{9,1... | collective-permute-start | bytes 3538952 | tf_op jit(solution)/shard_map/ppermute | solution.py:27
  515.9 68.6 %reduce-scatter.15.cloned.1.call-start = ((), (), s32[]{:S(2)}) async-start(), calls=%async_computation.12 | async-start | bytes 1474560 | tf_op jit(solution)/shard_map/reduce_scatter | solution.py:62
  517.1 28.0 %collective-permute-start.97 = (f32[384,768]{1,0:T(8,128)S(1)}, f32[384,768]{1,0:T(8,128)S(1)}, u32[]{:S(2)}, u32[]{:S(2)}) collective-permute-start(f32[384,768]{1,0:T(8,128)S(1)} %copy-done.43), channel_id=1, source_target_pairs={{0,4},{4,0},{1,5},{5,1},{2,6},{6,2},{3,7},{7,3},{8,12},{12,8},{9,1... | collective-permute-start | bytes 3538952 | tf_op jit(solution)/shard_map/ppermute | solution.py:27
  (198 other events, 1770.7 us)
Sparse Core Ops, SparseCore 0:
  17.2 47.6 all-gather.12
  67.0 50.4 all-gather.10
  119.1 29.2 all-gather.8
  149.8 29.5 all-gather.16
  180.8 29.5 all-gather.14
  367.5 26.8 reduce-scatter.6
  406.8 26.8 reduce-scatter.8
  442.6 26.9 reduce-scatter.10
  480.9 27.6 reduce-scatter.12
  516.0 27.8 reduce-scatter.16
  546.5 34.2 reduce-scatter.14

commit v4 on v3

--- a/solution.py
+++ b/solution.py
@@ -136,6 +136,18 @@
         copies.start(near, dst.at[pl.ds(0, half)]),
         copies.start(far, dst.at[pl.ds(half, half)]),
     )
+
+
+def load_halves(copies, x, xb, pieces, add):
+    half = xb.shape[0] // 2
+    made = []
+    for i in range(2):
+        here = pl.ds(i * half, half)
+        group = [copies.start(x[i] if isinstance(x, tuple) else x.at[here], xb.at[here])]
+        for j in (2 * i, 2 * i + 1):
+            group.append(copies.start(pieces[j], add.at[pl.ds(j * half, half)]))
+        made.append(group)
+    return made
 
 
 def send_parts(copies, part, half, mine, theirs):
@@ -258,7 +270,6 @@
     else:
         copies.wait(cx, *ca)
     gain = row(vec, l)
-    normed = []
     outs = []
     for i in range(2):
         here = pl.ds(i * z.half, z.half)
@@ -369,27 +380,20 @@
     copies = Copies(sems)
     half = z.hq if last else z.half
     if last:
-        cx = [
-            copies.start(xp.at[pl.ds(z.hc, z.hq)], xb.at[pl.ds(0, z.hq)]),
-            copies.start(xp.at[pl.ds(z.half + z.hc, z.hq)], xb.at[pl.ds(z.hq, z.hq)]),
-        ]
-    else:
-        cx = [copies.start(xp, xb)]
-    ca = [copies.start(p, add.at[pl.ds(i * half, half)]) for i, p in enumerate((pa, pb, pc, pd))]
+        xp = (xp.at[pl.ds(z.hc, z.hq)], xp.at[pl.ds(z.half + z.hc, z.hq)])
+    halves = load_halves(copies, xp, xb, (pa, pb, pc, pd), add)
     cu = load_weight(copies, ups, wb)
     cd = load_weight(copies, downs, vb)
-    copies.wait(*cx, *ca)
     gain = row(vec, z.depth + l)
     for i in range(2):
         here = pl.ds(i * half, half)
+        copies.wait(*halves[i])
         xb[here, :] = xb[here, :] + (
             add[pl.ds(2 * i * half, half), :] + add[pl.ds((2 * i + 1) * half, half), :]
         )
     copies.start(xb, x_out)
     copies.wait(*cu)
     split_into(wh, wl, wb[...])
-    copies.wait(*cd)
-    split_into(vh, vl, vb[...])
     tiles = [(0, 2 * half)] if last else [(half, half), (0, half)]
     for start, size in tiles:
         here = pl.ds(start, size)
@@ -397,6 +401,10 @@
         u = mm(split(nh * gain), (wh[...], wl[...]), 1, 0)
         ub[here, :] = u
         copies.start(ub.at[here], u_out.at[here])
+        if cd:
+            copies.wait(*cd)
+            split_into(vh, vl, vb[...])
+            cd = None
         g, _ = gelu_parts(u)
         part[here, :] = mm(split(g), (vh[...], vl[...]), 1, 1)
         if start > 0:
@@ -441,22 +449,26 @@
     copies = Copies(sems)
     r = z.queries if last else z.rows
     half = r // 2
-    ca = [copies.start(p, add.at[pl.ds(i * half, half)]) for i, p in enumerate((pa, pb, pc, pd))]
-    cx = [copies.start(xm, xb)]
-    if not last:
+    pieces = (pa, pb, pc, pd)
+    if last:
+        halves = load_halves(copies, xm, xb, pieces, add)
+    else:
         (xnb,) = rest
-        ca.append(copies.start(xn, xnb))
+        halves = load_halves(copies, xn, xnb, pieces, add)
+        halves[1].append(copies.start(xm, xb))
         for i in range(2):
-            ca.append(copies.start(res.at[pl.ds(i * z.hq, z.hq)], dyb.at[pl.ds(i * z.half + z.hc, z.hq)]))
+            target = dyb.at[pl.ds(i * z.half + z.hc, z.hq)]
+            halves[i].append(copies.start(res.at[pl.ds(i * z.hq, z.hq)], target))
     cd = load_weight(copies, downs, vb)
     cu_in = copies.start(u_in, ub)
     cu = load_weight(copies, ups, wb)
+    cx = []
     if accumulate:
         co = (*load_pair(copies, olds[0], olds[1], gub), *load_pair(copies, olds[2], olds[3], gdb))
     gvb[...] = jnp.zeros_like(gvb)
-    copies.wait(*ca, *cx)
     for i in range(2):
         here = pl.ds(i * half, half)
+        copies.wait(*halves[i])
         total = add[pl.ds(2 * i * half, half), :] + add[pl.ds((2 * i + 1) * half, half), :]
         if last:
             x4 = xb[here, :] + total
@@ -488,8 +500,10 @@
     copies.start(gvb, gv)
     copies.wait(*cd)
     split_into(vh, vl, vb[...])
-    copies.wait(*cu)
-    split_into(wh, wl, wb[...])
+    if not last:
+        copies.wait(*cu)
+        split_into(wh, wl, wb[...])
+        cu = None
     copies.wait(cu_in)
     gain = row(vec, z.depth + l)
     tiles = [(0, r)] if last else [(half, half), (0, half)]
@@ -501,6 +515,10 @@
         gh[here, :] = a
         gl[here, :] = b
         ub[here, :] = dh * slope
+        if cu:
+            copies.wait(*cu)
+            split_into(wh, wl, wb[...])
+            cu = None
         part[here, :] = mm(split(ub[here, :]), (wh[...], wl[...]), 1, 1)
         if start > 0:
             send_parts(copies, part, half, None, theirs)
@@ -515,6 +533,7 @@
     d_half = z.d // 2
     copies.start(gdb.at[pl.ds(0, d_half)], gdn)
     copies.start(gdb.at[pl.ds(d_half, d_half)], gdf)
+    copies.wait(*cx)
     nh, _ = norm_stats(xb[...])
     new = mm(split(nh * gain), split(ub[...]), 0, 0)
     gub[...] = gub[...] + new if accumulate else new
@@ -573,8 +592,10 @@
     copies = Copies(sems)
     rq = z.queries if last else z.rows
     half = rq // 2
-    ca = [copies.start(p, add.at[pl.ds(i * half, half)]) for i, p in enumerate((pa, pb, pc, pd))]
-    ca += [copies.start(dyp, dyb), copies.start(xm, xmb)]
+    halves = load_halves(copies, dyp, dyb, (pa, pb, pc, pd), add)
+    for i in range(2):
+        here = pl.ds(i * half, half)
+        halves[i].append(copies.start(xm.at[here], xmb.at[here]))
     cw = load_weight(copies, weights, wb, c_ref)
     cq = [copies.start(q_in, qb), copies.start(kv_in, kvb), copies.start(o_in, ob)]
     cq += [copies.start(lse_in, lseb), copies.start(mask, maskb)]
@@ -582,10 +603,10 @@
     if accumulate:
         co = list(load_pair(copies, olds[0], olds[1], gb))
     gvb[...] = jnp.zeros_like(gvb)
-    copies.wait(*ca)
     gain2 = row(vec, z.depth + l)
     for i in range(2):
         here = pl.ds(i * half, half)
+        copies.wait(*halves[i])
         total = add[pl.ds(2 * i * half, half), :] + add[pl.ds((2 * i + 1) * half, half), :]
         nh, rstd = norm_stats(xmb[here, :])
         dy = dyb[here, :] + norm_back(total * gain2, nh, rstd)
@@ -964,7 +985,8 @@
     if near_by:
         first = [blocks[0]] + [hop(blocks[0], m) for m in (1, 2, 3)]
         near[0] = tuple(first + [swap(block, "dl") for block in first])
-        near[2] = (rows_near(jnp.concatenate([blocks[2], swap(blocks[2], "dl")], axis=0)),)
+        crossed = [jnp.concatenate([blocks[i], swap(blocks[i], "dl")], axis=0) for i in (2, 5)]
+        near[2] = (rows_near(crossed[0]),)
     else:
         near[0] = gather_rows(blocks[0])
         near[2] = gather_rows(blocks[2])
@@ -973,8 +995,13 @@
     (far[1],) = attn_forward(0, 1, cross(1), strict=True)
     (near[3],) = ffn_forward(0, 0, gather(3))
     far[3], near[4] = ffn_forward(0, 1, cross(3), gather(4))
-    far[4], near[5] = attn_forward(1, 0, cross(4), gather(5))
-    (far[5],) = attn_forward(1, 1, cross(5), strict=True)
+    if near_by:
+        far[4], got = attn_forward(1, 0, cross(4), lambda: rows_near(crossed[1]))
+        near[5] = (got,)
+        attn_forward(1, 1)
+    else:
+        far[4], near[5] = attn_forward(1, 0, cross(4), gather(5))
+        (far[5],) = attn_forward(1, 1, cross(5), strict=True)
     ffn_forward(1, 0)
     ffn_forward(1, 1)
 

time: 643 us -> 633 us (0.984)
  waiting for transfers between devices: 162 us -> 155 us
    ppermute x92, waiting for transfers between devices: 128 us -> 117 us  [swap(): return lax.ppermute(values, axis, SWAP)]
    unnamed x235 -> x221, local copies, waits for them, and re-layouts: 17.8 us -> 17.4 us
  transfers between devices with their start and end apart: 114 -> 114, of which waited for: 48 -> 49; matrix products, arithmetic and copies ran while one was open for 10% -> 10% of each run, Pallas kernels for 44% -> 44%
where the time goes in v4:
time: 633 us; the launch traced here: 624 us
  Pallas kernels  276 us (44%)
  waiting for transfers between devices  155 us (24%)
  starting transfers between devices  76 us (12%)
  other arithmetic  58.6 us (9%)
  local copies, waits for them, and re-layouts  33.3 us (5%)
  between operations  25.7 us (4%)
    pallas_call x18, Pallas kernels, run(): pl.pallas_call(kernel, name=name, out_shape=[jax.ShapeDtypeStruct(s, F32)...  276 us
    ppermute x92, waiting for transfers between devices, swap(): return lax.ppermute(values, axis, SWAP)  117 us
    ppermute x92, starting transfers between devices, swap(): return lax.ppermute(values, axis, SWAP)  50.7 us
    ppermute x9, waiting for transfers between devices, hop(): return lax.ppermute(value, 'dh', [(i, i ^ step) for i in range(line)])  30.5 us
    add x14, other arithmetic, head_sum(): a = mine + jnp.concatenate([after(first, before), second], axis=0)  18.4 us
    unnamed x221, local copies, waits for them, and re-layouts  17.4 us
    ppermute x9, starting transfers between devices, hop(): return lax.ppermute(value, 'dh', [(i, i ^ step) for i in range(line)])  14.8 us
  transfers between devices with their start and end apart: 114, of which 49 were waited for; matrix products, arithmetic and copies ran while one was open for 10% of the time, Pallas kernels for 44%

profile of v4, /device:TPU:0, one launch (start us, length us, event | category | flops | bytes accessed | tf_op | source)
XLA Modules:
  0.0 623.9 jit_solution(8794204842967285177)
XLA Ops:
  9.5 5.0 collective-permute-start
  25.2 8.7 %select_reduce_fusion = (s32[256,16]{1,0:T(8,128)S(1)}, s32[256,16]{1,0:T(8,128)S(1)}) fusion(s32[256,256]{1,0:T(8,128)S(1)} %get-tuple-element.518, s32[256,256]{1,0:T(8,128)S(1)} %broadcast_shift-right-arithmetic_fusion, s32[256,256]{1,0:T(8,128)S(1)} %get-tuple-element.519, s32[256,256]{1,0:T(8,128)S(1)} %get-tuple-element.520), kind=kLoop, calls=%fused_computation | loop fusion | flops 6283264 | bytes 1081344 | tf_op jit(solution)/shard_map/reduce_sum | solution.py:828
  45.1 10.4 %collective-permute-done.4.refs_6_.refs_8_.refs_9_ = f32[96,768]{1,0:T(8,128)S(1)} collective-permute-done((f32[96,768]{1,0:T(8,128)S(1)}, f32[96,768]{1,0:T(8,128)S(1)}, u32[]{:S(2)}, u32[]{:S(2)}) %collective-permute-start.4) | collective-permute-done | bytes 294944 | tf_op jit(solution)/shard_map/ppermute | solution.py:885
  56.8 9.0 %collective-permute-done.5.refs_7_.refs_9_.refs_10_ = f32[96,768]{1,0:T(8,128)S(1)} collective-permute-done((f32[96,768]{1,0:T(8,128)S(1)}, f32[96,768]{1,0:T(8,128)S(1)}, u32[]{:S(2)}, u32[]{:S(2)}) %collective-permute-start.5) | collective-permute-done | bytes 294944 | tf_op jit(solution)/shard_map/ppermute | solution.py:885
  69.7 4.3 collective-permute-done.9.refs_11_.refs_13_.refs_14_
  74.8 14.9 %attn_fwd0.2 = (f32[768,768]{1,0:T(8,128)}, f32[768,256]{1,0:T(8,128)}, f32[512,384]{1,0:T(8,128)}, f32[768,256]{1,0:T(8,128)}, f32[768,128]{1,0:T(8,128)}, /*in...) custom-call(s32[2]{0:T(128)} %pad_add_fusion.refs_0_.refs_21_, f32[768,1]{1,0:T(8,128)} %broadcast_in_dim.59.refs_1_, ...), custom_call_target="tpu_custom_call" | custom-call | flops 317089376 | bytes 838860 | tf_op jit(solution)/shard_map/attn_fwd0/pallas_call | solution.py:182
  98.2 14.7 %attn_fwd0.3 = (f32[768,768]{1,0:T(8,128)}, f32[768,256]{1,0:T(8,128)}, f32[512,384]{1,0:T(8,128)}, f32[768,256]{1,0:T(8,128)}, f32[768,128]{1,0:T(8,128)}, /*in...) custom-call(s32[2]{0:T(128)} %pad_add_fusion.refs_0_.refs_21_, f32[768,1]{1,0:T(8,128)} %broadcast_in_dim.58.refs_1_, ...), custom_call_target="tpu_custom_call" | custom-call | flops 317089376 | bytes 838860 | tf_op jit(solution)/shard_map/attn_fwd0/pallas_call | solution.py:182
  113.1 5.2 collective-permute-done.13.refs_7_.refs_10_
  125.8 15.2 %ffn_fwd0.2 = (f32[768,768]{1,0:T(8,128)}, f32[768,768]{1,0:T(8,128)}, f32[384,768]{1,0:T(8,128)}, f32[192,768]{1,0:T(8,128)}, f32[192,768]{1,0:T(8,128)}) custom-call(f32[8,768]{1,0:T(8,128)} %pad.8.refs_2_.refs_0_, f32[768,768]{1,0:T(8,128)} %get-tuple-element.223.refs_1_.refs_15_.refs_4_, f32[384,768]{1,0:T(8,128)} %copy-done.16, ...), custom_call_target="tpu_custom_call" | custom-call | flops 271790912 | bytes 1258291 | tf_op jit(solution)/shard_map/ffn_fwd0/pallas_call | solution.py:182
  141.8 10.7 %collective-permute-done.21.refs_3_ = f32[384,768]{1,0:T(8,128)} collective-permute-done((f32[384,768]{1,0:T(8,128)S(1)}, f32[384,768]{1,0:T(8,128)}, u32[]{:S(2)}, u32[]{:S(2)}) %collective-permute-start.21) | collective-permute-done | bytes 1179680 | tf_op jit(solution)/shard_map/ppermute | solution.py:27
  164.1 15.1 %ffn_fwd0.3 = (f32[768,768]{1,0:T(8,128)}, f32[768,768]{1,0:T(8,128)}, f32[384,768]{1,0:T(8,128)}, f32[192,768]{1,0:T(8,128)}, f32[192,768]{1,0:T(8,128)}) custom-call(f32[8,768]{1,0:T(8,128)} %pad.8.refs_2_.refs_0_, f32[768,768]{1,0:T(8,128)} %get-tuple-element.214.refs_1_.refs_15_.refs_4_, f32[384,768]{1,0:T(8,128)} %copy-done.15, ...), custom_call_target="tpu_custom_call" | custom-call | flops 271790912 | bytes 1258291 | tf_op jit(solution)/shard_map/ffn_fwd0/pallas_call | solution.py:182
  188.8 19.1 %collective-permute-done.26.refs_7_.refs_8_ = f32[384,768]{1,0:T(8,128)S(1)} collective-permute-done((f32[384,768]{1,0:T(8,128)S(1)}, f32[384,768]{1,0:T(8,128)S(1)}, u32[]{:S(2)}, u32[]{:S(2)}) %collective-permute-start.26) | collective-permute-done | bytes 1179680 | tf_op jit(solution)/shard_map/ppermute | solution.py:27
  209.3 11.2 %attn_fwd1.2 = (f32[768,768]{1,0:T(8,128)}, f32[256,256]{1,0:T(8,128)}, f32[512,384]{1,0:T(8,128)}, f32[256,256]{1,0:T(8,128)}, f32[256,128]{1,0:T(8,128)}, /*in...) custom-call(f32[8,768]{1,0:T(8,128)} %pad.8.refs_2_.refs_0_, ...), custom_call_target="tpu_custom_call" | custom-call | flops 135895456 | bytes 838860 | tf_op jit(solution)/shard_map/attn_fwd1/pallas_call | solution.py:182
  236.3 10.7 %attn_fwd1.3 = (f32[768,768]{1,0:T(8,128)}, f32[256,256]{1,0:T(8,128)}, f32[512,384]{1,0:T(8,128)}, f32[256,256]{1,0:T(8,128)}, f32[256,128]{1,0:T(8,128)}, /*in...) custom-call(f32[8,768]{1,0:T(8,128)} %pad.8.refs_2_.refs_0_, ...), custom_call_target="tpu_custom_call" | custom-call | flops 135895456 | bytes 838860 | tf_op jit(solution)/shard_map/attn_fwd1/pallas_call | solution.py:182
  253.2 8.6 %ffn_fwd1.2 = (f32[256,768]{1,0:T(8,128)}, f32[256,768]{1,0:T(8,128)}, f32[128,768]{1,0:T(8,128)}, f32[64,768]{1,0:T(8,128)}, f32[64,768]{1,0:T(8,128)}) custom-call(f32[8,768]{1,0:T(8,128)} %pad.8.refs_2_.refs_0_, f32[768,768]{1,0:T(8,128)} %get-tuple-element.244.refs_1_.refs_9_.refs_2_, f32[128,768]{1,0:T(8,128)} %copy-done.37, f32[128,768]{1,0:T(8,128)} %copy-done.68, ...), custom_call_target="tpu_custom_call" | custom-call | flops 90596968 | bytes 1258291 | tf_op jit(solution)/shard_map/ffn_fwd1/pallas_call | solution.py:182
  266.9 8.7 %ffn_fwd1.3 = (f32[256,768]{1,0:T(8,128)}, f32[256,768]{1,0:T(8,128)}, f32[128,768]{1,0:T(8,128)}, f32[64,768]{1,0:T(8,128)}, f32[64,768]{1,0:T(8,128)}) custom-call(f32[8,768]{1,0:T(8,128)} %pad.8.refs_2_.refs_0_, f32[768,768]{1,0:T(8,128)} %get-tuple-element.259.refs_1_.refs_9_.refs_2_, f32[128,768]{1,0:T(8,128)} %copy-done.36, f32[128,768]{1,0:T(8,128)} %copy-done.67, ...), custom_call_target="tpu_custom_call" | custom-call | flops 90596968 | bytes 1258291 | tf_op jit(solution)/shard_map/ffn_fwd1/pallas_call | solution.py:182
  282.0 10.5 %ffn_bwd1.2 = (f32[256,768]{1,0:T(8,128)}, f32[128,768]{1,0:T(8,128)}, f32[64,768]{1,0:T(8,128)}, f32[64,768]{1,0:T(8,128)}, f32[8,768]{1,0:T(8,128)}, /*index=5...) custom-call(f32[8,768]{1,0:T(8,128)} %pad.8.refs_2_.refs_0_, ...), custom_call_target="tpu_custom_call" | custom-call | flops 181193936 | bytes 1677721 | tf_op jit(solution)/shard_map/ffn_bwd1/pallas_call | solution.py:182
  297.8 12.2 %ffn_bwd1.3 = (f32[256,768]{1,0:T(8,128)}, f32[128,768]{1,0:T(8,128)}, f32[64,768]{1,0:T(8,128)}, f32[64,768]{1,0:T(8,128)}, f32[8,768]{1,0:T(8,128)}, /*index=5...) custom-call(f32[8,768]{1,0:T(8,128)} %pad.8.refs_2_.refs_0_, ...), custom_call_target="tpu_custom_call", output_to_operand_aliasing={{5}: (11, {}), {6}: (12, {}), {7}: (13, {}), {8}: (14, {})} | custom-call | flops 181193936 | bytes 1677721 | tf_op jit(solution)/shard_map/ffn_bwd1/pallas_call | solution.py:182
  317.0 15.6 %attn_bwd1.2 = (f32[256,768]{1,0:T(8,128)}, f32[384,768]{1,0:T(8,128)}, f32[192,768]{1,0:T(8,128)}, f32[192,768]{1,0:T(8,128)}, f32[8,768]{1,0:T(8,128)}, /*index=5*/f32[384,768]{1,0:T(8,128)}, f32[384,768]{1,0:T(8,128)}) custom-call(f32[8,768]{1,0:T(8,128)} %pad.8.refs_2_.refs_0_, f32[256,768]{1,0:T(8,128)} %get-tuple-element.281.refs_1_, ...), custom_call_target="tpu_custom_call" | custom-call | flops 301989888 | bytes 1258291 | tf_op jit(solution)/shard_map/attn_bwd1/pallas_call | solution.py:182
  339.5 16.1 %attn_bwd1.3 = (f32[256,768]{1,0:T(8,128)}, f32[384,768]{1,0:T(8,128)}, f32[192,768]{1,0:T(8,128)}, f32[192,768]{1,0:T(8,128)}, f32[8,768]{1,0:T(8,128)}, /*index=5*/f32[384,768]{1,0:T(8,128)}, f32[384,768]{1,0:T(8,128)}) custom-call(f32[8,768]{1,0:T(8,128)} %pad.8.refs_2_.refs_0_, ...), custom_call_target="tpu_custom_call", output_to_operand_aliasing={{5}: (15, {}), {6}: (16, {})} | custom-call | flops 301989888 | bytes 1258291 | tf_op jit(solution)/shard_map/attn_bwd1/pallas_call | solution.py:182
  357.2 9.0 %collective-permute-done.71.refs_5_ = f32[384,768]{1,0:T(8,128)} collective-permute-done((f32[384,768]{1,0:T(8,128)S(1)}, f32[384,768]{1,0:T(8,128)}, u32[]{:S(2)}, u32[]{:S(2)}) %collective-permute-start.71) | collective-permute-done | bytes 1179680 | tf_op jit(solution)/shard_map/ppermute | solution.py:27
  372.9 22.2 %ffn_bwd0.2 = (f32[768,768]{1,0:T(8,128)}, f32[384,768]{1,0:T(8,128)}, f32[192,768]{1,0:T(8,128)}, f32[192,768]{1,0:T(8,128)}, f32[8,768]{1,0:T(8,128)}, /*index...) custom-call(f32[8,768]{1,0:T(8,128)} %pad.8.refs_2_.refs_0_, ...), custom_call_target="tpu_custom_call" | custom-call | flops 543581824 | bytes 1677721 | tf_op jit(solution)/shard_map/ffn_bwd0/pallas_call | solution.py:182
  405.7 23.9 %ffn_bwd0.3 = (f32[768,768]{1,0:T(8,128)}, f32[384,768]{1,0:T(8,128)}, f32[192,768]{1,0:T(8,128)}, f32[192,768]{1,0:T(8,128)}, f32[8,768]{1,0:T(8,128)}, /*index...) custom-call(f32[8,768]{1,0:T(8,128)} %pad.8.refs_2_.refs_0_, ...), custom_call_target="tpu_custom_call", output_to_operand_aliasing={{5}: (12, {}), {6}: (13, {}), {7}: (14, {}), {8}: (15, {})} | custom-call | flops 543581824 | bytes 1677721 | tf_op jit(solution)/shard_map/ffn_bwd0/pallas_call | solution.py:182
  441.5 27.0 %attn_bwd0.2 = (f32[768,768]{1,0:T(8,128)}, f32[768,256]{1,0:T(8,128)}, f32[512,384]{1,0:T(8,128)}, f32[8,768]{1,0:T(8,128)}, f32[384,768]{1,0:T(8,128)}, /*index=5*/f32[384,768]{1,0:T(8,128)}) custom-call(f32[8,768]{1,0:T(8,128)} %pad.8.refs_2_.refs_0_, f32[768,768]{1,0:T(8,128)} %get-tuple-element.325.refs_1_, ...), custom_call_target="tpu_custom_call" | custom-call | flops 724775744 | bytes 1258291 | tf_op jit(solution)/shard_map/attn_bwd0/pallas_call | solution.py:182
  475.9 27.3 %attn_bwd0.3 = (f32[768,768]{1,0:T(8,128)}, f32[768,256]{1,0:T(8,128)}, f32[512,384]{1,0:T(8,128)}, f32[8,768]{1,0:T(8,128)}, f32[384,768]{1,0:T(8,128)}, /*index=5*/f32[384,768]{1,0:T(8,128)}) custom-call(f32[8,768]{1,0:T(8,128)} %pad.8.refs_2_.refs_0_, f32[768,768]{1,0:T(8,128)} %get-tuple-element.343.refs_1_, ...), custom_call_target="tpu_custom_call", output_to_operand_aliasing={{4}: (22, {}), {5}: (23, {})} | custom-call | flops 724775744 | bytes 1258291 | tf_op jit(solution)/shard_map/attn_bwd0/pallas_call | solution.py:182
  507.5 10.9 %embed_bwd.2 = (f32[8,768]{1,0:T(8,128)}, f32[768,128]{1,0:T(8,128)}) custom-call(s32[2]{0:T(128)} %pad_add_fusion.refs_0_.refs_21_, f32[768,1]{1,0:T(8,128)} %broadcast_in_dim.59.refs_1_, f32[8,768]{1,0:T(8,128)} %pad.8.refs_2_.refs_0_, f32[768,128]{1,0:T(8,128)} %get-tuple-element.521.refs_3_, f32[768,768]{1,0:T(8,128)} %get-tuple-element.223.refs_1_.refs_15_.refs_4_, ...), custom_call_target="tpu_custom_call" | custom-call | flops 113246208 | bytes 629145 | tf_op jit(solution)/shard_map/embed_bwd/pallas_call | solution.py:182
  518.5 10.9 %embed_bwd.3 = (f32[8,768]{1,0:T(8,128)}, f32[768,128]{1,0:T(8,128)}) custom-call(s32[2]{0:T(128)} %pad_add_fusion.refs_0_.refs_21_, f32[768,1]{1,0:T(8,128)} %broadcast_in_dim.58.refs_1_, f32[8,768]{1,0:T(8,128)} %pad.8.refs_2_.refs_0_, f32[768,128]{1,0:T(8,128)} %get-tuple-element.522.refs_3_, ...), custom_call_target="tpu_custom_call", output_to_operand_aliasing={{1}: (16, {})} | custom-call | flops 113246208 | bytes 629145 | tf_op jit(solution)/shard_map/embed_bwd/pallas_call | solution.py:182
  529.3 5.6 collective-permute-done.97
  538.0 9.8 %collective-permute-done.91 = f32[384,135]{1,0:T(8,128)S(1)} collective-permute-done((f32[384,135]{1,0:T(8,128)S(1)}, f32[384,135]{1,0:T(8,128)S(1)}, u32[]{:S(2)}, u32[]{:S(2)}) %collective-permute-start.91) | collective-permute-done | bytes 207392 | tf_op jit(solution)/shard_map/ppermute | solution.py:27
  553.6 6.1 collective-permute-done.92
  559.7 4.9 collective-permute-done.93
  588.8 6.5 %collective-permute-start.101 = (f32[8,128]{1,0:T(8,128)S(1)}, f32[8,128]{1,0:T(8,128)S(1)}, u32[]{:S(2)}, u32[]{:S(2)}) collective-permute-start(f32[8,128]{1,0:T(8,128)S(1)} %add.289), channel_id=1, source_target_pairs={{0,8},{8,0},{16,24},{24,16},{1,9},{9,1},{17,25},{25,17},{2,10},{10... | collective-permute-start | bytes 12296 | tf_op jit(solution)/shard_map/ppermute | solution.py:52
  (561 shorter events, 208.3 us)
Async XLA Ops:
  7.2 62.5 %all-gather.14.cloned.1.call-start = ((), (), s32[]{:S(2)}) async-start(), calls=%async_computation.15 | async-start | bytes 1474560 | tf_op jit(solution)/shard_map/all_gather | solution.py:902
  9.5 29.6 %collective-permute-start = (f32[96,135]{0,1:T(8,128)}, f32[96,135]{0,1:T(8,128)}, u32[]{:S(2)}, u32[]{:S(2)}) collective-permute-start(f32[96,135]{0,1:T(8,128)} %pad_maximum_fusion.10), channel_id=1, source_target_pairs={{0,24},{8,16},{16,8},{24,0},{1,25},{9,17},{17,9},{25,1},{2,26},{10... | collective-permute-start | bytes 155528 | tf_op jit(solution)/shard_map/ppermute | solution.py:885
  17.1 108.7 %all-gather.10.cloned.1.call-start = ((), (), s32[]{:S(2)}) async-start(), calls=%async_computation.7 | async-start | bytes 2949120 | tf_op jit(solution)/shard_map/all_gather | solution.py:902
  35.6 127.5 %all-gather.8.cloned.1.call-start = ((), (), s32[]{:S(2)}) async-start(), calls=%async_computation.6 | async-start | bytes 1474560 | tf_op jit(solution)/shard_map/all_gather | solution.py:902
  39.2 26.7 %collective-permute-start.5 = (f32[96,768]{1,0:T(8,128)S(1)}, f32[96,768]{1,0:T(8,128)S(1)}, u32[]{:S(2)}, u32[]{:S(2)}) collective-permute-start(f32[96,768]{1,0:T(8,128)S(1)} %pad_maximum_fusion.6.refs_5_.refs_7_.refs_8_), channel_id=1, source_target_pairs={{0,16},{8,24},{16,0},{24,8},{1,17},{9,25},{17,1},{25,9},{2,18},{10... | collective-permute-start | bytes 884744 | tf_op jit(solution)/shard_map/ppermute | solution.py:885
  39.9 29.7 %collective-permute-start.7 = (f32[96,768]{1,0:T(8,128)S(1)}, f32[96,768]{1,0:T(8,128)S(1)}, u32[]{:S(2)}, u32[]{:S(2)}) collective-permute-start(f32[96,768]{1,0:T(8,128)S(1)} %pad_maximum_fusion.6.refs_5_.refs_7_.refs_8_), channel_id=1, source_target_pairs={{0,4},{4,0},{1,5},{5,1},{2,6},{6,2},{3,7},{7,3},{8,12},{12,8},{9,1... | collective-permute-start | bytes 884744 | tf_op jit(solution)/shard_map/ppermute | solution.py:27
  90.3 28.0 %collective-permute-start.13 = (f32[384,768]{1,0:T(8,128)S(1)}, f32[384,768]{1,0:T(8,128)S(1)}, u32[]{:S(2)}, u32[]{:S(2)}) collective-permute-start(f32[384,768]{1,0:T(8,128)S(1)} %bitcast.112), channel_id=1, source_target_pairs={{0,4},{4,0},{1,5},{5,1},{2,6},{6,2},{3,7},{7,3},{8,12},{12,8},{9,1... | collective-permute-start | bytes 3538952 | tf_op jit(solution)/shard_map/ppermute | solution.py:27
  94.3 28.2 %collective-permute-start.15 = (f32[384,768]{1,0:T(8,128)S(1)}, f32[384,768]{1,0:T(8,128)}, u32[]{:S(2)}, u32[]{:S(2)}) collective-permute-start(f32[384,768]{1,0:T(8,128)S(1)} %maximum_add_fusion.refs_2_), channel_id=1, source_target_pairs={{0,2},{2,0},{1,3},{3,1},{4,6},{6,4},{5,7},{7,5},{8,10},{10,8},{9,1... | collective-permute-start | bytes 3538952 | tf_op jit(solution)/shard_map/ppermute | solution.py:27
  96.7 111.1 %all-gather.16.cloned.1.call-start = ((), (), s32[]{:S(2)}) async-start(), calls=%async_computation.16 | async-start | bytes 1474560 | tf_op jit(solution)/shard_map/all_gather | solution.py:902
  123.9 28.5 %collective-permute-start.21 = (f32[384,768]{1,0:T(8,128)S(1)}, f32[384,768]{1,0:T(8,128)}, u32[]{:S(2)}, u32[]{:S(2)}) collective-permute-start(f32[384,768]{1,0:T(8,128)S(1)} %maximum_add_fusion.1.refs_2_), channel_id=1, source_target_pairs={{0,2},{2,0},{1,3},{3,1},{4,6},{6,4},{5,7},{7,5},{8,10},{10,8},{9,1... | collective-permute-start | bytes 3538952 | tf_op jit(solution)/shard_map/ppermute | solution.py:27
  125.5 105.5 %all-gather.12.cloned.1.call-start = ((), (), s32[]{:S(2)}) async-start(), calls=%async_computation.8 | async-start | bytes 2949120 | tf_op jit(solution)/shard_map/all_gather | solution.py:902
  156.4 28.4 %collective-permute-start.28 = (f32[384,768]{1,0:T(8,128)}, f32[384,768]{1,0:T(8,128)}, u32[]{:S(2)}, u32[]{:S(2)}) collective-permute-start(f32[384,768]{1,0:T(8,128)} %maximum_add_fusion.2.refs_2_), channel_id=1, source_target_pairs={{0,2},{2,0},{1,3},{3,1},{4,6},{6,4},{5,7},{7,5},{8,10},{10,8},{9,1... | collective-permute-start | bytes 3538952 | tf_op jit(solution)/shard_map/ppermute | solution.py:27
  162.8 242.9 %reduce-scatter.7.cloned.1.call-start = ((), (), s32[]{:S(2)}) async-start(), calls=%async_computation.9 | async-start | bytes 1474560 | tf_op jit(solution)/shard_map/reduce_scatter | solution.py:62
  179.9 28.0 %collective-permute-start.26 = (f32[384,768]{1,0:T(8,128)S(1)}, f32[384,768]{1,0:T(8,128)S(1)}, u32[]{:S(2)}, u32[]{:S(2)}) collective-permute-start(f32[384,768]{1,0:T(8,128)S(1)} %copy-done.3), channel_id=1, source_target_pairs={{0,4},{4,0},{1,5},{5,1},{2,6},{6,2},{3,7},{7,3},{8,12},{12,8},{9,1... | collective-permute-start | bytes 3538952 | tf_op jit(solution)/shard_map/ppermute | solution.py:27
  181.3 28.0 %collective-permute-start.30 = (f32[384,768]{1,0:T(8,128)}, f32[384,768]{1,0:T(8,128)}, u32[]{:S(2)}, u32[]{:S(2)}) collective-permute-start(f32[384,768]{1,0:T(8,128)} %maximum_add_fusion.2.refs_2_), channel_id=1, source_target_pairs={{0,1},{1,0},{2,3},{3,2},{4,5},{5,4},{6,7},{7,6},{8,9},{9,8},{10,11... | collective-permute-start | bytes 3538952 | tf_op jit(solution)/shard_map/ppermute | solution.py:27
  187.3 33.2 %collective-permute-start.34 = (f32[384,768]{1,0:T(8,128)}, f32[384,768]{1,0:T(8,128)}, u32[]{:S(2)}, u32[]{:S(2)}) collective-permute-start(f32[384,768]{1,0:T(8,128)} %maximum_add_fusion.3.refs_2_), channel_id=1, source_target_pairs={{0,2},{2,0},{1,3},{3,1},{4,6},{6,4},{5,7},{7,5},{8,10},{10,8},{9,1... | collective-permute-start | bytes 3538952 | tf_op jit(solution)/shard_map/ppermute | solution.py:27
  207.8 27.4 %collective-permute-start.25 = (f32[384,768]{1,0:T(8,128)}, f32[384,768]{1,0:T(8,128)S(1)}, u32[]{:S(2)}, u32[]{:S(2)}) collective-permute-start(f32[384,768]{1,0:T(8,128)} %bitcast.113), channel_id=1, source_target_pairs={{0,4},{4,0},{1,5},{5,1},{2,6},{6,2},{3,7},{7,3},{8,12},{12,8},{9,1... | collective-permute-start | bytes 3538952 | tf_op jit(solution)/shard_map/ppermute | solution.py:27
  314.6 41.1 %collective-permute-start.59 = (f32[384,768]{1,0:T(8,128)S(1)}, f32[384,768]{1,0:T(8,128)S(1)}, u32[]{:S(2)}, u32[]{:S(2)}) collective-permute-start(f32[384,768]{1,0:T(8,128)S(1)} %copy-done.52), channel_id=1, source_target_pairs={{0,4},{4,0},{1,5},{5,1},{2,6},{6,2},{3,7},{7,3},{8,12},{12,8},{9,1... | collective-permute-start | bytes 3538952 | tf_op jit(solution)/shard_map/ppermute | solution.py:27
  338.0 28.2 %collective-permute-start.71 = (f32[384,768]{1,0:T(8,128)S(1)}, f32[384,768]{1,0:T(8,128)}, u32[]{:S(2)}, u32[]{:S(2)}) collective-permute-start(f32[384,768]{1,0:T(8,128)S(1)} %maximum_add_fusion.4.refs_4_), channel_id=1, source_target_pairs={{0,2},{2,0},{1,3},{3,1},{4,6},{6,4},{5,7},{7,5},{8,10},{10,8},{9,1... | collective-permute-start | bytes 3538952 | tf_op jit(solution)/shard_map/ppermute | solution.py:27
  356.9 84.5 %reduce-scatter.9.cloned.1.call-start = ((), (), s32[]{:S(2)}) async-start(), calls=%async_computation.10 | async-start | bytes 1474560 | tf_op jit(solution)/shard_map/reduce_scatter | solution.py:62
  366.2 28.9 %collective-permute-start.58 = (f32[384,768]{1,0:T(8,128)}, f32[384,768]{1,0:T(8,128)S(1)}, u32[]{:S(2)}, u32[]{:S(2)}) collective-permute-start(f32[384,768]{1,0:T(8,128)} %get-tuple-element.288), channel_id=1, source_target_pairs={{0,4},{4,0},{1,5},{5,1},{2,6},{6,2},{3,7},{7,3},{8,12},{12,8},{9,1... | collective-permute-start | bytes 3538952 | tf_op jit(solution)/shard_map/ppermute | solution.py:27
  370.9 28.1 %collective-permute-start.76 = (f32[384,768]{1,0:T(8,128)S(1)}, f32[384,768]{1,0:T(8,128)S(1)}, u32[]{:S(2)}, u32[]{:S(2)}) collective-permute-start(f32[384,768]{1,0:T(8,128)S(1)} %maximum_add_fusion.5.refs_4_), channel_id=1, source_target_pairs={{0,2},{2,0},{1,3},{3,1},{4,6},{6,4},{5,7},{7,5},{8,10},{10,8},{9,1... | collective-permute-start | bytes 3538952 | tf_op jit(solution)/shard_map/ppermute | solution.py:27
  396.3 76.4 %reduce-scatter.11.cloned.1.call-start = ((), (), s32[]{:S(2)}) async-start(), calls=%async_computation.11 | async-start | bytes 1474560 | tf_op jit(solution)/shard_map/reduce_scatter | solution.py:62
  399.0 30.6 %collective-permute-start.81 = (f32[384,768]{1,0:T(8,128)}, f32[384,768]{1,0:T(8,128)}, u32[]{:S(2)}, u32[]{:S(2)}) collective-permute-start(f32[384,768]{1,0:T(8,128)} %get-tuple-element.342), channel_id=1, source_target_pairs={{0,4},{4,0},{1,5},{5,1},{2,6},{6,2},{3,7},{7,3},{8,12},{12,8},{9,1... | collective-permute-start | bytes 3538952 | tf_op jit(solution)/shard_map/ppermute | solution.py:27
  405.0 28.2 %collective-permute-start.83 = (f32[384,768]{1,0:T(8,128)S(1)}, f32[384,768]{1,0:T(8,128)}, u32[]{:S(2)}, u32[]{:S(2)}) collective-permute-start(f32[384,768]{1,0:T(8,128)S(1)} %maximum_add_fusion.6.refs_3_), channel_id=1, source_target_pairs={{0,2},{2,0},{1,3},{3,1},{4,6},{6,4},{5,7},{7,5},{8,10},{10,8},{9,1... | collective-permute-start | bytes 3538952 | tf_op jit(solution)/shard_map/ppermute | solution.py:27
  432.2 75.4 %reduce-scatter.13.cloned.1.call-start = ((), (), s32[]{:S(2)}) async-start(), calls=%async_computation.12 | async-start | bytes 1474560 | tf_op jit(solution)/shard_map/reduce_scatter | solution.py:62
  433.4 35.0 %collective-permute-start.80 = (f32[384,768]{1,0:T(8,128)S(1)}, f32[384,768]{1,0:T(8,128)}, u32[]{:S(2)}, u32[]{:S(2)}) collective-permute-start(f32[384,768]{1,0:T(8,128)S(1)} %copy-done.40), channel_id=1, source_target_pairs={{0,4},{4,0},{1,5},{5,1},{2,6},{6,2},{3,7},{7,3},{8,12},{12,8},{9,1... | collective-permute-start | bytes 3538952 | tf_op jit(solution)/shard_map/ppermute | solution.py:27
  440.0 31.1 %collective-permute-start.87 = (f32[384,768]{1,0:T(8,128)S(1)}, f32[384,768]{1,0:T(8,128)}, u32[]{:S(2)}, u32[]{:S(2)}) collective-permute-start(f32[384,768]{1,0:T(8,128)S(1)} %maximum_add_fusion.7.refs_3_), channel_id=1, source_target_pairs={{0,2},{2,0},{1,3},{3,1},{4,6},{6,4},{5,7},{7,5},{8,10},{10,8},{9,1... | collective-permute-start | bytes 3538952 | tf_op jit(solution)/shard_map/ppermute | solution.py:27
  470.9 101.2 %reduce-scatter.17.cloned.1.call-start = ((), (), s32[]{:S(2)}) async-start(), calls=%async_computation.14 | async-start | bytes 1474560 | tf_op jit(solution)/shard_map/reduce_scatter | solution.py:62
  472.2 31.1 %collective-permute-start.90 = (f32[384,768]{1,0:T(8,128)S(1)}, f32[384,768]{1,0:T(8,128)}, u32[]{:S(2)}, u32[]{:S(2)}) collective-permute-start(f32[384,768]{1,0:T(8,128)S(1)} %copy-done.41), channel_id=1, source_target_pairs={{0,4},{4,0},{1,5},{5,1},{2,6},{6,2},{3,7},{7,3},{8,12},{12,8},{9,1... | collective-permute-start | bytes 3538952 | tf_op jit(solution)/shard_map/ppermute | solution.py:27
  505.7 68.2 %reduce-scatter.15.cloned.1.call-start = ((), (), s32[]{:S(2)}) async-start(), calls=%async_computation.13 | async-start | bytes 1474560 | tf_op jit(solution)/shard_map/reduce_scatter | solution.py:62
  507.0 28.0 %collective-permute-start.97 = (f32[384,768]{1,0:T(8,128)S(1)}, f32[384,768]{1,0:T(8,128)S(1)}, u32[]{:S(2)}, u32[]{:S(2)}) collective-permute-start(f32[384,768]{1,0:T(8,128)S(1)} %copy-done.42), channel_id=1, source_target_pairs={{0,4},{4,0},{1,5},{5,1},{2,6},{6,2},{3,7},{7,3},{8,12},{12,8},{9,1... | collective-permute-start | bytes 3538952 | tf_op jit(solution)/shard_map/ppermute | solution.py:27
  (191 other events, 1723.5 us)
Sparse Core Ops, SparseCore 0:
  17.2 47.6 all-gather.13
  67.1 50.3 all-gather.9
  119.1 29.2 all-gather.7
  149.8 29.5 all-gather.15
  181.4 49.5 all-gather.11
  357.0 27.7 reduce-scatter.6
  396.5 27.7 reduce-scatter.8
  432.3 27.6 reduce-scatter.10
  471.0 27.1 reduce-scatter.12
  505.8 27.2 reduce-scatter.16
  536.4 33.5 reduce-scatter.14
